TPU v7x, 32 devices: a whole 2x2x4 slice. The times are simulated.
32 devices in a mesh: seq: 8 (over z, x), head: 4 (over y, core).
Axes of the slice: x: 2, y: 2, z: 4, core: 2. Of those that a mesh axis runs over, the one named last changes fastest.
Arguments:
- queries: bfloat16 [8192, 2048], P('seq', 'head'), may hold values from -100 to 100
- keys: bfloat16 [8192, 2048], P('seq', 'head'), may hold values from -8 to 8
- values: bfloat16 [8192, 2048], P('seq', 'head'), may hold values from -6 to 6
- rates: float32 [8192, 8], P('seq', 'head'), may hold values from 0.001 to 0.01
- head_scale: float32 [8], P('head'), may hold values from 0.3 to 3
- w_one: float32 [8, 256, 256], P('head'), may hold values from -0.375 to 0.375
- w_three: float32 [8, 256, 256], P('head'), may hold values from -0.375 to 0.375
- w_two: float32 [8, 256, 256], P('head'), may hold values from -0.375 to 0.375
Outputs:
- mixed: float32 [8192, 2048], P('seq', 'head')
- new_one: float32 [8, 256, 256], P('head')
- new_three: float32 [8, 256, 256], P('head')
- new_two: float32 [8, 256, 256], P('head')
All inputs are finite; a program needn't handle non-finite values.
Results may differ from a plain program's by a relative error of at most 0.00065.
Values may be sent and summed in bfloat16 or wider, within the bound.
No kernel may reach another device: no remote copies, remote signals or barrier semaphores. Data moves between devices by JAX's collectives and lax.ppermute only.
A program may use at most 64 MiB of HBM per device.

v0:
```python
import jax
import jax.numpy as jnp
from jax import lax
from jax.sharding import PartitionSpec as P

WINDOW_SPAN = 512


HIGH = lax.Precision.HIGHEST
EPS = 1e-06


def passed_along(block, axis, distance):
    devices = range(lax.axis_size(axis))
    route = [(i - distance, i) for i in devices if i - distance in devices]
    return lax.ppermute(block, axis, route)


def renorm(weight, grad):
    upd = weight + grad
    old = jnp.sqrt(jnp.sum(weight * weight, axis=2, keepdims=True) + EPS)
    cur = jnp.sqrt(jnp.sum(upd * upd, axis=2, keepdims=True) + EPS)
    return upd * (old / cur)


def per_device(queries, keys, values, rates, head_scale, w_one, w_three, w_two):
    tokens, width = queries.shape
    head_group = w_one.shape[0]
    span_size = w_one.shape[1]
    kf = keys.reshape(tokens, head_group, span_size).astype(jnp.float32)
    vf = values.reshape(tokens, head_group, span_size).astype(jnp.float32)
    h1 = jnp.einsum("thi,hij->thj", kf, w_one, precision=HIGH)
    h3 = jnp.einsum("thi,hij->thj", kf, w_three, precision=HIGH)
    sg = jax.nn.sigmoid(h1)
    sil = h1 * sg
    act = sil * h3
    scaled = rates[:, :, None] * vf
    g2 = jnp.einsum("thi,thj->hij", act, scaled, precision=HIGH)
    dact = jnp.einsum("thj,hij->thi", scaled, w_two, precision=HIGH)
    d1 = dact * h3 * sg * (1.0 + h1 * (1.0 - sg))
    d3 = dact * sil
    g1 = jnp.einsum("thi,thj->hij", kf, d1, precision=HIGH)
    g3 = jnp.einsum("thi,thj->hij", kf, d3, precision=HIGH)
    grads = jnp.stack([g1, g3, g2])
    weights = jnp.stack([w_one, w_three, w_two])
    summed = lax.psum(grads, "seq")
    updated = renorm(weights, summed)
    qf = queries.reshape(tokens, head_group, span_size).astype(jnp.float32)
    p1 = jnp.einsum("thi,hij->thj", qf, updated[0], precision=HIGH)
    p3 = jnp.einsum("thi,hij->thj", qf, updated[1], precision=HIGH)
    outer = jnp.einsum("thi,hij->thj", p1 * jax.nn.sigmoid(p1) * p3, updated[2], precision=HIGH)
    zed = outer * head_scale[None, :, None]
    local_sq = jnp.sum(zed * zed, axis=(1, 2))
    total_sq = lax.psum(local_sq, "head")
    all_heads = head_group * lax.axis_size("head")
    ynorm = zed / jnp.sqrt(total_sq / (all_heads * span_size) + EPS)[:, None, None]
    prior_keys, prior_values = passed_along(
        (keys[tokens - WINDOW_SPAN :], values[tokens - WINDOW_SPAN :]), "seq", 1
    )
    ext_keys = jnp.concatenate([prior_keys, keys], axis=0)
    ext_values = jnp.concatenate([prior_values, values], axis=0)
    offset = lax.axis_index("seq") * tokens
    block_span = min(512, tokens)
    scale = span_size ** (-0.5)
    query_rows = queries.reshape(tokens, head_group, span_size)
    rows = jnp.arange(block_span, dtype=jnp.int32)[:, None]
    cols = jnp.arange(block_span + WINDOW_SPAN, dtype=jnp.int32)[None, :]
    outputs = []
    for index in range(tokens // block_span):
        start_offset = index * block_span
        qb = query_rows[start_offset : start_offset + block_span]
        kb = ext_keys[start_offset : start_offset + block_span + WINDOW_SPAN].reshape(
            block_span + WINDOW_SPAN, head_group, span_size
        )
        value_block = ext_values[start_offset : start_offset + block_span + WINDOW_SPAN].reshape(
            block_span + WINDOW_SPAN, head_group, span_size
        )
        scores = jnp.einsum("ihd,jhd->hij", qb, kb, preferred_element_type=jnp.float32) * scale
        allowed = (
            (cols > rows)
            & (cols <= rows + WINDOW_SPAN)
            & (offset + start_offset + cols - WINDOW_SPAN >= 0)
        )
        scores = jnp.where(allowed[None], scores, -jnp.inf)
        top = jnp.max(scores, axis=-1, keepdims=True)
        expo = jnp.exp(scores - top)
        probs = (expo / jnp.sum(expo, axis=-1, keepdims=True)).astype(jnp.bfloat16)
        outputs.append(
            jnp.einsum("hij,jhd->ihd", probs, value_block, preferred_element_type=jnp.float32)
        )
    attn = jnp.concatenate(outputs, axis=0)
    mixed = (attn + ynorm).reshape(tokens, width)
    return (mixed, updated[0], updated[1], updated[2])


def solution(mesh):
    placed = (
        P("seq", "head"),
        P("seq", "head"),
        P("seq", "head"),
        P("seq", "head"),
        P("head"),
        P("head", None, None),
        P("head", None, None),
        P("head", None, None),
    )
    return jax.shard_map(
        per_device,
        mesh=mesh,
        in_specs=placed,
        out_specs=(
            P("seq", "head"),
            P("head", None, None),
            P("head", None, None),
            P("head", None, None),
        ),
        check_vma=False,
    )
```

profile of v0, /device:TPU:0, one launch (start us, length us, event | category | flops | bytes accessed | tf_op | source)
XLA Modules:
  0.0 156.2 jit_solution(4085122820597127520)
XLA Ops:
  7.2 0.0 copy-start.7
  7.2 0.0 all-reduce.2.cloned.1.call-start
  7.2 2.0 %slice.36 = bf16[512,512]{1,0:T(8,128)(2,1)} slice(bf16[1024,512]{1,0:T(8,128)(2,1)} %param.10), slice={[512:1024], [0:512]} | slice | bytes 1048576 | tf_op jit(solution)/shard_map/slice | solution.py:58
  9.2 5.7 %collective-permute-start = (bf16[512,512]{1,0:T(8,128)(2,1)}, bf16[512,512]{1,0:T(8,128)(2,1)}, u32[]{:S(2)}, u32[]{:S(2)}) collective-permute-start(bf16[512,512]{1,0:T(8,128)(2,1)} %slice.36), channel_id=1, source_target_pairs={{0,4},{4,8},{8,12},{12,16},{16,20},{20,24},{24,28},{1,5},{5,9},{9,... | collective-permute-start | bytes 1572872 | tf_op jit(solution)/shard_map/ppermute | solution.py:16
  14.9 1.5 copy.42
  16.4 0.8 slice.47
  17.2 3.6 %collective-permute-start.1 = (bf16[512,512]{0,1:T(8,128)(2,1)}, bf16[512,512]{0,1:T(8,128)(2,1)}, u32[]{:S(2)}, u32[]{:S(2)}) collective-permute-start(bf16[512,512]{0,1:T(8,128)(2,1)} %slice.47), channel_id=1, source_target_pairs={{0,4},{4,8},{8,12},{12,16},{16,20},{20,24},{24,28},{1,5},{5,9},{9,... | collective-permute-start | bytes 1572872 | tf_op jit(solution)/shard_map/ppermute | solution.py:16
  20.8 1.1 fusion.49
  21.9 0.0 copy-start.1
  21.9 0.0 copy-start.6
  21.9 1.1 fusion.47
  23.0 0.1 copy-done.1
  23.1 0.1 copy-done.6
  23.3 2.1 %fusion.22 = f32[2,1024,256]{2,1,0:T(8,128)S(1)} fusion(f32[2,256,256]{2,1,0:T(8,128)S(1)} %copy-done.6, f32[1024,2]{0,1:T(2,128)S(1)} %copy-done.9, bf16[128,2,8,256]{3,2,1,0:T(8,128)(2,1)S(1)} %bitcast.165), kind=kOutput, calls=%fused_computation.37 | convolution fusion | flops 1611661312 | bytes 3678208 | tf_op jit(solution)/shard_map/thj,hij->thi/dot_general | solution.py:39
  25.3 4.2 %fusion.39 = f32[1,2,256,256]{2,3,1,0:T(8,128)S(1)} fusion(f32[2,256,1024]{1,2,0:T(8,128)S(1)} %fusion.49, f32[1024,2]{0,1:T(2,128)S(1)} %copy-done.9, bf16[128,2,8,256]{3,2,1,0:T(8,128)(2,1)S(1)} %bitcast.166, f32[2,256,1024]{1,2,0:T(8,128)S(1)} %fusion.47), kind=kOutput, calls=%fused_computation.58 | convolution fusion | flops 1614282752 | bytes 5775360 | tf_op jit(solution)/shard_map/thi,thj->hij/dot_general | solution.py:38
  29.6 2.0 %fusion.40 = f32[1,2,256,256]{2,3,1,0:T(8,128)S(1)} fusion(f32[2,1024,256]{2,1,0:T(8,128)S(1)} %fusion.22, bf16[128,2,8,256]{3,2,1,0:T(8,128)(2,1)S(1)} %bitcast.159, f32[2,256,1024]{1,2,0:T(8,128)S(1)} %fusion.47), kind=kOutput, calls=%fused_computation.59 | convolution fusion | flops 1613234176 | bytes 5767168 | tf_op jit(solution)/shard_map/thi,thj->hij/dot_general | solution.py:43
  31.6 2.5 %fusion.36 = f32[1,2,256,256]{2,3,1,0:T(8,128)S(1)} fusion(f32[2,256,1024]{1,2,0:T(8,128)S(1)} %fusion.47, f32[2,256,1024]{1,2,0:T(8,128)S(1)} %fusion.49, f32[2,1024,256]{2,1,0:T(8,128)S(1)} %fusion.22, bf16[128,2,8,256]{3,2,1,0:T(8,128)(2,1)S(1)} %bitcast.160), kind=kOutput, calls=%fused_computation.57 | convolution fusion | flops 1615331328 | bytes 7864320 | tf_op jit(solution)/shard_map/thi,thj->hij/dot_general | solution.py:42
  34.1 1.2 pad_maximum_fusion.1
  35.3 0.0 all-reduce.2.cloned.1.call-update
  35.4 2.2 %fusion.77 = (bf16[512,512]{1,0:T(8,128)(2,1)}, bf16[512,512]{1,0:T(8,128)(2,1)}) fusion(bf16[1024,512]{1,0:T(8,128)(2,1)} %param.8), kind=kLoop, calls=%fused_computation.106 | loop fusion | bytes 2097152 | tf_op jit(solution)/shard_map/slice | solution.py:71
  37.6 2.0 %copy.95 = bf16[512,512]{0,1:T(8,128)(2,1)} copy(bf16[512,512]{1,0:T(8,128)(2,1)} %get-tuple-element.18) | data formatting | bytes 1048576
  39.7 3.9 %fusion.51 = f32[2,512,1024]{1,2,0:T(8,128)} fusion(bf16[512,2,256]{0,2,1:T(8,128)(2,1)} %bitcast.174, bf16[128,2,8,256]{3,2,1,0:T(8,128)(2,1)S(1)} %bitcast.161), kind=kOutput, calls=%fused_computation.70 | convolution fusion | flops 536870912 | bytes 5767168 | tf_op jit(solution)/shard_map/ihd,jhd->hij/dot_general | solution.py:78
  43.6 1.7 %fusion.33 = (pred[512,1024]{0,1:T(8,128)(4,1)}, pred[512,1024]{0,1:T(8,128)(4,1)S(1)}) fusion(s32[512]{0:T(512)S(1)} %iota_add_fusion, pred[1024]{0:T(1024)(128)(4,1)S(1)} %get-tuple-element.28, pred[1024]{0:T(1024)(128)(4,1)S(1)} %get-tuple-element.27), kind=kLoop, calls=%fused_computation.50 | loop fusion | flops 2621440 | bytes 1052672 | tf_op jit(solution)/shard_map/and | solution.py:80
  45.3 5.7 %fusion.78 = (f32[2,512]{1,0:T(2,128)S(1)}, f32[2,512,1024]{1,2,0:T(8,128)S(1)}) fusion(f32[2,512,1024]{1,2,0:T(8,128)} %fusion.51, pred[512,1024]{0,1:T(8,128)(4,1)S(1)} %get-tuple-element.20), kind=kOutput, calls=%fused_computation.107 | output fusion | flops 6292479 | bytes 8916992 | tf_op jit(solution)/shard_map/sub | solution.py:86
  51.0 1.7 %fusion.34 = f32[512,2,256]{0,2,1:T(8,128)} fusion(f32[2,512,1024]{1,2,0:T(8,128)S(1)} %get-tuple-element.22, f32[2,512]{1,0:T(2,128)S(1)} %get-tuple-element.21, bf16[128,2,8,256]{3,2,1,0:T(8,128)(2,1)S(1)} %bitcast.167), kind=kOutput, calls=%fused_computation.55 | convolution fusion | flops 538968064 | bytes 6295552 | tf_op jit(solution)/shard_map/hij,jhd->ihd/dot_general | solution.py:89
  52.7 1.5 copy.96
  54.2 2.1 %copy.57 = f32[2,256,256]{1,2,0:T(8,128)} copy(f32[2,256,256]{2,1,0:T(8,128)} %param.15) | data formatting | bytes 1048576 | tf_op args[7]
  56.3 2.0 %copy.56 = f32[2,256,256]{1,2,0:T(8,128)} copy(f32[2,256,256]{2,1,0:T(8,128)} %param.14) | data formatting | bytes 1048576 | tf_op args[6]
  58.3 2.1 %copy.55 = f32[2,256,256]{1,2,0:T(8,128)} copy(f32[2,256,256]{2,1,0:T(8,128)} %param.13) | data formatting | bytes 1048576 | tf_op args[5]
  60.4 2.1 %copy.94 = bf16[512,512]{0,1:T(8,128)(2,1)} copy(bf16[512,512]{1,0:T(8,128)(2,1)} %get-tuple-element.17) | data formatting | bytes 1048576
  62.4 2.1 %pad_maximum_fusion.3 = bf16[1024,512]{1,0:T(8,128)(2,1)} fusion(bf16[1024,512]{1,0:T(8,128)(2,1)S(1)} %copy-done.1, bf16[512,512]{1,0:T(8,128)(2,1)} %collective-permute-done), kind=kLoop, calls=%fused_computation.73 | loop fusion | flops 2097152 | bytes 2621440 | tf_op jit(solution)/shard_map/concatenate | solution.py:61
  64.5 2.3 %copy.41 = bf16[1024,512]{0,1:T(8,128)(2,1)} copy(bf16[1024,512]{1,0:T(8,128)(2,1)} %pad_maximum_fusion.3) | data formatting | bytes 2097152 | tf_op jit(solution)/shard_map/slice | solution.py:75
  66.8 1.1 pad_maximum_fusion.2
  68.0 5.0 %fusion.79 = (f32[2,512]{1,0:T(2,128)S(1)}, f32[2,512,1024]{1,2,0:T(8,128)}) fusion(pred[512,1024]{0,1:T(8,128)(4,1)} %get-tuple-element.19, bf16[1024,2,256]{0,2,1:T(8,128)(2,1)S(1)} %bitcast.176, bf16[512,2,256]{0,2,1:T(8,128)(2,1)} %bitcast.177), kind=kOutput, calls=%fused_computation.108 | convolution fusion | flops 541066240 | bytes 6295552 | tf_op jit(solution)/shard_map/sub | solution.py:86
  73.0 4.4 %fusion.35 = f32[512,2,256]{0,2,1:T(8,128)} fusion(bf16[1024,2,256]{0,2,1:T(8,128)(2,1)} %bitcast.175, f32[2,512,1024]{1,2,0:T(8,128)} %get-tuple-element.24, f32[2,512]{1,0:T(2,128)S(1)} %get-tuple-element.23), kind=kOutput, calls=%fused_computation.56 | convolution fusion | flops 538968064 | bytes 6295552 | tf_op jit(solution)/shard_map/hij,jhd->ihd/dot_general | solution.py:89
  77.4 46.9 %all-reduce.2.cloned.1.call-done = f32[3,2,256,256]{2,3,1,0:T(8,128)} async-done(((f32[3,2,256,256]{2,3,1,0:T(8,128)}), f32[3,2,256,256]{2,3,1,0:T(8,128)}) %all-reduce.2.cloned.1.call-update) | async-done | bytes 1572880 | tf_op jit(solution)/shard_map/psum | solution.py:46
  124.3 2.0 %multiply_reduce_fusion.2 = (f32[3,2,256]{2,1,0:T(2,128)S(1)}, f32[3,2,256]{2,1,0:T(2,128)S(1)}) fusion(f32[1,2,256,256]{2,3,1,0:T(8,128)S(1)} %bitcast.168, f32[1,2,256,256]{2,3,1,0:T(8,128)S(1)} %bitcast.170, f32[1,2,256,256]{2,3,1,0:T(8,128)S(1)} %bitcast.172, f32[3,2,256,256]{2,3,1,0:T(8,128)} %all-reduce.2.cloned.1.call-done), kind=kLoop, calls=%fused_computation.54 | loop fusion | flops 2749440 | bytes 3158016 | tf_op jit(solution)/shard_map/reduce_sum | solution.py:21
  126.3 0.4 broadcast_multiply_fusion
  126.7 1.2 fusion.76
  128.0 1.2 fusion.75
  129.2 1.0 slice_bitcast_fusion.2
  130.2 3.8 %multiply_reduce_fusion = (f32[1024]{0:T(1024)S(1)}, f32[2,256,1024]{2,1,0:T(8,128)}) fusion(f32[2]{0:T(128)S(1)} %copy-done.10, f32[2,256,1024]{1,2,0:T(8,128)S(1)} %fusion.76, f32[2,256,1024]{1,2,0:T(8,128)S(1)} %fusion.75, f32[3,2,256,256]{2,3,1,0:T(8,128)S(1)} %broadcast_multiply_fusion), kind=kOutput, calls=%fused_computation.34 | convolution fusion | flops 1614806016 | bytes 6820352 | tf_op jit(solution)/shard_map/thi,hij->thj/dot_general | solution.py:51
  134.0 6.8 %psum.15 = f32[1024]{0:T(1024)S(1)} all-reduce(f32[1024]{0:T(1024)S(1)} %get-tuple-element.25), channel_id=1, replica_groups=mesh['seq'=8,'head'=4] {'head'}, use_global_device_ids=true, to_apply=%region_8.9 | all-reduce | flops 1024 | bytes 8192 | tf_op jit(solution)/shard_map/psum | solution.py:54
  140.8 2.7 %maximum_add_fusion = f32[1024,2,256]{0,2,1:T(8,128)S(1)} fusion(f32[512,2,256]{0,2,1:T(8,128)} %fusion.34, f32[512,2,256]{0,2,1:T(8,128)} %fusion.35, f32[2,256,1024]{2,1,0:T(8,128)} %get-tuple-element.26, f32[1024]{0:T(1024)S(1)} %add_sqrt_fusion, f32[2]{0:T(128)S(1)} %copy-done.10), kind=kLoop, calls=%fused_computation.10 | loop fusion | flops 2097152 | bytes 6295560 | tf_op jit(solution)/shard_map/add | solution.py:92
  143.6 1.8 %copy.73 = f32[1024,512]{1,0:T(8,128)} copy(f32[1024,512]{0,1:T(8,128)S(1)} %bitcast.164) | data formatting | bytes 4194304
  145.4 2.0 %copy.74 = f32[2,256,256]{2,1,0:T(8,128)} copy(f32[2,256,256]{1,2,0:T(8,128)} %get-tuple-element.16) | data formatting | bytes 1048576
  147.4 1.0 copy.75
  148.4 1.0 copy.76
  (23 shorter events, 0.1 us)
Async XLA Ops:
  7.2 13.7 %copy-start = (bf16[1024,512]{1,0:T(8,128)(2,1)S(1)}, bf16[1024,512]{1,0:T(8,128)(2,1)}, u32[]{:S(2)}) copy-start(bf16[1024,512]{1,0:T(8,128)(2,1)} %param.9) | copy-start | bytes 3145732
  7.2 13.6 %copy-start.7 = (f32[2,256,256]{2,1,0:T(8,128)S(1)}, f32[2,256,256]{2,1,0:T(8,128)}, u32[]{:S(2)}) copy-start(f32[2,256,256]{2,1,0:T(8,128)} %param.14) | copy-start | bytes 1572868
  7.2 117.1 %all-reduce.2.cloned.1.call-start = ((), (), s32[]{:S(2)}) async-start(), calls=%async_computation | async-start | bytes 3145728 | tf_op jit(solution)/shard_map/psum | solution.py:46
  9.2 53.2 %collective-permute-start = (bf16[512,512]{1,0:T(8,128)(2,1)}, bf16[512,512]{1,0:T(8,128)(2,1)}, u32[]{:S(2)}, u32[]{:S(2)}) collective-permute-start(bf16[512,512]{1,0:T(8,128)(2,1)} %slice.36), channel_id=1, source_target_pairs={{0,4},{4,8},{8,12},{12,16},{16,20},{20,24},{24,28},{1,5},{5,9},{9,... | collective-permute-start | bytes 1572872 | tf_op jit(solution)/shard_map/ppermute | solution.py:16
  17.2 4.6 %copy-start.8 = (f32[2,256,256]{2,1,0:T(8,128)S(1)}, f32[2,256,256]{2,1,0:T(8,128)}, u32[]{:S(2)}) copy-start(f32[2,256,256]{2,1,0:T(8,128)} %param.13) | copy-start | bytes 1572868
  17.2 49.6 %collective-permute-start.1 = (bf16[512,512]{0,1:T(8,128)(2,1)}, bf16[512,512]{0,1:T(8,128)(2,1)}, u32[]{:S(2)}, u32[]{:S(2)}) collective-permute-start(bf16[512,512]{0,1:T(8,128)(2,1)} %slice.47), channel_id=1, source_target_pairs={{0,4},{4,8},{8,12},{12,16},{16,20},{20,24},{24,28},{1,5},{5,9},{9,... | collective-permute-start | bytes 1572872 | tf_op jit(solution)/shard_map/ppermute | solution.py:16
  21.9 1.2 copy-start.1
  21.9 1.3 copy-start.6
  21.9 1.3 copy-start.9
  73.0 51.3 %copy-start.3 = (f32[2,256,256]{1,2,0:T(8,128)S(1)}, f32[2,256,256]{1,2,0:T(8,128)}, u32[]{:S(2)}) copy-start(f32[2,256,256]{1,2,0:T(8,128)} %copy.57) | copy-start | bytes 1572868
  73.0 51.3 %copy-start.4 = (f32[2,256,256]{1,2,0:T(8,128)S(1)}, f32[2,256,256]{1,2,0:T(8,128)}, u32[]{:S(2)}) copy-start(f32[2,256,256]{1,2,0:T(8,128)} %copy.56) | copy-start | bytes 1572868
  73.0 51.3 %copy-start.5 = (f32[2,256,256]{1,2,0:T(8,128)S(1)}, f32[2,256,256]{1,2,0:T(8,128)}, u32[]{:S(2)}) copy-start(f32[2,256,256]{1,2,0:T(8,128)} %copy.55) | copy-start | bytes 1572868
  124.3 2.1 %copy-start.2 = (f32[3,2,256,256]{2,3,1,0:T(8,128)S(1)}, f32[3,2,256,256]{2,3,1,0:T(8,128)}, u32[]{:S(2)}) copy-start(f32[3,2,256,256]{2,3,1,0:T(8,128)} %all-reduce.2.cloned.1.call-done) | copy-start | bytes 4718596
  129.2 1.0 copy-start.10
Sparse Core Ops, SparseCore 0:
  35.5 88.7 all-reduce.1
where the time goes:
time: 157 us; the launch traced here: 156 us
  waiting for transfers between devices  46.9 us (30%)
  matrix products  34.3 us (22%)
  local copies, waits for them, and re-layouts  27.7 us (18%)
  other arithmetic  17 us (11%)
  between operations  14.2 us (9%)
  starting transfers between devices  9.28 us (6%)
  blocking collectives  6.81 us (4%)
    psum x1, waiting for transfers between devices, per_device(): summed = lax.psum(grads, 'seq')  46.9 us
    unnamed x32, local copies, waits for them, and re-layouts  17.9 us
    ppermute x2, starting transfers between devices, passed_along(): return lax.ppermute(block, axis, route)  9.25 us
    psum x1, blocking collectives, per_device(): total_sq = lax.psum(local_sq, 'head')  6.81 us
    dot_general x2, matrix products, per_device(): jnp.einsum('hij,jhd->ihd', probs, value_block, preferred_element_type=jnp...  6.11 us
    sub x1, other arithmetic, per_device(): expo = jnp.exp(scores - top)  5.66 us
    sub x1, matrix products, per_device(): expo = jnp.exp(scores - top)  5 us
    dot_general x1, matrix products, per_device(): g2 = jnp.einsum('thi,thj->hij', act, scaled, precision=HIGH)  4.22 us
  transfers between devices with their start and end apart: 3, of which 1 were waited for; matrix products, arithmetic and copies ran while one was open for 37% of the time, Pallas kernels for 0%

commit v1 on v0

v1 whole, which is shorter than its diff:
```python
import functools

import jax
import jax.numpy as jnp
from jax import lax
from jax.experimental import pallas as pl
from jax.experimental.pallas import tpu as pltpu
from jax.sharding import PartitionSpec as P


WINDOW_SPAN = 512
EPS = 1e-06
PAD = 16
KIND = 0
ORDERS = ((3, 1, 2), (2, 1, 3))
WIRE = jnp.bfloat16
REACH = 120.0
BF = jnp.bfloat16
F32 = jnp.float32


def params(mib=24):
    return pltpu.CompilerParams(vmem_limit_bytes=mib * 1024 * 1024)


VM = pl.BlockSpec(memory_space=pltpu.VMEM)
SM = pl.BlockSpec(memory_space=pltpu.SMEM)
FAR = pl.BlockSpec(memory_space=pltpu.HBM)


def call(body, outs, args, specs=None, away=False, scratch=(), flops=0):
    many = isinstance(outs, (tuple, list))
    listed = list(outs) if many else [outs]
    away = list(away) if isinstance(away, tuple) else [away] * len(listed)
    made = [pltpu.HBM(o.shape, o.dtype) if a else pltpu.VMEM(o.shape, o.dtype) for o, a in zip(listed, away)]
    places = [FAR if a else VM for a in away]
    return pl.pallas_call(
        body,
        out_shape=tuple(made) if many else made[0],
        in_specs=specs or [VM] * len(args),
        out_specs=tuple(places) if many else places[0],
        scratch_shapes=list(scratch),
        compiler_params=params(),
        cost_estimate=pl.CostEstimate(flops=flops or 1 << 24, bytes_accessed=1 << 21, transcendentals=0),
    )(*args)


def spec(shape, dtype):
    return jax.ShapeDtypeStruct(shape, dtype)


def nn(a, b):
    return lax.dot_general(a, b, (((1,), (0,)), ((), ())), preferred_element_type=F32)


def nt(a, b):
    return lax.dot_general(a, b, (((1,), (1,)), ((), ())), preferred_element_type=F32)


def split(x):
    high = x.astype(BF)
    return high, (x - high.astype(F32)).astype(BF)


def encode(x, ref):
    rows, size = x.shape
    top = jnp.max(jnp.abs(x), axis=1, keepdims=True)
    scale = (jnp.maximum(top, 1e-30) * 1.008).astype(WIRE).astype(F32)
    code = jnp.exp2(jnp.abs(x) * (2.0 * REACH / scale) - REACH)
    ref[0:rows] = jnp.where(x < 0, -code, code).astype(WIRE)
    column = jnp.concatenate([scale, jnp.zeros((size - rows, 1), F32)], axis=0)
    ref[rows : rows + PAD] = jnp.broadcast_to(column, (size, 128)).T[0:PAD].astype(WIRE)


def decode(ref):
    rows = ref.shape[0] - PAD
    scale = ref[rows : rows + PAD].astype(F32).T[0:rows, 0:1]
    code = ref[0:rows].astype(F32)
    size = (jnp.log2(jnp.abs(code)) + REACH) * (scale * (0.5 / REACH))
    return jnp.where(code < 0, -size, size)


def grads_body(quarter, q_far, k_far, v_far, r_far, w1_far, w3_far, w2_far, *refs):
    own_ref, p1_ref, p2_ref, p3_ref, mine_far, q_ref, k_ref, v_ref, *tails = refs[:-7]
    acc, part, r_ref, w1_ref, w3_ref, w2_ref, sems = refs[-7:]
    heads, size = w1_ref.shape[0], w1_ref.shape[1]
    tokens = k_ref.shape[0]
    step = min(256, tokens)
    count = tokens // step
    used = []

    def copy(source, target):
        made = pltpu.make_async_copy(source, target, sems.at[len(used)])
        made.start()
        used.append(made)
        return made

    def block(ref, index):
        return ref.at[index * step : (index + 1) * step]

    def fetch(index):
        return copy(block(k_far, index), block(k_ref, index)), copy(block(v_far, index), block(v_ref, index))

    first = [copy(w1_far, w1_ref)]
    coming = [fetch(0)]
    first += [copy(w3_far, w3_ref), copy(w2_far, w2_ref), copy(r_far, r_ref)]
    coming += [fetch(index) for index in range(1, count)]
    late = [copy(q_far, q_ref)]
    rows = 3 * size // 4
    q = quarter[0]
    own_rows = pl.ds(pl.multiple_of(q * rows, 8), rows)
    halves = []
    for made in first:
        made.wait()
    for head in range(heads):
        w1t, w3t, w2 = w1_ref[head].T, w3_ref[head].T, w2_ref[head]
        halves.append((*split(w1t), *split(w3t), *split(w2)))
        acc[0:size] = w1t
        acc[size : 2 * size] = w3t
        acc[2 * size : 3 * size] = w2.T
        part[head] = acc[own_rows]
        late.append(copy(part.at[head], mine_far.at[head]))
    sums = [None] * heads
    edge = tokens - WINDOW_SPAN
    for index in range(count):
        for made in coming[index]:
            made.wait()
        start = index * step
        if start >= edge:
            late.append(copy(block(v_ref, index), tails[(start - edge) // step]))
        for head in range(heads):
            w1h, w1l, w3h, w3l, w2h, w2l = halves[head]
            cols = slice(head * size, (head + 1) * size)
            kb = k_ref[start : start + step, cols]
            vb = v_ref[start : start + step, cols]
            rate = r_ref[head : head + 1, start : start + step]
            h1 = nt(w1h, kb) + nt(w1l, kb)
            h3 = nt(w3h, kb) + nt(w3l, kb)
            da = (nt(w2h, vb) + nt(w2l, vb)) * rate
            sg = 1.0 / (1.0 + jnp.exp(-h1))
            sil = h1 * sg
            act = sil * h3 * rate
            d3 = da * sil
            d1 = da * h3 * (sg * (1.0 + h1 * (1.0 - sg)))
            ah, al = split(act)
            d1h, d1l = split(d1)
            d3h, d3l = split(d3)
            new = (nn(d1h, kb) + nn(d1l, kb), nn(d3h, kb) + nn(d3l, kb), nn(ah, vb) + nn(al, vb))
            sums[head] = new if sums[head] is None else tuple(x + y for x, y in zip(sums[head], new))
    for head in range(heads):
        g1, g3, g2 = sums[head]
        acc[0:size] = g1
        acc[size : 2 * size] = g3
        acc[2 * size : 3 * size] = g2.T
        own_ref[head] = acc[own_rows]
        for j, ref in ((1, p1_ref), (2, p2_ref), (3, p3_ref)):
            encode(acc[pl.ds(pl.multiple_of((q ^ j) * rows, 8), rows)], ref.at[head])
    for made in late:
        made.wait()


def far(*args):
    return [pltpu.with_memory_space_constraint(a, pltpu.HBM) for a in args]


def near(*args):
    return [pltpu.with_memory_space_constraint(a, pltpu.VMEM) for a in args]


def grads(quarter, queries, keys, values, rates_t, w1, w3, w2):
    heads, size = w1.shape[0], w1.shape[1]
    rows = 3 * size // 4
    whole = pltpu.VMEM(w1.shape, F32)
    step = min(256, keys.shape[0])
    pieces = WINDOW_SPAN // step
    scratch = (
        pltpu.VMEM((3 * size, size), F32),
        pltpu.VMEM((heads, rows, size), F32),
        pltpu.VMEM(rates_t.shape, F32),
        whole,
        whole,
        whole,
        pltpu.SemaphoreType.DMA((4 + 2 * (keys.shape[0] // step) + 1 + heads + pieces,)),
    )
    wire = spec((heads, rows + PAD, size), WIRE)
    part = spec((heads, rows, size), F32)
    inputs = [spec(a.shape, a.dtype) for a in (queries, keys, values)]
    tail = spec((step, keys.shape[1]), keys.dtype)
    outs = (part, wire, wire, wire, part, *inputs, *[tail] * pieces)
    away = (False, False, False, False, True, False, False, False, *[True] * pieces)
    args = (quarter, *far(queries, keys, values, rates_t, w1, w3, w2))
    out = call(grads_body, outs, args, [SM] + [FAR] * 7, away, scratch, 1 << 31)
    return out[:8], out[8:]


def tail_body(k_far, out_ref, sems):
    edge = k_far.shape[0] - WINDOW_SPAN
    half = WINDOW_SPAN // 2
    copies = [
        pltpu.make_async_copy(k_far.at[edge + at : edge + at + half], out_ref.at[at : at + half], sems.at[at // half])
        for at in (0, half)
    ]
    for made in copies:
        made.start()
    for made in copies:
        made.wait()


def tail(keys):
    out = spec((WINDOW_SPAN, keys.shape[1]), keys.dtype)
    return call(tail_body, out, far(keys), [FAR], False, (pltpu.SemaphoreType.DMA((2,)),))


class Rows:
    def __init__(self, ref, head, size, step):
        self.ref, self.step, self.count = ref, step, ref.shape[0] // step
        self.cols = slice(head * size, (head + 1) * size)

    def at(self, index):
        return self.ref.at[index * self.step : (index + 1) * self.step, self.cols]

    def __call__(self, index):
        return self.ref[index * self.step : (index + 1) * self.step, self.cols]


def heads_of(ref):
    return range(ref.shape[0])


def gather_body(own_ref, r1_ref, r2_ref, r3_ref, out_ref):
    for h in heads_of(out_ref):
        pair = decode(r2_ref.at[h]) + decode(r3_ref.at[h])
        encode(own_ref[h] + decode(r1_ref.at[h]) + pair, out_ref.at[h])


def cross_body(mine_ref, other_ref, out_ref):
    for h in heads_of(out_ref):
        encode(decode(mine_ref.at[h]) + decode(other_ref.at[h]), out_ref.at[h])


def renorm_body(w_far, mine_ref, other_ref, out_ref, w_ref, sem):
    fetch = pltpu.make_async_copy(w_far, w_ref, sem)
    fetch.start()
    sums = [decode(mine_ref.at[h]) + decode(other_ref.at[h]) for h in heads_of(out_ref)]
    fetch.wait()
    for h, total in enumerate(sums):
        w = w_ref[h]
        upd = w + total
        old = jnp.sqrt(jnp.sum(w * w, axis=1, keepdims=True) + EPS)
        cur = jnp.sqrt(jnp.sum(upd * upd, axis=1, keepdims=True) + EPS)
        encode(upd * (old / cur), out_ref.at[h])


def apply_body(quarter, s_ref, q_ref, own_ref, r1_ref, r2_ref, r3_ref, z_ref, sq_ref, n_ref):
    heads, rows, size = own_ref.shape
    rows -= PAD
    tokens = q_ref.shape[0]
    q = quarter[0]
    block = min(256, tokens)
    for head in range(heads):
        for j, ref in enumerate((own_ref, r1_ref, r2_ref, r3_ref)):
            n_ref[head, pl.ds(pl.multiple_of((q ^ j) * rows, 8), rows)] = decode(ref.at[head])
        n1h, n1l = split(n_ref[head, 0:size])
        n3h, n3l = split(n_ref[head, size : 2 * size])
        n2h, n2l = split(n_ref[head, 2 * size : 3 * size])
        scale = s_ref[head]
        for start in range(0, tokens, block):
            qb = q_ref[start : start + block, head * size : (head + 1) * size]
            p1 = nt(qb, n1h) + nt(qb, n1l)
            p3 = nt(qb, n3h) + nt(qb, n3l)
            hh, hl = split(p1 * (1.0 / (1.0 + jnp.exp(-p1))) * p3)
            zed = (nt(hh, n2h) + nt(hl, n2h) + nt(hh, n2l)) * scale
            z_ref[start : start + block, head * size : (head + 1) * size] = zed
            zz = zed * zed
            half = zz[:, 0:128]
            for lane in range(128, size, 128):
                half = half + zz[:, lane : lane + 128]
            found = jnp.sum(half.T, axis=0, keepdims=True)
            if head == 0:
                sq_ref[:, start : start + block] = found
            else:
                sq_ref[:, start : start + block] += found


def apply(quarter, queries, scale, pieces):
    heads, _, size = pieces[0].shape
    tokens = queries.shape[0]
    outs = (spec((tokens, heads * size), F32), spec((1, tokens), F32), spec((heads, 3 * size, size), F32))
    args = (quarter, scale, queries, *pieces)
    return call(apply_body, outs, args, [SM, SM] + [VM] * 5, flops=1 << 31)


def weights_body(n_ref, o1, o3, o2, buf, sems):
    size = o1.shape[1]
    copies = []
    for head in heads_of(n_ref):
        for place, out in enumerate((o1, o3, o2)):
            index = 3 * head + place
            buf[index] = n_ref[head, place * size : (place + 1) * size].T
            made = pltpu.make_async_copy(buf.at[index], out.at[head], sems.at[index])
            made.start()
            copies.append(made)
    for made in copies:
        made.wait()


def weights(new):
    heads, _, size = new.shape
    square = spec((heads, size, size), F32)
    scratch = (pltpu.VMEM((3 * heads, size, size), F32), pltpu.SemaphoreType.DMA((3 * heads,)))
    return call(weights_body, (square,) * 3, (new,), away=True, scratch=scratch)


def attend_body(size, blocks, *refs):
    for head in range(refs[-1].shape[1] // size):
        attend_head(head, size, blocks, *refs)


def attend_head(head, size, blocks, first_ref, q_ref, k_ref, v_ref, *refs):
    halo = refs[:-1]
    out_ref = refs[-1]
    step = 256
    span = WINDOW_SPAN // step
    scale = size ** (-0.5)
    q, k, v = (Rows(ref, head, size, step) for ref in (q_ref, k_ref, v_ref))
    rows = lax.broadcasted_iota(jnp.int32, (step, step), 0)
    cols = lax.broadcasted_iota(jnp.int32, (step, step), 1)
    for place, block in enumerate(blocks):
        qb = q(block)
        scores, vals = [], []
        for back in range(span, -1, -1):
            source = block - back
            if source < 0:
                at = (source + span) * step
                kb, vb = halo[0][at : at + step, q.cols], halo[1 + at // step][:, q.cols]
            else:
                kb, vb = k(source), v(source)
            s = nt(qb, kb) * scale
            allowed = None
            if back == 0:
                allowed = cols <= rows
            if back == span:
                allowed = cols > rows
            if source < 0:
                here = first_ref[0] == 0
                allowed = here if allowed is None else allowed & here
            if allowed is not None:
                s = jnp.where(allowed, s, -jnp.inf)
            scores.append(s)
            vals.append(vb)
        top = scores[0].max(axis=-1, keepdims=True)
        for s in scores[1:]:
            top = jnp.maximum(top, s.max(axis=-1, keepdims=True))
        expo = [jnp.exp(s - top) for s in scores]
        total = expo[0].sum(axis=-1, keepdims=True)
        for x in expo[1:]:
            total = total + x.sum(axis=-1, keepdims=True)
        inverse = 1.0 / total
        out = None
        for x, vb in zip(expo, vals):
            part = nn((x * inverse).astype(BF), vb)
            out = part if out is None else out + part
        out_ref[place * step : (place + 1) * step, q.cols] = out


def attend(first, queries, keys, values, halo, blocks, size):
    args = (first, queries, keys, values) + (() if halo is None else tuple(halo))
    return call(
        functools.partial(attend_body, size, blocks),
        spec((len(blocks) * 256, queries.shape[1]), F32),
        args,
        [SM] + [VM] * (len(args) - 1),
        flops=1 << 30,
    )


def mix_body(features, r_ref, z_ref, a_ref, b_ref, out, buf, sems):
    tokens = buf.shape[0]
    step = 128
    half = tokens // 2
    inverse = 1.0 / jnp.sqrt(r_ref[...] / features + EPS)
    copies = []
    for index in range(tokens // step):
        start = index * step
        column = jnp.broadcast_to(inverse[:, start : start + step], (128, step)).T[:, 0:1]
        attn = a_ref[start : start + step] if start < half else b_ref[start - half : start - half + step]
        buf[start : start + step] = attn + z_ref[start : start + step] * column
        made = pltpu.make_async_copy(buf.at[start : start + step], out.at[start : start + step], sems.at[index])
        made.start()
        copies.append(made)
    for made in copies:
        made.wait()


def mix(total, z, low, high, features):
    scratch = (pltpu.VMEM(z.shape, F32), pltpu.SemaphoreType.DMA((z.shape[0] // 128,)))
    args = (total, z, low, high)
    return call(functools.partial(mix_body, features), spec(z.shape, F32), args, away=True, scratch=scratch)


def swap(x, axis, mask):
    return lax.ppermute(x, axis, [(i, i ^ mask) for i in range(lax.axis_size(axis))])


def after(x, *others):
    return lax.optimization_barrier((x, *others))[0]


def plan(place, devices, kind):
    bits = [(place >> n) & 1 for n in range(3)]
    rest = [1 << n for n in range(3, devices.bit_length() - 1)]
    if kind == 0:
        return bits[0] + 2 * (bits[1] ^ bits[2]), (1, 2, 3), ORDERS[0], [6, *rest]
    return bits[1] + 2 * bits[2], (2, 4, 6), ORDERS[1], [1, *rest]


def per_device(queries, keys, values, rates, head_scale, w_one, w_three, w_two):
    tokens, _ = queries.shape
    heads, size = w_one.shape[0], w_one.shape[1]
    rows = 3 * size // 4
    devices = lax.axis_size("seq")
    place = lax.axis_index("seq").astype(jnp.int32)
    first = (place == 0).astype(jnp.int32).reshape(1)
    blocks = tuple(range(tokens // 256))
    half = len(blocks) // 2
    wire = spec((heads, rows + PAD, size), WIRE)
    ring = [(i, (i + 1) % devices) for i in range(devices)]
    quarter, masks, order, shared = plan(place, devices, KIND)
    quarter = quarter.reshape(1)

    def spread(parts):
        out = {}
        for j in order:
            out[j] = near(swap(parts[j - 1], "seq", masks[j - 1]))[0]
        return out[1], out[2], out[3]

    halo = [lax.ppermute(tail(keys), "seq", ring)]
    out, ends = grads(quarter, queries, keys, values, rates.T, w_one, w_three, w_two)
    own, p1, p2, p3, mine_w, q, k, v = out
    got = spread((p1, p2, p3))
    halo.append(lax.ppermute(ends[0], "seq", ring))
    high = attend(first, q, k, v, None, blocks[half:], size)
    mine = call(gather_body, wire, (after(own, high), *got))
    for mask in shared[:-1]:
        mine = call(cross_body, wire, (mine, swap(mine, "seq", mask)))
    other = near(swap(mine, "seq", shared[-1]))[0]
    for place, end in enumerate(ends[1:], 1):
        halo.append(lax.ppermute(after(end, mine), "seq", ring))
    scratch = (pltpu.VMEM((heads, rows, size), F32), pltpu.SemaphoreType.DMA)
    new = call(renorm_body, wire, (mine_w, mine, other), [FAR, VM, VM], scratch=scratch)
    pieces = (new, *spread((new, new, new)))
    low = attend(first, q, after(k, new), v, halo, blocks[:half], size)
    pieces = (after(new, low), *pieces[1:])
    zed, total, new_t = apply(quarter, q, head_scale, pieces)
    mask = 1
    while mask < lax.axis_size("head"):
        total = total + swap(total, "head", mask)
        mask *= 2
    new_one, new_three, new_two = weights(new_t)
    mixed = mix(total, zed, low, high, heads * lax.axis_size("head") * size)
    return (mixed, new_one, new_three, new_two)


def solution(mesh):
    placed = (
        P("seq", "head"),
        P("seq", "head"),
        P("seq", "head"),
        P("seq", "head"),
        P("head"),
        P("head", None, None),
        P("head", None, None),
        P("head", None, None),
    )
    return jax.shard_map(
        per_device,
        mesh=mesh,
        in_specs=placed,
        out_specs=(
            P("seq", "head"),
            P("head", None, None),
            P("head", None, None),
            P("head", None, None),
        ),
        check_vma=False,
    )
```

time: 157 us -> 82.3 us (0.52)
  matrix products: 34.3 us -> 0 us
  waiting for transfers between devices: 46.9 us -> 14.9 us
  starting transfers between devices: 9.28 us -> 40.1 us
  local copies, waits for them, and re-layouts: 27.7 us -> 0.01 us
  Pallas kernels: 0 us -> 26.2 us
  other arithmetic: 17 us -> 0.01 us
  between operations: 14.2 us -> 0.89 us
  blocking collectives: 6.81 us -> 0 us
    psum x1 -> x0, waiting for transfers between devices: 46.9 us -> none  [per_device(): summed = lax.psum(grads, 'seq')]
    ppermute x2 -> x12, starting transfers between devices: 9.25 us -> 40.1 us  [the longest x9 36.4 us: swap(): lax.ppermute(x, axis, [(i, i ^ mask) for i in range(lax.axis_size(axis))])]
    dot_general x12 -> x0, matrix products: 29.3 us -> none  [the longest x2 6.11 us: per_device(): jnp.einsum('hij,jhd->ihd', probs, value_block, preferred_element_type=jnp...]
    pallas_call x0 -> x9, Pallas kernels: none -> 26.2 us  [call(): pl.pallas_call(body, out_shape=tuple(made) if many else made[0], in_specs...]
    unnamed x32 -> x6, local copies, waits for them, and re-layouts: 17.9 us -> 0.01 us
    ppermute x2 -> x12, waiting for transfers between devices: 0.01 us -> 14.9 us  [the longest x9 14.9 us: swap(): lax.ppermute(x, axis, [(i, i ^ mask) for i in range(lax.axis_size(axis))])]
    slice x4 -> x0, local copies, waits for them, and re-layouts: 7.37 us -> none  [the longest x1 2.29 us: per_device(): ext_values[start_offset:start_offset + block_span + WINDOW_SPAN]]
    psum x1 -> x0, blocking collectives: 6.81 us -> none  [per_device(): total_sq = lax.psum(local_sq, 'head')]
  transfers between devices with their start and end apart: 3 -> 12, of which waited for: 1 -> 7; matrix products, arithmetic and copies ran while one was open for 37% -> 0% of each run, Pallas kernels for 0% -> 14%
where the time goes in v1:
time: 82.3 us; the launch traced here: 82.1 us
  starting transfers between devices  40.1 us (49%)
  Pallas kernels  26.2 us (32%)
  waiting for transfers between devices  14.9 us (18%)
  between operations  0.89 us (1%)
    ppermute x9, starting transfers between devices, swap(): lax.ppermute(x, axis, [(i, i ^ mask) for i in range(lax.axis_size(axis))])  36.4 us
    pallas_call x9, Pallas kernels, call(): pl.pallas_call(body, out_shape=tuple(made) if many else made[0], in_specs...  26.2 us
    ppermute x9, waiting for transfers between devices, swap(): lax.ppermute(x, axis, [(i, i ^ mask) for i in range(lax.axis_size(axis))])  14.9 us
    ppermute x1, starting transfers between devices, per_device(): halo = [lax.ppermute(tail(keys), 'seq', ring)]  1.97 us
  transfers between devices with their start and end apart: 12, of which 7 were waited for; matrix products, arithmetic and copies ran while one was open for 0% of the time, Pallas kernels for 14%

profile of v1, /device:TPU:0, one launch (start us, length us, event | category | flops | bytes accessed | tf_op | source)
XLA Modules:
  0.0 82.1 jit_solution(9948079614481887160)
XLA Ops:
  0.6 9.0 %shard_map.111 = (f32[2,192,256]{2,1,0:T(8,128)S(1)}, bf16[2,208,256]{2,1,0:T(8,128)(2,1)}, bf16[2,208,256]{2,1,0:T(8,128)(2,1)}, bf16[2,208,256]{2,1,0:T(8,128)...) custom-call(s32[1]{0:T(128)} %bitcast.quarter, ...), custom_call_target="tpu_custom_call" | custom-call | flops 2147483648 | bytes 2097152 | tf_op jit(solution)/shard_map/pallas_call | solution.py:37
  9.7 3.0 %collective-permute-start = (bf16[2,208,256]{2,1,0:T(8,128)(2,1)}, bf16[2,208,256]{2,1,0:T(8,128)(2,1)}, u32[]{:S(2)}, u32[]{:S(2)}) collective-permute-start(bf16[2,208,256]{2,1,0:T(8,128)(2,1)} %get-tuple-element.30), channel_id=1, source_target_pairs={{0,4},{4,0},{8,12},{12,8},{16,20},{20,16},{24,28},{28,24},{1,5},{5... | collective-permute-start | bytes 638984 | tf_op jit(solution)/shard_map/ppermute | solution.py:402
  12.7 1.6 %collective-permute-start.1 = (bf16[2,208,256]{2,1,0:T(8,128)(2,1)}, bf16[2,208,256]{2,1,0:T(8,128)(2,1)}, u32[]{:S(2)}, u32[]{:S(2)}) collective-permute-start(bf16[2,208,256]{2,1,0:T(8,128)(2,1)} %get-tuple-element.31), channel_id=1, source_target_pairs={{0,8},{4,12},{8,0},{12,4},{16,24},{20,28},{24,16},{28,20},{1,9},{5... | collective-permute-start | bytes 638984 | tf_op jit(solution)/shard_map/ppermute | solution.py:402
  14.3 0.0 collective-permute-start.2
  14.3 1.8 %shard_map.115 = bf16[512,512]{1,0:T(8,128)(2,1)} custom-call(bf16[1024,512]{1,0:T(8,128)(2,1)} %k_far.3), custom_call_target="tpu_custom_call" | custom-call | flops 16777216 | bytes 2097152 | tf_op jit(solution)/shard_map/pallas_call | solution.py:37
  16.1 2.0 %collective-permute-start.4 = (bf16[512,512]{1,0:T(8,128)(2,1)}, bf16[512,512]{1,0:T(8,128)(2,1)}, u32[]{:S(2)}, u32[]{:S(2)}) collective-permute-start(bf16[512,512]{1,0:T(8,128)(2,1)} %shard_map.115), channel_id=1, source_target_pairs={{0,4},{4,8},{8,12},{12,16},{16,20},{20,24},{24,28},{28,0},{1,5},{5... | collective-permute-start | bytes 1572872 | tf_op jit(solution)/shard_map/ppermute | solution.py:437
  18.1 1.6 %collective-permute-start.5 = (bf16[256,512]{1,0:T(8,128)(2,1)}, bf16[256,512]{1,0:T(8,128)(2,1)}, u32[]{:S(2)}, u32[]{:S(2)}) collective-permute-start(bf16[256,512]{1,0:T(8,128)(2,1)} %get-tuple-element.34), channel_id=1, source_target_pairs={{0,4},{4,8},{8,12},{12,16},{16,20},{20,24},{24,28},{28,0},{1,5},{5... | collective-permute-start | bytes 786440 | tf_op jit(solution)/shard_map/ppermute | solution.py:441
  19.7 0.0 copy-start.2
  19.7 0.0 copy-start
  19.7 1.7 %shard_map.112.b_ref = f32[512,512]{1,0:T(8,128)S(1)} custom-call(s32[1]{0:T(128)} %bitcast.2.refs_0_, bf16[1024,512]{1,0:T(8,128)(2,1)S(1)} %get-tuple-element.24.refs_1_.q_ref, bf16[1024,512]{1,0:T(8,128)(2,1)S(1)} %get-tuple-element.33.refs_2_, bf16[1024,512]{1,0:T(8,128)(2,1)S(1)} %get-tuple-element.28.refs_3_), custom_call_target="tpu_custom_call" | custom-call | flops 1073741824 | bytes 2097152 | tf_op jit(solution)/shard_map/pallas_call | solution.py:37
  21.4 0.0 collective-permute-done.r1_ref
  21.4 0.0 collective-permute-done.1.r2_ref
  21.4 2.7 %collective-permute-done.2.r3_ref = bf16[2,208,256]{2,1,0:T(8,128)(2,1)} collective-permute-done((bf16[2,208,256]{2,1,0:T(8,128)(2,1)}, bf16[2,208,256]{2,1,0:T(8,128)(2,1)}, u32[]{:S(2)}, u32[]{:S(2)}) %collective-permute-start.2) | collective-permute-done | bytes 213024 | tf_op jit(solution)/shard_map/ppermute | solution.py:402
  24.1 2.2 %shard_map.113.mine_ref = bf16[2,208,256]{2,1,0:T(8,128)(2,1)S(1)} custom-call(f32[2,192,256]{2,1,0:T(8,128)S(1)} %get-tuple-element.29.own_ref, bf16[2,208,256]{2,1,0:T(8,128)(2,1)} %collective-permute-done.r1_ref, bf16[2,208,256]{2,1,0:T(8,128)(2,1)} %collective-permute-done.1.r2_ref, bf16[2,208,256]{2,1,0:T(8,128)(2,1)} %collective-permute-done.2.r3_ref), custom_call_target="tpu_custom_call" | custom-call | flops 16777216 | bytes 2097152 | tf_op jit(solution)/shard_map/pallas_call | solution.py:37
  26.3 5.2 %collective-permute-start.3 = (bf16[2,208,256]{2,1,0:T(8,128)(2,1)S(1)}, bf16[2,208,256]{2,1,0:T(8,128)(2,1)S(1)}, u32[]{:S(2)}, u32[]{:S(2)}) collective-permute-start(bf16[2,208,256]{2,1,0:T(8,128)(2,1)S(1)} %shard_map.113.mine_ref), channel_id=1, source_target_pairs={{0,24},{4,28},{8,16},{12,20},{16,8},{20,12},{24,0},{28,4},{1,25},{... | collective-permute-start | bytes 638984 | tf_op jit(solution)/shard_map/ppermute | solution.py:402
  31.5 0.0 copy-done.2
  31.5 0.2 collective-permute-start.6
  31.7 3.8 %collective-permute-done.3.other_ref = bf16[2,208,256]{2,1,0:T(8,128)(2,1)S(1)} collective-permute-done((bf16[2,208,256]{2,1,0:T(8,128)(2,1)S(1)}, bf16[2,208,256]{2,1,0:T(8,128)(2,1)S(1)}, u32[]{:S(2)}, u32[]{:S(2)}) %collective-permute-start.3) | collective-permute-done | bytes 213024 | tf_op jit(solution)/shard_map/ppermute | solution.py:402
  35.5 0.0 copy-done
  35.5 1.2 %shard_map.114.own_ref = bf16[2,208,256]{2,1,0:T(8,128)(2,1)S(1)} custom-call(f32[2,192,256]{2,1,0:T(8,128)S(1)} %copy-done, bf16[2,208,256]{2,1,0:T(8,128)(2,1)S(1)} %shard_map.113.mine_ref, bf16[2,208,256]{2,1,0:T(8,128)(2,1)S(1)} %collective-permute-done.3.other_ref), custom_call_target="tpu_custom_call" | custom-call | flops 16777216 | bytes 2097152 | tf_op jit(solution)/shard_map/pallas_call | solution.py:37
  36.7 0.0 copy-start.1
  36.7 24.3 %collective-permute-start.9 = (bf16[2,208,256]{2,1,0:T(8,128)(2,1)S(1)}, bf16[2,208,256]{2,1,0:T(8,128)(2,1)S(1)}, u32[]{:S(2)}, u32[]{:S(2)}) collective-permute-start(bf16[2,208,256]{2,1,0:T(8,128)(2,1)S(1)} %shard_map.114.own_ref), channel_id=1, source_target_pairs={{0,12},{4,8},{8,4},{12,0},{16,28},{20,24},{24,20},{28,16},{1,13},{... | collective-permute-start | bytes 638984 | tf_op jit(solution)/shard_map/ppermute | solution.py:402
  61.0 0.0 collective-permute-start.8
  61.0 0.0 collective-permute-done.5.refs_5_
  61.0 0.6 collective-permute-start.7
  61.7 0.0 collective-permute-done.6.refs_6_
  61.7 0.0 collective-permute-done.4.refs_4_
  61.7 2.8 %shard_map.116.a_ref = f32[512,512]{1,0:T(8,128)S(1)} custom-call(s32[1]{0:T(128)} %bitcast.2.refs_0_, bf16[1024,512]{1,0:T(8,128)(2,1)S(1)} %get-tuple-element.24.refs_1_.q_ref, bf16[1024,512]{1,0:T(8,128)(2,1)S(1)} %get-tuple-element.33.refs_2_, bf16[1024,512]{1,0:T(8,128)(2,1)S(1)} %get-tuple-element.28.refs_3_, ...), custom_call_target="tpu_custom_call" | custom-call | flops 1073741824 | bytes 2097152 | tf_op jit(solution)/shard_map/pallas_call | solution.py:37
  64.5 2.7 %collective-permute-done.9.r3_ref = bf16[2,208,256]{2,1,0:T(8,128)(2,1)S(1)} collective-permute-done((bf16[2,208,256]{2,1,0:T(8,128)(2,1)S(1)}, bf16[2,208,256]{2,1,0:T(8,128)(2,1)S(1)}, u32[]{:S(2)}, u32[]{:S(2)}) %collective-permute-start.9) | collective-permute-done | bytes 213024 | tf_op jit(solution)/shard_map/ppermute | solution.py:402
  67.2 3.2 %collective-permute-done.8.r2_ref = bf16[2,208,256]{2,1,0:T(8,128)(2,1)S(1)} collective-permute-done((bf16[2,208,256]{2,1,0:T(8,128)(2,1)S(1)}, bf16[2,208,256]{2,1,0:T(8,128)(2,1)S(1)}, u32[]{:S(2)}, u32[]{:S(2)}) %collective-permute-start.8) | collective-permute-done | bytes 213024 | tf_op jit(solution)/shard_map/ppermute | solution.py:402
  70.3 0.7 collective-permute-done.7.r1_ref
  71.0 0.0 copy-done.1
  71.0 4.4 %shard_map.117 = (f32[1024,512]{1,0:T(8,128)S(1)}, f32[1,1024]{1,0:T(1,128)S(1)}, f32[2,768,256]{2,1,0:T(8,128)S(1)}) custom-call(s32[1]{0:T(128)} %bitcast.quarter, f32[2]{0:T(128)S(1)} %copy-done.1, bf16[1024,512]{1,0:T(8,128)(2,1)S(1)} %get-tuple-element.24.refs_1_.q_ref, bf16[2,208,256]{2,1,0:T(8,128)(2,1)S(1)} %shard_map.114.own_ref, ...), custom_call_target="tpu_custom_call" | custom-call | flops 2147483648 | bytes 2097152 | tf_op jit(solution)/shard_map/pallas_call | solution.py:37
  75.4 0.1 collective-permute-start.10
  75.5 1.2 %collective-permute-done.10 = f32[1,1024]{1,0:T(1,128)S(1)} collective-permute-done((f32[1,1024]{1,0:T(1,128)S(1)}, f32[1,1024]{1,0:T(1,128)S(1)}, u32[]{:S(2)}, u32[]{:S(2)}) %collective-permute-start.10) | collective-permute-done | bytes 4128 | tf_op jit(solution)/shard_map/ppermute | solution.py:402
  76.7 1.5 %collective-permute-start.11 = (f32[1,1024]{1,0:T(1,128)S(1)}, f32[1,1024]{1,0:T(1,128)S(1)}, u32[]{:S(2)}, u32[]{:S(2)}) collective-permute-start(f32[1,1024]{1,0:T(1,128)S(1)} %add.10), channel_id=1, source_target_pairs={{0,2},{1,3},{2,0},{3,1},{4,6},{5,7},{6,4},{7,5},{8,10},{9,11},{10,... | collective-permute-start | bytes 12296 | tf_op jit(solution)/shard_map/ppermute | solution.py:402
  78.1 1.3 %shard_map.119 = (f32[2,256,256]{2,1,0:T(8,128)}, f32[2,256,256]{2,1,0:T(8,128)}, f32[2,256,256]{2,1,0:T(8,128)}) custom-call(f32[2,768,256]{2,1,0:T(8,128)S(1)} %get-tuple-element.40.n_ref), custom_call_target="tpu_custom_call" | custom-call | flops 16777216 | bytes 2097152 | tf_op jit(solution)/shard_map/pallas_call | solution.py:37
  79.5 0.8 collective-permute-done.11
  80.3 1.6 %shard_map.118 = f32[1024,512]{1,0:T(8,128)} custom-call(f32[1,1024]{1,0:T(1,128)S(1)} %add.11.r_ref, f32[1024,512]{1,0:T(8,128)S(1)} %get-tuple-element.39.z_ref, f32[512,512]{1,0:T(8,128)S(1)} %shard_map.116.a_ref, f32[512,512]{1,0:T(8,128)S(1)} %shard_map.112.b_ref), custom_call_target="tpu_custom_call" | custom-call | flops 16777216 | bytes 2097152 | tf_op jit(solution)/shard_map/pallas_call | solution.py:37
  (2 shorter events, 0.0 us)
Async XLA Ops:
  9.7 11.7 %collective-permute-start = (bf16[2,208,256]{2,1,0:T(8,128)(2,1)}, bf16[2,208,256]{2,1,0:T(8,128)(2,1)}, u32[]{:S(2)}, u32[]{:S(2)}) collective-permute-start(bf16[2,208,256]{2,1,0:T(8,128)(2,1)} %get-tuple-element.30), channel_id=1, source_target_pairs={{0,4},{4,0},{8,12},{12,8},{16,20},{20,16},{24,28},{28,24},{1,5},{5... | collective-permute-start | bytes 638984 | tf_op jit(solution)/shard_map/ppermute | solution.py:402
  12.7 8.7 %collective-permute-start.1 = (bf16[2,208,256]{2,1,0:T(8,128)(2,1)}, bf16[2,208,256]{2,1,0:T(8,128)(2,1)}, u32[]{:S(2)}, u32[]{:S(2)}) collective-permute-start(bf16[2,208,256]{2,1,0:T(8,128)(2,1)} %get-tuple-element.31), channel_id=1, source_target_pairs={{0,8},{4,12},{8,0},{12,4},{16,24},{20,28},{24,16},{28,20},{1,9},{5... | collective-permute-start | bytes 638984 | tf_op jit(solution)/shard_map/ppermute | solution.py:402
  14.3 9.8 %collective-permute-start.2 = (bf16[2,208,256]{2,1,0:T(8,128)(2,1)}, bf16[2,208,256]{2,1,0:T(8,128)(2,1)}, u32[]{:S(2)}, u32[]{:S(2)}) collective-permute-start(bf16[2,208,256]{2,1,0:T(8,128)(2,1)} %get-tuple-element.32), channel_id=1, source_target_pairs={{0,12},{4,8},{8,4},{12,0},{16,28},{20,24},{24,20},{28,16},{1,13},{... | collective-permute-start | bytes 638984 | tf_op jit(solution)/shard_map/ppermute | solution.py:402
  16.1 45.5 %collective-permute-start.4 = (bf16[512,512]{1,0:T(8,128)(2,1)}, bf16[512,512]{1,0:T(8,128)(2,1)}, u32[]{:S(2)}, u32[]{:S(2)}) collective-permute-start(bf16[512,512]{1,0:T(8,128)(2,1)} %shard_map.115), channel_id=1, source_target_pairs={{0,4},{4,8},{8,12},{12,16},{16,20},{20,24},{24,28},{28,0},{1,5},{5... | collective-permute-start | bytes 1572872 | tf_op jit(solution)/shard_map/ppermute | solution.py:437
  18.1 42.9 %collective-permute-start.5 = (bf16[256,512]{1,0:T(8,128)(2,1)}, bf16[256,512]{1,0:T(8,128)(2,1)}, u32[]{:S(2)}, u32[]{:S(2)}) collective-permute-start(bf16[256,512]{1,0:T(8,128)(2,1)} %get-tuple-element.34), channel_id=1, source_target_pairs={{0,4},{4,8},{8,12},{12,16},{16,20},{20,24},{24,28},{28,0},{1,5},{5... | collective-permute-start | bytes 786440 | tf_op jit(solution)/shard_map/ppermute | solution.py:441
  19.7 11.9 %copy-start.2 = (bf16[256,512]{1,0:T(8,128)(2,1)S(1)}, bf16[256,512]{1,0:T(8,128)(2,1)}, u32[]{:S(2)}) copy-start(bf16[256,512]{1,0:T(8,128)(2,1)} %get-tuple-element.36) | copy-start | bytes 786436
  19.7 15.8 %copy-start = (f32[2,192,256]{2,1,0:T(8,128)S(1)}, f32[2,192,256]{2,1,0:T(8,128)}, u32[]{:S(2)}) copy-start(f32[2,192,256]{2,1,0:T(8,128)} %get-tuple-element.25.w_far) | copy-start | bytes 1179652
  26.3 9.2 %collective-permute-start.3 = (bf16[2,208,256]{2,1,0:T(8,128)(2,1)S(1)}, bf16[2,208,256]{2,1,0:T(8,128)(2,1)S(1)}, u32[]{:S(2)}, u32[]{:S(2)}) collective-permute-start(bf16[2,208,256]{2,1,0:T(8,128)(2,1)S(1)} %shard_map.113.mine_ref), channel_id=1, source_target_pairs={{0,24},{4,28},{8,16},{12,20},{16,8},{20,12},{24,0},{28,4},{1,25},{... | collective-permute-start | bytes 638984 | tf_op jit(solution)/shard_map/ppermute | solution.py:402
  31.5 30.1 %collective-permute-start.6 = (bf16[256,512]{1,0:T(8,128)(2,1)S(1)}, bf16[256,512]{1,0:T(8,128)(2,1)S(1)}, u32[]{:S(2)}, u32[]{:S(2)}) collective-permute-start(bf16[256,512]{1,0:T(8,128)(2,1)S(1)} %copy-done.2), channel_id=1, source_target_pairs={{0,4},{4,8},{8,12},{12,16},{16,20},{20,24},{24,28},{28,0},{1,5},{5... | collective-permute-start | bytes 786440 | tf_op jit(solution)/shard_map/ppermute | solution.py:448
  36.7 34.3 %copy-start.1 = (f32[2]{0:T(128)S(1)}, f32[2]{0:T(128)}, u32[]{:S(2)}) copy-start(f32[2]{0:T(128)} %s_ref.1) | copy-start | bytes 28
  36.7 30.5 %collective-permute-start.9 = (bf16[2,208,256]{2,1,0:T(8,128)(2,1)S(1)}, bf16[2,208,256]{2,1,0:T(8,128)(2,1)S(1)}, u32[]{:S(2)}, u32[]{:S(2)}) collective-permute-start(bf16[2,208,256]{2,1,0:T(8,128)(2,1)S(1)} %shard_map.114.own_ref), channel_id=1, source_target_pairs={{0,12},{4,8},{8,4},{12,0},{16,28},{20,24},{24,20},{28,16},{1,13},{... | collective-permute-start | bytes 638984 | tf_op jit(solution)/shard_map/ppermute | solution.py:402
  61.0 9.3 %collective-permute-start.8 = (bf16[2,208,256]{2,1,0:T(8,128)(2,1)S(1)}, bf16[2,208,256]{2,1,0:T(8,128)(2,1)S(1)}, u32[]{:S(2)}, u32[]{:S(2)}) collective-permute-start(bf16[2,208,256]{2,1,0:T(8,128)(2,1)S(1)} %shard_map.114.own_ref), channel_id=1, source_target_pairs={{0,8},{4,12},{8,0},{12,4},{16,24},{20,28},{24,16},{28,20},{1,9},{5... | collective-permute-start | bytes 638984 | tf_op jit(solution)/shard_map/ppermute | solution.py:402
  61.0 10.0 %collective-permute-start.7 = (bf16[2,208,256]{2,1,0:T(8,128)(2,1)S(1)}, bf16[2,208,256]{2,1,0:T(8,128)(2,1)S(1)}, u32[]{:S(2)}, u32[]{:S(2)}) collective-permute-start(bf16[2,208,256]{2,1,0:T(8,128)(2,1)S(1)} %shard_map.114.own_ref), channel_id=1, source_target_pairs={{0,4},{4,0},{8,12},{12,8},{16,20},{20,16},{24,28},{28,24},{1,5},{5... | collective-permute-start | bytes 638984 | tf_op jit(solution)/shard_map/ppermute | solution.py:402
  75.4 1.2 %collective-permute-start.10 = (f32[1,1024]{1,0:T(1,128)S(1)}, f32[1,1024]{1,0:T(1,128)S(1)}, u32[]{:S(2)}, u32[]{:S(2)}) collective-permute-start(f32[1,1024]{1,0:T(1,128)S(1)} %get-tuple-element.38), channel_id=1, source_target_pairs={{0,1},{1,0},{2,3},{3,2},{4,5},{5,4},{6,7},{7,6},{8,9},{9,8},{10,11... | collective-permute-start | bytes 12296 | tf_op jit(solution)/shard_map/ppermute | solution.py:402
  76.7 3.6 %collective-permute-start.11 = (f32[1,1024]{1,0:T(1,128)S(1)}, f32[1,1024]{1,0:T(1,128)S(1)}, u32[]{:S(2)}, u32[]{:S(2)}) collective-permute-start(f32[1,1024]{1,0:T(1,128)S(1)} %add.10), channel_id=1, source_target_pairs={{0,2},{1,3},{2,0},{3,1},{4,6},{5,7},{6,4},{7,5},{8,10},{9,11},{10,... | collective-permute-start | bytes 12296 | tf_op jit(solution)/shard_map/ppermute | solution.py:402

commit v2 on v1

--- a/solution.py
+++ b/solution.py
@@ -10,9 +10,9 @@
 
 WINDOW_SPAN = 512
 EPS = 1e-06
-PAD = 16
+PAD = 8
 KIND = 0
-ORDERS = ((3, 1, 2), (2, 1, 3))
+ORDERS = ((1, 2, 3), (2, 1, 3))
 WIRE = jnp.bfloat16
 REACH = 120.0
 BF = jnp.bfloat16
@@ -81,8 +81,8 @@
 
 
 def grads_body(quarter, q_far, k_far, v_far, r_far, w1_far, w3_far, w2_far, *refs):
-    own_ref, p1_ref, p2_ref, p3_ref, mine_far, q_ref, k_ref, v_ref, *tails = refs[:-7]
-    acc, part, r_ref, w1_ref, w3_ref, w2_ref, sems = refs[-7:]
+    own_far, *wires, mine_far, q_ref, k_ref, v_ref, low_far, high_far = refs[:-9]
+    acc, part, sent, wire, r_ref, w1_ref, w3_ref, w2_ref, sems = refs[-9:]
     heads, size = w1_ref.shape[0], w1_ref.shape[1]
     tokens = k_ref.shape[0]
     step = min(256, tokens)
@@ -101,36 +101,41 @@
     def fetch(index):
         return copy(block(k_far, index), block(k_ref, index)), copy(block(v_far, index), block(v_ref, index))
 
-    first = [copy(w1_far, w1_ref)]
+    def weights_of(head):
+        return [copy(a.at[head], b.at[head]) for a, b in ((w1_far, w1_ref), (w3_far, w3_ref), (w2_far, w2_ref))]
+
+    first = [weights_of(0)]
     coming = [fetch(0)]
-    first += [copy(w3_far, w3_ref), copy(w2_far, w2_ref), copy(r_far, r_ref)]
-    coming += [fetch(index) for index in range(1, count)]
-    late = [copy(q_far, q_ref)]
+    rates = copy(r_far, r_ref)
+    coming += [fetch(later) for later in range(1, count)]
+    late = []
     rows = 3 * size // 4
     q = quarter[0]
     own_rows = pl.ds(pl.multiple_of(q * rows, 8), rows)
-    halves = []
-    for made in first:
-        made.wait()
+    edge = tokens - WINDOW_SPAN
     for head in range(heads):
+        for made in first[head]:
+            made.wait()
         w1t, w3t, w2 = w1_ref[head].T, w3_ref[head].T, w2_ref[head]
-        halves.append((*split(w1t), *split(w3t), *split(w2)))
+        w1h, w1l = split(w1t)
+        w3h, w3l = split(w3t)
+        w2h, w2l = split(w2)
         acc[0:size] = w1t
         acc[size : 2 * size] = w3t
         acc[2 * size : 3 * size] = w2.T
         part[head] = acc[own_rows]
         late.append(copy(part.at[head], mine_far.at[head]))
-    sums = [None] * heads
-    edge = tokens - WINDOW_SPAN
-    for index in range(count):
-        for made in coming[index]:
-            made.wait()
-        start = index * step
-        if start >= edge:
-            late.append(copy(block(v_ref, index), tails[(start - edge) // step]))
-        for head in range(heads):
-            w1h, w1l, w3h, w3l, w2h, w2l = halves[head]
-            cols = slice(head * size, (head + 1) * size)
+        g1 = g3 = g2 = None
+        cols = slice(head * size, (head + 1) * size)
+        for index in range(count):
+            if head == 0:
+                for made in coming[index]:
+                    made.wait()
+                if index == 0:
+                    rates.wait()
+                    first += [weights_of(later) for later in range(1, heads)]
+                    late.append(copy(q_far, q_ref))
+            start = index * step
             kb = k_ref[start : start + step, cols]
             vb = v_ref[start : start + step, cols]
             rate = r_ref[head : head + 1, start : start + step]
@@ -145,16 +150,24 @@
             ah, al = split(act)
             d1h, d1l = split(d1)
             d3h, d3l = split(d3)
-            new = (nn(d1h, kb) + nn(d1l, kb), nn(d3h, kb) + nn(d3l, kb), nn(ah, vb) + nn(al, vb))
-            sums[head] = new if sums[head] is None else tuple(x + y for x, y in zip(sums[head], new))
-    for head in range(heads):
-        g1, g3, g2 = sums[head]
+            t1 = nn(d1h, kb) + nn(d1l, kb)
+            t3 = nn(d3h, kb) + nn(d3l, kb)
+            t2 = nn(ah, vb) + nn(al, vb)
+            g1 = t1 if g1 is None else g1 + t1
+            g3 = t3 if g3 is None else g3 + t3
+            g2 = t2 if g2 is None else g2 + t2
+        if head == 0:
+            middle = edge + WINDOW_SPAN // 2
+            late.append(copy(v_ref.at[middle:], low_far))
+            late.append(copy(v_ref.at[edge:middle], high_far))
         acc[0:size] = g1
         acc[size : 2 * size] = g3
         acc[2 * size : 3 * size] = g2.T
-        own_ref[head] = acc[own_rows]
-        for j, ref in ((1, p1_ref), (2, p2_ref), (3, p3_ref)):
-            encode(acc[pl.ds(pl.multiple_of((q ^ j) * rows, 8), rows)], ref.at[head])
+        for j, far_ref in enumerate(wires, 1):
+            encode(acc[pl.ds(pl.multiple_of((q ^ j) * rows, 8), rows)], wire.at[head, j - 1])
+            late.append(copy(wire.at[head, j - 1], far_ref.at[head]))
+        sent[head] = acc[own_rows]
+        late.append(copy(sent.at[head], own_far.at[head]))
     for made in late:
         made.wait()
 
@@ -172,43 +185,37 @@
     rows = 3 * size // 4
     whole = pltpu.VMEM(w1.shape, F32)
     step = min(256, keys.shape[0])
-    pieces = WINDOW_SPAN // step
+    copies = 1 + 3 * heads + 2 * (keys.shape[0] // step) + 1 + 5 * heads + 2
     scratch = (
         pltpu.VMEM((3 * size, size), F32),
         pltpu.VMEM((heads, rows, size), F32),
+        pltpu.VMEM((heads, rows, size), F32),
+        pltpu.VMEM((heads, 3, rows + PAD, size), WIRE),
         pltpu.VMEM(rates_t.shape, F32),
         whole,
         whole,
         whole,
-        pltpu.SemaphoreType.DMA((4 + 2 * (keys.shape[0] // step) + 1 + heads + pieces,)),
+        pltpu.SemaphoreType.DMA((copies,)),
     )
     wire = spec((heads, rows + PAD, size), WIRE)
     part = spec((heads, rows, size), F32)
     inputs = [spec(a.shape, a.dtype) for a in (queries, keys, values)]
-    tail = spec((step, keys.shape[1]), keys.dtype)
-    outs = (part, wire, wire, wire, part, *inputs, *[tail] * pieces)
-    away = (False, False, False, False, True, False, False, False, *[True] * pieces)
+    half = (WINDOW_SPAN // 2, keys.shape[1])
+    outs = (part, wire, wire, wire, part, *inputs, spec(half, keys.dtype), spec(half, keys.dtype))
+    away = (True, True, True, True, True, False, False, False, True, True)
     args = (quarter, *far(queries, keys, values, rates_t, w1, w3, w2))
-    out = call(grads_body, outs, args, [SM] + [FAR] * 7, away, scratch, 1 << 31)
-    return out[:8], out[8:]
-
-
-def tail_body(k_far, out_ref, sems):
-    edge = k_far.shape[0] - WINDOW_SPAN
-    half = WINDOW_SPAN // 2
-    copies = [
-        pltpu.make_async_copy(k_far.at[edge + at : edge + at + half], out_ref.at[at : at + half], sems.at[at // half])
-        for at in (0, half)
-    ]
-    for made in copies:
-        made.start()
-    for made in copies:
-        made.wait()
+    return call(grads_body, outs, args, [SM] + [FAR] * 7, away, scratch, 1 << 31)
+
+
+def tail_body(k_far, out_ref, sem):
+    made = pltpu.make_async_copy(k_far.at[k_far.shape[0] - out_ref.shape[0] :], out_ref, sem)
+    made.start()
+    made.wait()
 
 
 def tail(keys):
     out = spec((WINDOW_SPAN, keys.shape[1]), keys.dtype)
-    return call(tail_body, out, far(keys), [FAR], False, (pltpu.SemaphoreType.DMA((2,)),))
+    return call(tail_body, out, far(keys), [FAR], False, (pltpu.SemaphoreType.DMA,))
 
 
 class Rows:
@@ -332,7 +339,7 @@
             source = block - back
             if source < 0:
                 at = (source + span) * step
-                kb, vb = halo[0][at : at + step, q.cols], halo[1 + at // step][:, q.cols]
+                kb, vb = halo[0][at : at + step, q.cols], halo[span - at // step][:, q.cols]
             else:
                 kb, vb = k(source), v(source)
             s = nt(qb, kb) * scale
@@ -374,17 +381,18 @@
     )
 
 
-def mix_body(features, r_ref, z_ref, a_ref, b_ref, out, buf, sems):
+def mix_body(features, r_ref, z_ref, *refs):
+    *parts, out, buf, sems = refs
     tokens = buf.shape[0]
     step = 128
-    half = tokens // 2
+    attended = [(ref, at) for ref in parts for at in range(0, ref.shape[0], step)]
     inverse = 1.0 / jnp.sqrt(r_ref[...] / features + EPS)
     copies = []
     for index in range(tokens // step):
         start = index * step
         column = jnp.broadcast_to(inverse[:, start : start + step], (128, step)).T[:, 0:1]
-        attn = a_ref[start : start + step] if start < half else b_ref[start - half : start - half + step]
-        buf[start : start + step] = attn + z_ref[start : start + step] * column
+        ref, at = attended[index]
+        buf[start : start + step] = ref[at : at + step] + z_ref[start : start + step] * column
         made = pltpu.make_async_copy(buf.at[start : start + step], out.at[start : start + step], sems.at[index])
         made.start()
         copies.append(made)
@@ -392,9 +400,9 @@
         made.wait()
 
 
-def mix(total, z, low, high, features):
+def mix(total, z, *parts, features):
     scratch = (pltpu.VMEM(z.shape, F32), pltpu.SemaphoreType.DMA((z.shape[0] // 128,)))
-    args = (total, z, low, high)
+    args = (total, z, *parts)
     return call(functools.partial(mix_body, features), spec(z.shape, F32), args, away=True, scratch=scratch)
 
 
@@ -424,40 +432,41 @@
     blocks = tuple(range(tokens // 256))
     half = len(blocks) // 2
     wire = spec((heads, rows + PAD, size), WIRE)
-    ring = [(i, (i + 1) % devices) for i in range(devices)]
+    line = [(i, i + 1) for i in range(devices - 1)]
+    ring = [*line, (devices - 1, 0)]
     quarter, masks, order, shared = plan(place, devices, KIND)
     quarter = quarter.reshape(1)
 
     def spread(parts):
         out = {}
         for j in order:
-            out[j] = near(swap(parts[j - 1], "seq", masks[j - 1]))[0]
+            out[j] = swap(parts[j - 1], "seq", masks[j - 1])
         return out[1], out[2], out[3]
 
     halo = [lax.ppermute(tail(keys), "seq", ring)]
-    out, ends = grads(quarter, queries, keys, values, rates.T, w_one, w_three, w_two)
-    own, p1, p2, p3, mine_w, q, k, v = out
+    out = grads(quarter, queries, keys, values, rates.T, w_one, w_three, w_two)
+    own, p1, p2, p3, mine_w, q, k, v, end, rest = out
     got = spread((p1, p2, p3))
-    halo.append(lax.ppermute(ends[0], "seq", ring))
     high = attend(first, q, k, v, None, blocks[half:], size)
     mine = call(gather_body, wire, (after(own, high), *got))
     for mask in shared[:-1]:
         mine = call(cross_body, wire, (mine, swap(mine, "seq", mask)))
     other = near(swap(mine, "seq", shared[-1]))[0]
-    for place, end in enumerate(ends[1:], 1):
-        halo.append(lax.ppermute(after(end, mine), "seq", ring))
+    halo.append(lax.ppermute(after(end, mine), "seq", line))
     scratch = (pltpu.VMEM((heads, rows, size), F32), pltpu.SemaphoreType.DMA)
     new = call(renorm_body, wire, (mine_w, mine, other), [FAR, VM, VM], scratch=scratch)
     pieces = (new, *spread((new, new, new)))
-    low = attend(first, q, after(k, new), v, halo, blocks[:half], size)
-    pieces = (after(new, low), *pieces[1:])
+    halo.append(lax.ppermute(after(rest, *pieces), "seq", ring))
+    low1 = attend(first, q, after(k, new), v, halo[:2], blocks[1:half], size)
+    pieces = (after(new, low1), *pieces[1:])
     zed, total, new_t = apply(quarter, q, head_scale, pieces)
+    low0 = attend(first, q, after(k, new_t), v, halo, blocks[:1], size)
     mask = 1
     while mask < lax.axis_size("head"):
         total = total + swap(total, "head", mask)
         mask *= 2
     new_one, new_three, new_two = weights(new_t)
-    mixed = mix(total, zed, low, high, heads * lax.axis_size("head") * size)
+    mixed = mix(total, zed, low0, low1, high, features=heads * lax.axis_size("head") * size)
     return (mixed, new_one, new_three, new_two)
 
 

time: 82.3 us -> 74.9 us (0.910)
  starting transfers between devices: 40.1 us -> 29.8 us
  waiting for transfers between devices: 14.9 us -> 16.5 us
  Pallas kernels: 26.2 us -> 27.3 us
    ppermute x9, starting transfers between devices: 36.4 us -> 24.9 us  [swap(): lax.ppermute(x, axis, [(i, i ^ mask) for i in range(lax.axis_size(axis))])]
    ppermute x9, waiting for transfers between devices: 14.9 us -> 16.5 us  [swap(): lax.ppermute(x, axis, [(i, i ^ mask) for i in range(lax.axis_size(axis))])]
    ppermute x2, starting transfers between devices: 1.72 us -> 2.94 us  [the longest x1 2.09 us: per_device(): halo.append(lax.ppermute(after(end, mine), 'seq', line))]
    pallas_call x9 -> x10, Pallas kernels: 26.2 us -> 27.3 us  [call(): pl.pallas_call(body, out_shape=tuple(made) if many else made[0], in_specs...]
  transfers between devices with their start and end apart: 12 -> 12, of which waited for: 7 -> 8; matrix products, arithmetic and copies ran while one was open for 0% -> 0% of each run, Pallas kernels for 14% -> 20%
where the time goes in v2:
time: 74.9 us; the launch traced here: 74.5 us
  starting transfers between devices  29.8 us (40%)
  Pallas kernels  27.3 us (36%)
  waiting for transfers between devices  16.5 us (22%)
  between operations  0.92 us (1%)
    pallas_call x10, Pallas kernels, call(): pl.pallas_call(body, out_shape=tuple(made) if many else made[0], in_specs...  27.3 us
    ppermute x9, starting transfers between devices, swap(): lax.ppermute(x, axis, [(i, i ^ mask) for i in range(lax.axis_size(axis))])  24.9 us
    ppermute x9, waiting for transfers between devices, swap(): lax.ppermute(x, axis, [(i, i ^ mask) for i in range(lax.axis_size(axis))])  16.5 us
    ppermute x1, starting transfers between devices, per_device(): halo.append(lax.ppermute(after(end, mine), 'seq', line))  2.09 us
    ppermute x1, starting transfers between devices, per_device(): halo = [lax.ppermute(tail(keys), 'seq', ring)]  1.98 us
  transfers between devices with their start and end apart: 12, of which 8 were waited for; matrix products, arithmetic and copies ran while one was open for 0% of the time, Pallas kernels for 20%

profile of v2, /device:TPU:0, one launch (start us, length us, event | category | flops | bytes accessed | tf_op | source)
XLA Modules:
  0.0 74.5 jit_solution(4449454755988867842)
XLA Ops:
  0.6 8.7 %shard_map.111 = (f32[2,192,256]{2,1,0:T(8,128)}, bf16[2,200,256]{2,1,0:T(8,128)(2,1)}, bf16[2,200,256]{2,1,0:T(8,128)(2,1)}, bf16[2,200,256]{2,1,0:T(8,128)(2,1...) custom-call(s32[1]{0:T(128)} %bitcast.quarter, ...), custom_call_target="tpu_custom_call" | custom-call | flops 2147483648 | bytes 2097152 | tf_op jit(solution)/shard_map/pallas_call | solution.py:37
  9.4 3.0 %collective-permute-start = (bf16[2,200,256]{2,1,0:T(8,128)(2,1)}, bf16[2,200,256]{2,1,0:T(8,128)(2,1)S(1)}, u32[]{:S(2)}, u32[]{:S(2)}) collective-permute-start(bf16[2,200,256]{2,1,0:T(8,128)(2,1)} %get-tuple-element.32), channel_id=1, source_target_pairs={{0,4},{4,0},{8,12},{12,8},{16,20},{20,16},{24,28},{28,24},{1,5},{5... | collective-permute-start | bytes 614408 | tf_op jit(solution)/shard_map/ppermute | solution.py:410
  12.4 1.6 %collective-permute-start.1 = (bf16[2,200,256]{2,1,0:T(8,128)(2,1)}, bf16[2,200,256]{2,1,0:T(8,128)(2,1)S(1)}, u32[]{:S(2)}, u32[]{:S(2)}) collective-permute-start(bf16[2,200,256]{2,1,0:T(8,128)(2,1)} %get-tuple-element.33), channel_id=1, source_target_pairs={{0,8},{4,12},{8,0},{12,4},{16,24},{20,28},{24,16},{28,20},{1,9},{5... | collective-permute-start | bytes 614408 | tf_op jit(solution)/shard_map/ppermute | solution.py:410
  14.0 0.0 collective-permute-start.2
  14.0 1.8 %shard_map.115 = bf16[512,512]{1,0:T(8,128)(2,1)} custom-call(bf16[1024,512]{1,0:T(8,128)(2,1)} %k_far.3), custom_call_target="tpu_custom_call" | custom-call | flops 16777216 | bytes 2097152 | tf_op jit(solution)/shard_map/pallas_call | solution.py:37
  15.8 2.0 %collective-permute-start.4 = (bf16[512,512]{1,0:T(8,128)(2,1)}, bf16[512,512]{1,0:T(8,128)(2,1)}, u32[]{:S(2)}, u32[]{:S(2)}) collective-permute-start(bf16[512,512]{1,0:T(8,128)(2,1)} %shard_map.115), channel_id=1, source_target_pairs={{0,4},{4,8},{8,12},{12,16},{16,20},{20,24},{24,28},{28,0},{1,5},{5... | collective-permute-start | bytes 1572872 | tf_op jit(solution)/shard_map/ppermute | solution.py:446
  17.8 0.0 copy-start.1
  17.8 0.0 copy-start.4
  17.8 0.0 copy-start
  17.8 1.7 %shard_map.112.refs_2_ = f32[512,512]{1,0:T(8,128)S(1)} custom-call(s32[1]{0:T(128)} %bitcast.2.refs_0_, bf16[1024,512]{1,0:T(8,128)(2,1)S(1)} %get-tuple-element.26.refs_1_.q_ref, bf16[1024,512]{1,0:T(8,128)(2,1)S(1)} %get-tuple-element.42.refs_2_, bf16[1024,512]{1,0:T(8,128)(2,1)S(1)} %get-tuple-element.30.refs_3_), custom_call_target="tpu_custom_call" | custom-call | flops 1073741824 | bytes 2097152 | tf_op jit(solution)/shard_map/pallas_call | solution.py:37
  19.6 0.0 copy-start.3
  19.6 0.0 collective-permute-done.r1_ref
  19.6 1.0 %collective-permute-done.1.r2_ref = bf16[2,200,256]{2,1,0:T(8,128)(2,1)S(1)} collective-permute-done((bf16[2,200,256]{2,1,0:T(8,128)(2,1)}, bf16[2,200,256]{2,1,0:T(8,128)(2,1)S(1)}, u32[]{:S(2)}, u32[]{:S(2)}) %collective-permute-start.1) | collective-permute-done | bytes 204832 | tf_op jit(solution)/shard_map/ppermute | solution.py:410
  20.6 2.9 %collective-permute-done.2.r3_ref = bf16[2,200,256]{2,1,0:T(8,128)(2,1)} collective-permute-done((bf16[2,200,256]{2,1,0:T(8,128)(2,1)}, bf16[2,200,256]{2,1,0:T(8,128)(2,1)}, u32[]{:S(2)}, u32[]{:S(2)}) %collective-permute-start.2) | collective-permute-done | bytes 204832 | tf_op jit(solution)/shard_map/ppermute | solution.py:410
  23.5 0.0 copy-done.1
  23.5 2.0 %shard_map.113.mine_ref = bf16[2,200,256]{2,1,0:T(8,128)(2,1)S(1)} custom-call(f32[2,192,256]{2,1,0:T(8,128)S(1)} %copy-done.1, bf16[2,200,256]{2,1,0:T(8,128)(2,1)S(1)} %collective-permute-done.r1_ref, bf16[2,200,256]{2,1,0:T(8,128)(2,1)S(1)} %collective-permute-done.1.r2_ref, bf16[2,200,256]{2,1,0:T(8,128)(2,1)} %collective-permute-done.2.r3_ref), custom_call_target="tpu_custom_call" | custom-call | flops 16777216 | bytes 2097152 | tf_op jit(solution)/shard_map/pallas_call | solution.py:37
  25.5 5.2 %collective-permute-start.3 = (bf16[2,200,256]{2,1,0:T(8,128)(2,1)S(1)}, bf16[2,200,256]{2,1,0:T(8,128)(2,1)S(1)}, u32[]{:S(2)}, u32[]{:S(2)}) collective-permute-start(bf16[2,200,256]{2,1,0:T(8,128)(2,1)S(1)} %shard_map.113.mine_ref), channel_id=1, source_target_pairs={{0,24},{4,28},{8,16},{12,20},{16,8},{20,12},{24,0},{28,4},{1,25},{... | collective-permute-start | bytes 614408 | tf_op jit(solution)/shard_map/ppermute | solution.py:410
  30.7 0.0 copy-done.4
  30.7 2.1 %collective-permute-start.5 = (bf16[256,512]{1,0:T(8,128)(2,1)S(1)}, bf16[256,512]{1,0:T(8,128)(2,1)S(1)}, u32[]{:S(2)}, u32[]{:S(2)}) collective-permute-start(bf16[256,512]{1,0:T(8,128)(2,1)S(1)} %copy-done.4), channel_id=1, source_target_pairs={{0,4},{4,8},{8,12},{12,16},{16,20},{20,24},{24,28},{1,5},{5,9},{9,... | collective-permute-start | bytes 786440 | tf_op jit(solution)/shard_map/ppermute | solution.py:455
  32.8 1.7 %collective-permute-done.3.other_ref = bf16[2,200,256]{2,1,0:T(8,128)(2,1)S(1)} collective-permute-done((bf16[2,200,256]{2,1,0:T(8,128)(2,1)S(1)}, bf16[2,200,256]{2,1,0:T(8,128)(2,1)S(1)}, u32[]{:S(2)}, u32[]{:S(2)}) %collective-permute-start.3) | collective-permute-done | bytes 204832 | tf_op jit(solution)/shard_map/ppermute | solution.py:410
  34.6 0.0 copy-done
  34.6 1.2 %shard_map.114.own_ref = bf16[2,200,256]{2,1,0:T(8,128)(2,1)S(1)} custom-call(f32[2,192,256]{2,1,0:T(8,128)S(1)} %copy-done, bf16[2,200,256]{2,1,0:T(8,128)(2,1)S(1)} %shard_map.113.mine_ref, bf16[2,200,256]{2,1,0:T(8,128)(2,1)S(1)} %collective-permute-done.3.other_ref), custom_call_target="tpu_custom_call" | custom-call | flops 16777216 | bytes 2097152 | tf_op jit(solution)/shard_map/pallas_call | solution.py:37
  35.8 12.8 %collective-permute-start.8 = (bf16[2,200,256]{2,1,0:T(8,128)(2,1)S(1)}, bf16[2,200,256]{2,1,0:T(8,128)(2,1)S(1)}, u32[]{:S(2)}, u32[]{:S(2)}) collective-permute-start(bf16[2,200,256]{2,1,0:T(8,128)(2,1)S(1)} %shard_map.114.own_ref), channel_id=1, source_target_pairs={{0,12},{4,8},{8,4},{12,0},{16,28},{20,24},{24,20},{28,16},{1,13},{... | collective-permute-start | bytes 614408 | tf_op jit(solution)/shard_map/ppermute | solution.py:410
  48.6 0.0 collective-permute-start.7
  48.6 0.6 collective-permute-start.6
  49.2 5.3 %collective-permute-done.8.r3_ref = bf16[2,200,256]{2,1,0:T(8,128)(2,1)S(1)} collective-permute-done((bf16[2,200,256]{2,1,0:T(8,128)(2,1)S(1)}, bf16[2,200,256]{2,1,0:T(8,128)(2,1)S(1)}, u32[]{:S(2)}, u32[]{:S(2)}) %collective-permute-start.8) | collective-permute-done | bytes 204832 | tf_op jit(solution)/shard_map/ppermute | solution.py:410
  54.6 3.0 %collective-permute-done.7.r2_ref = bf16[2,200,256]{2,1,0:T(8,128)(2,1)S(1)} collective-permute-done((bf16[2,200,256]{2,1,0:T(8,128)(2,1)S(1)}, bf16[2,200,256]{2,1,0:T(8,128)(2,1)S(1)}, u32[]{:S(2)}, u32[]{:S(2)}) %collective-permute-start.7) | collective-permute-done | bytes 204832 | tf_op jit(solution)/shard_map/ppermute | solution.py:410
  57.5 0.7 collective-permute-done.6.r1_ref
  58.2 0.0 copy-done.3
  58.2 0.0 copy-start.2
  58.2 0.8 %collective-permute-start.11 = (bf16[256,512]{1,0:T(8,128)(2,1)S(1)}, bf16[256,512]{1,0:T(8,128)(2,1)S(1)}, u32[]{:S(2)}, u32[]{:S(2)}) collective-permute-start(bf16[256,512]{1,0:T(8,128)(2,1)S(1)} %copy-done.3), channel_id=1, source_target_pairs={{0,4},{4,8},{8,12},{12,16},{16,20},{20,24},{24,28},{28,0},{1,5},{5... | collective-permute-start | bytes 786440 | tf_op jit(solution)/shard_map/ppermute | solution.py:459
  59.1 0.0 collective-permute-done.5.refs_5_
  59.1 0.0 collective-permute-done.4.refs_4_
  59.1 2.2 %shard_map.116.refs_1_ = f32[256,512]{1,0:T(8,128)S(1)} custom-call(s32[1]{0:T(128)} %bitcast.2.refs_0_, bf16[1024,512]{1,0:T(8,128)(2,1)S(1)} %get-tuple-element.26.refs_1_.q_ref, bf16[1024,512]{1,0:T(8,128)(2,1)S(1)} %get-tuple-element.42.refs_2_, bf16[1024,512]{1,0:T(8,128)(2,1)S(1)} %get-tuple-element.30.refs_3_, ...), custom_call_target="tpu_custom_call" | custom-call | flops 1073741824 | bytes 2097152 | tf_op jit(solution)/shard_map/pallas_call | solution.py:37
  61.3 0.0 copy-done.2
  61.3 4.4 %shard_map.117 = (f32[1024,512]{1,0:T(8,128)S(1)}, f32[1,1024]{1,0:T(1,128)S(1)}, f32[2,768,256]{2,1,0:T(8,128)S(1)}) custom-call(s32[1]{0:T(128)} %bitcast.quarter, f32[2]{0:T(128)S(1)} %copy-done.2, bf16[1024,512]{1,0:T(8,128)(2,1)S(1)} %get-tuple-element.26.refs_1_.q_ref, bf16[2,200,256]{2,1,0:T(8,128)(2,1)S(1)} %shard_map.114.own_ref, ...), custom_call_target="tpu_custom_call" | custom-call | flops 2147483648 | bytes 2097152 | tf_op jit(solution)/shard_map/pallas_call | solution.py:37
  65.7 0.1 collective-permute-start.9
  65.8 1.2 %collective-permute-done.9 = f32[1,1024]{1,0:T(1,128)S(1)} collective-permute-done((f32[1,1024]{1,0:T(1,128)S(1)}, f32[1,1024]{1,0:T(1,128)S(1)}, u32[]{:S(2)}, u32[]{:S(2)}) %collective-permute-start.9) | collective-permute-done | bytes 4128 | tf_op jit(solution)/shard_map/ppermute | solution.py:410
  67.0 1.6 %collective-permute-start.10 = (f32[1,1024]{1,0:T(1,128)S(1)}, f32[1,1024]{1,0:T(1,128)S(1)}, u32[]{:S(2)}, u32[]{:S(2)}) collective-permute-start(f32[1,1024]{1,0:T(1,128)S(1)} %add.10), channel_id=1, source_target_pairs={{0,2},{1,3},{2,0},{3,1},{4,6},{5,7},{6,4},{7,5},{8,10},{9,11},{10,... | collective-permute-start | bytes 12296 | tf_op jit(solution)/shard_map/ppermute | solution.py:410
  68.5 1.3 %shard_map.120 = (f32[2,256,256]{2,1,0:T(8,128)}, f32[2,256,256]{2,1,0:T(8,128)}, f32[2,256,256]{2,1,0:T(8,128)}) custom-call(f32[2,768,256]{2,1,0:T(8,128)S(1)} %get-tuple-element.41.n_ref), custom_call_target="tpu_custom_call" | custom-call | flops 16777216 | bytes 2097152 | tf_op jit(solution)/shard_map/pallas_call | solution.py:37
  69.8 0.7 collective-permute-done.10
  70.6 0.0 collective-permute-done.11.refs_6_
  70.6 2.2 %shard_map.118.refs_0_ = f32[256,512]{1,0:T(8,128)S(1)} custom-call(s32[1]{0:T(128)} %bitcast.2.refs_0_, bf16[1024,512]{1,0:T(8,128)(2,1)S(1)} %get-tuple-element.26.refs_1_.q_ref, bf16[1024,512]{1,0:T(8,128)(2,1)S(1)} %get-tuple-element.42.refs_2_, bf16[1024,512]{1,0:T(8,128)(2,1)S(1)} %get-tuple-element.30.refs_3_, ...), custom_call_target="tpu_custom_call" | custom-call | flops 1073741824 | bytes 2097152 | tf_op jit(solution)/shard_map/pallas_call | solution.py:37
  72.7 1.6 %shard_map.119 = f32[1024,512]{1,0:T(8,128)} custom-call(f32[1,1024]{1,0:T(1,128)S(1)} %add.11.r_ref, f32[1024,512]{1,0:T(8,128)S(1)} %get-tuple-element.40.z_ref, f32[256,512]{1,0:T(8,128)S(1)} %shard_map.118.refs_0_, f32[256,512]{1,0:T(8,128)S(1)} %shard_map.116.refs_1_, f32[512,512]{1,0:T(8,128)S(1)} %shard_map.112.refs_2_), custom_call_target="tpu_custom_call" | custom-call | flops 16777216 | bytes 2097152 | tf_op jit(solution)/shard_map/pallas_call | solution.py:37
  (2 shorter events, 0.0 us)
Async XLA Ops:
  9.4 10.2 %collective-permute-start = (bf16[2,200,256]{2,1,0:T(8,128)(2,1)}, bf16[2,200,256]{2,1,0:T(8,128)(2,1)S(1)}, u32[]{:S(2)}, u32[]{:S(2)}) collective-permute-start(bf16[2,200,256]{2,1,0:T(8,128)(2,1)} %get-tuple-element.32), channel_id=1, source_target_pairs={{0,4},{4,0},{8,12},{12,8},{16,20},{20,16},{24,28},{28,24},{1,5},{5... | collective-permute-start | bytes 614408 | tf_op jit(solution)/shard_map/ppermute | solution.py:410
  12.4 8.2 %collective-permute-start.1 = (bf16[2,200,256]{2,1,0:T(8,128)(2,1)}, bf16[2,200,256]{2,1,0:T(8,128)(2,1)S(1)}, u32[]{:S(2)}, u32[]{:S(2)}) collective-permute-start(bf16[2,200,256]{2,1,0:T(8,128)(2,1)} %get-tuple-element.33), channel_id=1, source_target_pairs={{0,8},{4,12},{8,0},{12,4},{16,24},{20,28},{24,16},{28,20},{1,9},{5... | collective-permute-start | bytes 614408 | tf_op jit(solution)/shard_map/ppermute | solution.py:410
  14.0 9.5 %collective-permute-start.2 = (bf16[2,200,256]{2,1,0:T(8,128)(2,1)}, bf16[2,200,256]{2,1,0:T(8,128)(2,1)}, u32[]{:S(2)}, u32[]{:S(2)}) collective-permute-start(bf16[2,200,256]{2,1,0:T(8,128)(2,1)} %get-tuple-element.34), channel_id=1, source_target_pairs={{0,12},{4,8},{8,4},{12,0},{16,28},{20,24},{24,20},{28,16},{1,13},{... | collective-permute-start | bytes 614408 | tf_op jit(solution)/shard_map/ppermute | solution.py:410
  15.8 43.2 %collective-permute-start.4 = (bf16[512,512]{1,0:T(8,128)(2,1)}, bf16[512,512]{1,0:T(8,128)(2,1)}, u32[]{:S(2)}, u32[]{:S(2)}) collective-permute-start(bf16[512,512]{1,0:T(8,128)(2,1)} %shard_map.115), channel_id=1, source_target_pairs={{0,4},{4,8},{8,12},{12,16},{16,20},{20,24},{24,28},{28,0},{1,5},{5... | collective-permute-start | bytes 1572872 | tf_op jit(solution)/shard_map/ppermute | solution.py:446
  17.8 5.7 %copy-start.1 = (f32[2,192,256]{2,1,0:T(8,128)S(1)}, f32[2,192,256]{2,1,0:T(8,128)}, u32[]{:S(2)}) copy-start(f32[2,192,256]{2,1,0:T(8,128)} %get-tuple-element.31.own_ref) | copy-start | bytes 1179652
  17.8 12.9 %copy-start.4 = (bf16[256,512]{1,0:T(8,128)(2,1)S(1)}, bf16[256,512]{1,0:T(8,128)(2,1)}, u32[]{:S(2)}) copy-start(bf16[256,512]{1,0:T(8,128)(2,1)} %get-tuple-element.37) | copy-start | bytes 786436
  17.8 16.7 %copy-start = (f32[2,192,256]{2,1,0:T(8,128)S(1)}, f32[2,192,256]{2,1,0:T(8,128)}, u32[]{:S(2)}) copy-start(f32[2,192,256]{2,1,0:T(8,128)} %get-tuple-element.27.w_far) | copy-start | bytes 1179652
  19.6 38.7 %copy-start.3 = (bf16[256,512]{1,0:T(8,128)(2,1)S(1)}, bf16[256,512]{1,0:T(8,128)(2,1)}, u32[]{:S(2)}) copy-start(bf16[256,512]{1,0:T(8,128)(2,1)} %get-tuple-element.44) | copy-start | bytes 786436
  25.5 9.1 %collective-permute-start.3 = (bf16[2,200,256]{2,1,0:T(8,128)(2,1)S(1)}, bf16[2,200,256]{2,1,0:T(8,128)(2,1)S(1)}, u32[]{:S(2)}, u32[]{:S(2)}) collective-permute-start(bf16[2,200,256]{2,1,0:T(8,128)(2,1)S(1)} %shard_map.113.mine_ref), channel_id=1, source_target_pairs={{0,24},{4,28},{8,16},{12,20},{16,8},{20,12},{24,0},{28,4},{1,25},{... | collective-permute-start | bytes 614408 | tf_op jit(solution)/shard_map/ppermute | solution.py:410
  30.7 28.4 %collective-permute-start.5 = (bf16[256,512]{1,0:T(8,128)(2,1)S(1)}, bf16[256,512]{1,0:T(8,128)(2,1)S(1)}, u32[]{:S(2)}, u32[]{:S(2)}) collective-permute-start(bf16[256,512]{1,0:T(8,128)(2,1)S(1)} %copy-done.4), channel_id=1, source_target_pairs={{0,4},{4,8},{8,12},{12,16},{16,20},{20,24},{24,28},{1,5},{5,9},{9,... | collective-permute-start | bytes 786440 | tf_op jit(solution)/shard_map/ppermute | solution.py:455
  35.8 18.8 %collective-permute-start.8 = (bf16[2,200,256]{2,1,0:T(8,128)(2,1)S(1)}, bf16[2,200,256]{2,1,0:T(8,128)(2,1)S(1)}, u32[]{:S(2)}, u32[]{:S(2)}) collective-permute-start(bf16[2,200,256]{2,1,0:T(8,128)(2,1)S(1)} %shard_map.114.own_ref), channel_id=1, source_target_pairs={{0,12},{4,8},{8,4},{12,0},{16,28},{20,24},{24,20},{28,16},{1,13},{... | collective-permute-start | bytes 614408 | tf_op jit(solution)/shard_map/ppermute | solution.py:410
  48.6 8.9 %collective-permute-start.7 = (bf16[2,200,256]{2,1,0:T(8,128)(2,1)S(1)}, bf16[2,200,256]{2,1,0:T(8,128)(2,1)S(1)}, u32[]{:S(2)}, u32[]{:S(2)}) collective-permute-start(bf16[2,200,256]{2,1,0:T(8,128)(2,1)S(1)} %shard_map.114.own_ref), channel_id=1, source_target_pairs={{0,8},{4,12},{8,0},{12,4},{16,24},{20,28},{24,16},{28,20},{1,9},{5... | collective-permute-start | bytes 614408 | tf_op jit(solution)/shard_map/ppermute | solution.py:410
  48.6 9.6 %collective-permute-start.6 = (bf16[2,200,256]{2,1,0:T(8,128)(2,1)S(1)}, bf16[2,200,256]{2,1,0:T(8,128)(2,1)S(1)}, u32[]{:S(2)}, u32[]{:S(2)}) collective-permute-start(bf16[2,200,256]{2,1,0:T(8,128)(2,1)S(1)} %shard_map.114.own_ref), channel_id=1, source_target_pairs={{0,4},{4,0},{8,12},{12,8},{16,20},{20,16},{24,28},{28,24},{1,5},{5... | collective-permute-start | bytes 614408 | tf_op jit(solution)/shard_map/ppermute | solution.py:410
  58.2 3.0 %copy-start.2 = (f32[2]{0:T(128)S(1)}, f32[2]{0:T(128)}, u32[]{:S(2)}) copy-start(f32[2]{0:T(128)} %s_ref.1) | copy-start | bytes 28
  58.2 12.3 %collective-permute-start.11 = (bf16[256,512]{1,0:T(8,128)(2,1)S(1)}, bf16[256,512]{1,0:T(8,128)(2,1)S(1)}, u32[]{:S(2)}, u32[]{:S(2)}) collective-permute-start(bf16[256,512]{1,0:T(8,128)(2,1)S(1)} %copy-done.3), channel_id=1, source_target_pairs={{0,4},{4,8},{8,12},{12,16},{16,20},{20,24},{24,28},{28,0},{1,5},{5... | collective-permute-start | bytes 786440 | tf_op jit(solution)/shard_map/ppermute | solution.py:459
  65.7 1.2 %collective-permute-start.9 = (f32[1,1024]{1,0:T(1,128)S(1)}, f32[1,1024]{1,0:T(1,128)S(1)}, u32[]{:S(2)}, u32[]{:S(2)}) collective-permute-start(f32[1,1024]{1,0:T(1,128)S(1)} %get-tuple-element.39), channel_id=1, source_target_pairs={{0,1},{1,0},{2,3},{3,2},{4,5},{5,4},{6,7},{7,6},{8,9},{9,8},{10,11... | collective-permute-start | bytes 12296 | tf_op jit(solution)/shard_map/ppermute | solution.py:410
  67.0 3.6 %collective-permute-start.10 = (f32[1,1024]{1,0:T(1,128)S(1)}, f32[1,1024]{1,0:T(1,128)S(1)}, u32[]{:S(2)}, u32[]{:S(2)}) collective-permute-start(f32[1,1024]{1,0:T(1,128)S(1)} %add.10), channel_id=1, source_target_pairs={{0,2},{1,3},{2,0},{3,1},{4,6},{5,7},{6,4},{7,5},{8,10},{9,11},{10,... | collective-permute-start | bytes 12296 | tf_op jit(solution)/shard_map/ppermute | solution.py:410

commit v3 on v2

--- a/solution.py
+++ b/solution.py
@@ -11,6 +11,7 @@
 WINDOW_SPAN = 512
 EPS = 1e-06
 PAD = 8
+CUT = 128
 KIND = 0
 ORDERS = ((1, 2, 3), (2, 1, 3))
 WIRE = jnp.bfloat16
@@ -81,7 +82,7 @@
 
 
 def grads_body(quarter, q_far, k_far, v_far, r_far, w1_far, w3_far, w2_far, *refs):
-    own_far, *wires, mine_far, q_ref, k_ref, v_ref, low_far, high_far = refs[:-9]
+    own_far, *wires, mine_far, q_ref, k_ref, v_ref, low_far, high_far, mid_far = refs[:-9]
     acc, part, sent, wire, r_ref, w1_ref, w3_ref, w2_ref, sems = refs[-9:]
     heads, size = w1_ref.shape[0], w1_ref.shape[1]
     tokens = k_ref.shape[0]
@@ -114,11 +115,14 @@
     own_rows = pl.ds(pl.multiple_of(q * rows, 8), rows)
     edge = tokens - WINDOW_SPAN
     for head in range(heads):
-        for made in first[head]:
-            made.wait()
-        w1t, w3t, w2 = w1_ref[head].T, w3_ref[head].T, w2_ref[head]
+        first[head][0].wait()
+        w1t = w1_ref[head].T
         w1h, w1l = split(w1t)
+        first[head][1].wait()
+        w3t = w3_ref[head].T
         w3h, w3l = split(w3t)
+        first[head][2].wait()
+        w2 = w2_ref[head]
         w2h, w2l = split(w2)
         acc[0:size] = w1t
         acc[size : 2 * size] = w3t
@@ -139,9 +143,10 @@
             kb = k_ref[start : start + step, cols]
             vb = v_ref[start : start + step, cols]
             rate = r_ref[head : head + 1, start : start + step]
-            h1 = nt(w1h, kb) + nt(w1l, kb)
-            h3 = nt(w3h, kb) + nt(w3l, kb)
-            da = (nt(w2h, vb) + nt(w2l, vb)) * rate
+            kk = jnp.concatenate([kb, kb], axis=1)
+            h1 = nt(jnp.concatenate([w1h, w1l], axis=1), kk)
+            h3 = nt(jnp.concatenate([w3h, w3l], axis=1), kk)
+            da = nt(jnp.concatenate([w2h, w2l], axis=1), jnp.concatenate([vb, vb], axis=1)) * rate
             sg = 1.0 / (1.0 + jnp.exp(-h1))
             sil = h1 * sg
             act = sil * h3 * rate
@@ -150,14 +155,16 @@
             ah, al = split(act)
             d1h, d1l = split(d1)
             d3h, d3l = split(d3)
-            t1 = nn(d1h, kb) + nn(d1l, kb)
-            t3 = nn(d3h, kb) + nn(d3l, kb)
-            t2 = nn(ah, vb) + nn(al, vb)
+            kk = jnp.concatenate([kb, kb], axis=0)
+            t1 = nn(jnp.concatenate([d1h, d1l], axis=1), kk)
+            t3 = nn(jnp.concatenate([d3h, d3l], axis=1), kk)
+            t2 = nn(jnp.concatenate([ah, al], axis=1), jnp.concatenate([vb, vb], axis=0))
             g1 = t1 if g1 is None else g1 + t1
             g3 = t3 if g3 is None else g3 + t3
             g2 = t2 if g2 is None else g2 + t2
         if head == 0:
             middle = edge + WINDOW_SPAN // 2
+            late.append(copy(k_ref.at[edge : edge + CUT], mid_far))
             late.append(copy(v_ref.at[middle:], low_far))
             late.append(copy(v_ref.at[edge:middle], high_far))
         acc[0:size] = g1
@@ -185,7 +192,7 @@
     rows = 3 * size // 4
     whole = pltpu.VMEM(w1.shape, F32)
     step = min(256, keys.shape[0])
-    copies = 1 + 3 * heads + 2 * (keys.shape[0] // step) + 1 + 5 * heads + 2
+    copies = 1 + 3 * heads + 2 * (keys.shape[0] // step) + 1 + 5 * heads + 3
     scratch = (
         pltpu.VMEM((3 * size, size), F32),
         pltpu.VMEM((heads, rows, size), F32),
@@ -201,8 +208,8 @@
     part = spec((heads, rows, size), F32)
     inputs = [spec(a.shape, a.dtype) for a in (queries, keys, values)]
     half = (WINDOW_SPAN // 2, keys.shape[1])
-    outs = (part, wire, wire, wire, part, *inputs, spec(half, keys.dtype), spec(half, keys.dtype))
-    away = (True, True, True, True, True, False, False, False, True, True)
+    outs = (part, wire, wire, wire, part, *inputs, spec(half, keys.dtype), spec(half, keys.dtype), spec((CUT, keys.shape[1]), keys.dtype))
+    away = (True, True, True, True, True, False, False, False, True, True, True)
     args = (quarter, *far(queries, keys, values, rates_t, w1, w3, w2))
     return call(grads_body, outs, args, [SM] + [FAR] * 7, away, scratch, 1 << 31)
 
@@ -214,7 +221,7 @@
 
 
 def tail(keys):
-    out = spec((WINDOW_SPAN, keys.shape[1]), keys.dtype)
+    out = spec((WINDOW_SPAN - CUT, keys.shape[1]), keys.dtype)
     return call(tail_body, out, far(keys), [FAR], False, (pltpu.SemaphoreType.DMA,))
 
 
@@ -263,7 +270,7 @@
     rows -= PAD
     tokens = q_ref.shape[0]
     q = quarter[0]
-    block = min(256, tokens)
+    block = min(1024, tokens)
     for head in range(heads):
         for j, ref in enumerate((own_ref, r1_ref, r2_ref, r3_ref)):
             n_ref[head, pl.ds(pl.multiple_of((q ^ j) * rows, 8), rows)] = decode(ref.at[head])
@@ -273,10 +280,11 @@
         scale = s_ref[head]
         for start in range(0, tokens, block):
             qb = q_ref[start : start + block, head * size : (head + 1) * size]
-            p1 = nt(qb, n1h) + nt(qb, n1l)
-            p3 = nt(qb, n3h) + nt(qb, n3l)
+            qq = jnp.concatenate([qb, qb], axis=1)
+            p1 = nt(qq, jnp.concatenate([n1h, n1l], axis=1))
+            p3 = nt(qq, jnp.concatenate([n3h, n3l], axis=1))
             hh, hl = split(p1 * (1.0 / (1.0 + jnp.exp(-p1))) * p3)
-            zed = (nt(hh, n2h) + nt(hl, n2h) + nt(hh, n2l)) * scale
+            zed = nt(jnp.concatenate([hh, hl, hh], axis=1), jnp.concatenate([n2h, n2h, n2l], axis=1)) * scale
             z_ref[start : start + block, head * size : (head + 1) * size] = zed
             zz = zed * zed
             half = zz[:, 0:128]
@@ -318,14 +326,14 @@
     return call(weights_body, (square,) * 3, (new,), away=True, scratch=scratch)
 
 
-def attend_body(size, blocks, *refs):
-    for head in range(refs[-1].shape[1] // size):
+def attend_body(heads, size, blocks, *refs):
+    for head in range(heads):
         attend_head(head, size, blocks, *refs)
 
 
 def attend_head(head, size, blocks, first_ref, q_ref, k_ref, v_ref, *refs):
-    halo = refs[:-1]
-    out_ref = refs[-1]
+    early, part, mid = refs[:3] if len(refs) > 1 else (None, None, None)
+    out_ref, probs_ref = (refs[3], refs[4]) if len(refs) > 1 else (refs[0], None)
     step = 256
     span = WINDOW_SPAN // step
     scale = size ** (-0.5)
@@ -339,7 +347,10 @@
             source = block - back
             if source < 0:
                 at = (source + span) * step
-                kb, vb = halo[0][at : at + step, q.cols], halo[span - at // step][:, q.cols]
+                if at == 0:
+                    kb, vb = jnp.concatenate([part[:, q.cols], early[0 : step - CUT, q.cols]], axis=0), None
+                else:
+                    kb, vb = early[at - CUT : at - CUT + step, q.cols], mid[:, q.cols]
             else:
                 kb, vb = k(source), v(source)
             s = nt(qb, kb) * scale
@@ -365,34 +376,47 @@
         inverse = 1.0 / total
         out = None
         for x, vb in zip(expo, vals):
-            part = nn((x * inverse).astype(BF), vb)
+            weight = (x * inverse).astype(BF)
+            if vb is None:
+                probs_ref[:, head * step : (head + 1) * step] = weight
+                continue
+            part = nn(weight, vb)
             out = part if out is None else out + part
         out_ref[place * step : (place + 1) * step, q.cols] = out
 
 
 def attend(first, queries, keys, values, halo, blocks, size):
-    args = (first, queries, keys, values) + (() if halo is None else tuple(halo))
+    heads = queries.shape[1] // size
+    args = (first, queries, keys, values, *halo)
+    out = spec((len(blocks) * 256, queries.shape[1]), F32)
     return call(
-        functools.partial(attend_body, size, blocks),
-        spec((len(blocks) * 256, queries.shape[1]), F32),
+        functools.partial(attend_body, heads, size, blocks),
+        (out, spec((256, heads * 256), BF)) if halo else out,
         args,
         [SM] + [VM] * (len(args) - 1),
         flops=1 << 30,
     )
 
 
-def mix_body(features, r_ref, z_ref, *refs):
-    *parts, out, buf, sems = refs
-    tokens = buf.shape[0]
+def mix_body(features, heads, r_ref, z_ref, low_ref, high_ref, probs_ref, late_ref, out, buf, sems):
+    tokens, width = buf.shape
+    size = width // heads
     step = 128
-    attended = [(ref, at) for ref in parts for at in range(0, ref.shape[0], step)]
+    half = low_ref.shape[0]
     inverse = 1.0 / jnp.sqrt(r_ref[...] / features + EPS)
     copies = []
-    for index in range(tokens // step):
+    for index in reversed(range(tokens // step)):
         start = index * step
         column = jnp.broadcast_to(inverse[:, start : start + step], (128, step)).T[:, 0:1]
-        ref, at = attended[index]
-        buf[start : start + step] = ref[at : at + step] + z_ref[start : start + step] * column
+        attn = low_ref[start : start + step] if start < half else high_ref[start - half : start - half + step]
+        if start < 256:
+            keys = late_ref.shape[0]
+            parts = [
+                nn(probs_ref[start : start + step, h * keys : (h + 1) * keys], late_ref[:, h * size : (h + 1) * size])
+                for h in range(heads)
+            ]
+            attn = attn + jnp.concatenate(parts, axis=1)
+        buf[start : start + step] = attn + z_ref[start : start + step] * column
         made = pltpu.make_async_copy(buf.at[start : start + step], out.at[start : start + step], sems.at[index])
         made.start()
         copies.append(made)
@@ -400,10 +424,11 @@
         made.wait()
 
 
-def mix(total, z, *parts, features):
+def mix(total, z, low, high, probs, late, features, heads):
     scratch = (pltpu.VMEM(z.shape, F32), pltpu.SemaphoreType.DMA((z.shape[0] // 128,)))
-    args = (total, z, *parts)
-    return call(functools.partial(mix_body, features), spec(z.shape, F32), args, away=True, scratch=scratch)
+    args = (total, z, low, high, probs, late)
+    body = functools.partial(mix_body, features, heads)
+    return call(body, spec(z.shape, F32), args, away=True, scratch=scratch)
 
 
 def swap(x, axis, mask):
@@ -445,9 +470,10 @@
 
     halo = [lax.ppermute(tail(keys), "seq", ring)]
     out = grads(quarter, queries, keys, values, rates.T, w_one, w_three, w_two)
-    own, p1, p2, p3, mine_w, q, k, v, end, rest = out
+    own, p1, p2, p3, mine_w, q, k, v, end, rest, part = out
     got = spread((p1, p2, p3))
-    high = attend(first, q, k, v, None, blocks[half:], size)
+    halo.append(lax.ppermute(part, "seq", ring))
+    high = attend(first, q, k, v, (), blocks[half:], size)
     mine = call(gather_body, wire, (after(own, high), *got))
     for mask in shared[:-1]:
         mine = call(cross_body, wire, (mine, swap(mine, "seq", mask)))
@@ -456,17 +482,17 @@
     scratch = (pltpu.VMEM((heads, rows, size), F32), pltpu.SemaphoreType.DMA)
     new = call(renorm_body, wire, (mine_w, mine, other), [FAR, VM, VM], scratch=scratch)
     pieces = (new, *spread((new, new, new)))
-    halo.append(lax.ppermute(after(rest, *pieces), "seq", ring))
-    low1 = attend(first, q, after(k, new), v, halo[:2], blocks[1:half], size)
-    pieces = (after(new, low1), *pieces[1:])
+    late = lax.ppermute(after(rest, *pieces), "seq", ring)
+    low, probs = attend(first, q, after(k, new), v, halo, blocks[:half], size)
+    pieces = (after(new, low), *pieces[1:])
     zed, total, new_t = apply(quarter, q, head_scale, pieces)
-    low0 = attend(first, q, after(k, new_t), v, halo, blocks[:1], size)
     mask = 1
     while mask < lax.axis_size("head"):
         total = total + swap(total, "head", mask)
         mask *= 2
     new_one, new_three, new_two = weights(new_t)
-    mixed = mix(total, zed, low0, low1, high, features=heads * lax.axis_size("head") * size)
+    features = heads * lax.axis_size("head") * size
+    mixed = mix(total, zed, low, high, probs, late, features, heads)
     return (mixed, new_one, new_three, new_two)
 
 

time: 74.9 us -> 77.3 us (1.032)
  waiting for transfers between devices: 16.5 us -> 21.2 us
  Pallas kernels: 27.3 us -> 24 us
    ppermute x9, waiting for transfers between devices: 16.5 us -> 20.9 us  [swap(): lax.ppermute(x, axis, [(i, i ^ mask) for i in range(lax.axis_size(axis))])]
    pallas_call x10 -> x9, Pallas kernels: 27.3 us -> 24 us  [call(): pl.pallas_call(body, out_shape=tuple(made) if many else made[0], in_specs...]
    ppermute x1 -> x2, starting transfers between devices: 0.85 us -> 2.48 us  [the longest x1 2.48 us: per_device(): late = lax.ppermute(after(rest, *pieces), 'seq', ring)]
    ppermute x1, starting transfers between devices: 2.09 us -> 1.29 us  [per_device(): halo.append(lax.ppermute(after(end, mine), 'seq', line))]
  transfers between devices with their start and end apart: 12 -> 13, of which waited for: 8 -> 10; matrix products, arithmetic and copies ran while one was open for 0% -> 0% of each run, Pallas kernels for 20% -> 15%
where the time goes in v3:
time: 77.3 us; the launch traced here: 76.2 us
  starting transfers between devices  30 us (39%)
  Pallas kernels  24 us (31%)
  waiting for transfers between devices  21.2 us (27%)
  between operations  0.93 us (1%)
    ppermute x9, starting transfers between devices, swap(): lax.ppermute(x, axis, [(i, i ^ mask) for i in range(lax.axis_size(axis))])  24.6 us
    pallas_call x9, Pallas kernels, call(): pl.pallas_call(body, out_shape=tuple(made) if many else made[0], in_specs...  24 us
    ppermute x9, waiting for transfers between devices, swap(): lax.ppermute(x, axis, [(i, i ^ mask) for i in range(lax.axis_size(axis))])  20.9 us
    ppermute x1, starting transfers between devices, per_device(): late = lax.ppermute(after(rest, *pieces), 'seq', ring)  2.48 us
  transfers between devices with their start and end apart: 13, of which 10 were waited for; matrix products, arithmetic and copies ran while one was open for 0% of the time, Pallas kernels for 15%

profile of v3, /device:TPU:0, one launch (start us, length us, event | category | flops | bytes accessed | tf_op | source)
XLA Modules:
  0.0 76.2 jit_solution(10372537555065968204)
XLA Ops:
  0.6 9.1 %shard_map.111 = (f32[2,192,256]{2,1,0:T(8,128)}, bf16[2,200,256]{2,1,0:T(8,128)(2,1)}, bf16[2,200,256]{2,1,0:T(8,128)(2,1)}, bf16[2,200,256]{2,1,0:T(8,128)(2,1...) custom-call(s32[1]{0:T(128)} %bitcast.quarter, ...), custom_call_target="tpu_custom_call" | custom-call | flops 2147483648 | bytes 2097152 | tf_op jit(solution)/shard_map/pallas_call | solution.py:38
  9.8 3.0 %collective-permute-start = (bf16[2,200,256]{2,1,0:T(8,128)(2,1)}, bf16[2,200,256]{2,1,0:T(8,128)(2,1)S(1)}, u32[]{:S(2)}, u32[]{:S(2)}) collective-permute-start(bf16[2,200,256]{2,1,0:T(8,128)(2,1)} %get-tuple-element.34), channel_id=1, source_target_pairs={{0,4},{4,0},{8,12},{12,8},{16,20},{20,16},{24,28},{28,24},{1,5},{5... | collective-permute-start | bytes 614408 | tf_op jit(solution)/shard_map/ppermute | solution.py:435
  12.8 1.6 %collective-permute-start.1 = (bf16[2,200,256]{2,1,0:T(8,128)(2,1)}, bf16[2,200,256]{2,1,0:T(8,128)(2,1)S(1)}, u32[]{:S(2)}, u32[]{:S(2)}) collective-permute-start(bf16[2,200,256]{2,1,0:T(8,128)(2,1)} %get-tuple-element.35), channel_id=1, source_target_pairs={{0,8},{4,12},{8,0},{12,4},{16,24},{20,28},{24,16},{28,20},{1,9},{5... | collective-permute-start | bytes 614408 | tf_op jit(solution)/shard_map/ppermute | solution.py:435
  14.4 0.0 collective-permute-start.2
  14.4 0.0 copy-start.1
  14.4 1.7 %shard_map.112.high_ref = f32[512,512]{1,0:T(8,128)S(1)} custom-call(s32[1]{0:T(128)} %bitcast.2.refs_0_, bf16[1024,512]{1,0:T(8,128)(2,1)S(1)} %get-tuple-element.28.refs_1_.q_ref, bf16[1024,512]{1,0:T(8,128)(2,1)S(1)} %get-tuple-element.37.refs_2_, bf16[1024,512]{1,0:T(8,128)(2,1)S(1)} %get-tuple-element.32.refs_3_), custom_call_target="tpu_custom_call" | custom-call | flops 1073741824 | bytes 2097152 | tf_op jit(solution)/shard_map/pallas_call | solution.py:38
  16.1 0.0 copy-start
  16.1 0.0 copy-start.4
  16.2 0.0 copy-start.5
  16.2 0.0 copy-start.3
  16.2 1.9 %collective-permute-done.r1_ref = bf16[2,200,256]{2,1,0:T(8,128)(2,1)S(1)} collective-permute-done((bf16[2,200,256]{2,1,0:T(8,128)(2,1)}, bf16[2,200,256]{2,1,0:T(8,128)(2,1)S(1)}, u32[]{:S(2)}, u32[]{:S(2)}) %collective-permute-start) | collective-permute-done | bytes 204832 | tf_op jit(solution)/shard_map/ppermute | solution.py:435
  18.1 2.9 %collective-permute-done.1.r2_ref = bf16[2,200,256]{2,1,0:T(8,128)(2,1)S(1)} collective-permute-done((bf16[2,200,256]{2,1,0:T(8,128)(2,1)}, bf16[2,200,256]{2,1,0:T(8,128)(2,1)S(1)}, u32[]{:S(2)}, u32[]{:S(2)}) %collective-permute-start.1) | collective-permute-done | bytes 204832 | tf_op jit(solution)/shard_map/ppermute | solution.py:435
  21.0 2.9 %collective-permute-done.2.r3_ref = bf16[2,200,256]{2,1,0:T(8,128)(2,1)} collective-permute-done((bf16[2,200,256]{2,1,0:T(8,128)(2,1)}, bf16[2,200,256]{2,1,0:T(8,128)(2,1)}, u32[]{:S(2)}, u32[]{:S(2)}) %collective-permute-start.2) | collective-permute-done | bytes 204832 | tf_op jit(solution)/shard_map/ppermute | solution.py:435
  23.8 0.0 copy-done.1
  23.8 2.0 %shard_map.113.mine_ref = bf16[2,200,256]{2,1,0:T(8,128)(2,1)S(1)} custom-call(f32[2,192,256]{2,1,0:T(8,128)S(1)} %copy-done.1, bf16[2,200,256]{2,1,0:T(8,128)(2,1)S(1)} %collective-permute-done.r1_ref, bf16[2,200,256]{2,1,0:T(8,128)(2,1)S(1)} %collective-permute-done.1.r2_ref, bf16[2,200,256]{2,1,0:T(8,128)(2,1)} %collective-permute-done.2.r3_ref), custom_call_target="tpu_custom_call" | custom-call | flops 16777216 | bytes 2097152 | tf_op jit(solution)/shard_map/pallas_call | solution.py:38
  25.9 3.8 %collective-permute-start.3 = (bf16[2,200,256]{2,1,0:T(8,128)(2,1)S(1)}, bf16[2,200,256]{2,1,0:T(8,128)(2,1)S(1)}, u32[]{:S(2)}, u32[]{:S(2)}) collective-permute-start(bf16[2,200,256]{2,1,0:T(8,128)(2,1)S(1)} %shard_map.113.mine_ref), channel_id=1, source_target_pairs={{0,24},{4,28},{8,16},{12,20},{16,8},{20,12},{24,0},{28,4},{1,25},{... | collective-permute-start | bytes 614408 | tf_op jit(solution)/shard_map/ppermute | solution.py:435
  29.7 1.0 %shard_map.115 = bf16[384,512]{1,0:T(8,128)(2,1)S(1)} custom-call(bf16[1024,512]{1,0:T(8,128)(2,1)} %k_far.3), custom_call_target="tpu_custom_call" | custom-call | flops 16777216 | bytes 2097152 | tf_op jit(solution)/shard_map/pallas_call | solution.py:38
  30.7 1.5 %collective-permute-start.4 = (bf16[384,512]{1,0:T(8,128)(2,1)S(1)}, bf16[384,512]{1,0:T(8,128)(2,1)S(1)}, u32[]{:S(2)}, u32[]{:S(2)}) collective-permute-start(bf16[384,512]{1,0:T(8,128)(2,1)S(1)} %shard_map.115), channel_id=1, source_target_pairs={{0,4},{4,8},{8,12},{12,16},{16,20},{20,24},{24,28},{28,0},{1,5},{5... | collective-permute-start | bytes 1179656 | tf_op jit(solution)/shard_map/ppermute | solution.py:471
  32.2 1.5 %collective-permute-done.3.other_ref = bf16[2,200,256]{2,1,0:T(8,128)(2,1)S(1)} collective-permute-done((bf16[2,200,256]{2,1,0:T(8,128)(2,1)S(1)}, bf16[2,200,256]{2,1,0:T(8,128)(2,1)S(1)}, u32[]{:S(2)}, u32[]{:S(2)}) %collective-permute-start.3) | collective-permute-done | bytes 204832 | tf_op jit(solution)/shard_map/ppermute | solution.py:435
  33.8 0.0 copy-done
  33.8 1.2 %shard_map.114.own_ref = bf16[2,200,256]{2,1,0:T(8,128)(2,1)S(1)} custom-call(f32[2,192,256]{2,1,0:T(8,128)S(1)} %copy-done, bf16[2,200,256]{2,1,0:T(8,128)(2,1)S(1)} %shard_map.113.mine_ref, bf16[2,200,256]{2,1,0:T(8,128)(2,1)S(1)} %collective-permute-done.3.other_ref), custom_call_target="tpu_custom_call" | custom-call | flops 16777216 | bytes 2097152 | tf_op jit(solution)/shard_map/pallas_call | solution.py:38
  35.0 0.0 copy-start.2
  35.0 13.4 %collective-permute-start.9 = (bf16[2,200,256]{2,1,0:T(8,128)(2,1)S(1)}, bf16[2,200,256]{2,1,0:T(8,128)(2,1)S(1)}, u32[]{:S(2)}, u32[]{:S(2)}) collective-permute-start(bf16[2,200,256]{2,1,0:T(8,128)(2,1)S(1)} %shard_map.114.own_ref), channel_id=1, source_target_pairs={{0,12},{4,8},{8,4},{12,0},{16,28},{20,24},{24,20},{28,16},{1,13},{... | collective-permute-start | bytes 614408 | tf_op jit(solution)/shard_map/ppermute | solution.py:435
  48.4 0.0 copy-done.4
  48.4 1.3 %collective-permute-start.6 = (bf16[256,512]{1,0:T(8,128)(2,1)S(1)}, bf16[256,512]{1,0:T(8,128)(2,1)S(1)}, u32[]{:S(2)}, u32[]{:S(2)}) collective-permute-start(bf16[256,512]{1,0:T(8,128)(2,1)S(1)} %copy-done.4), channel_id=1, source_target_pairs={{0,4},{4,8},{8,12},{12,16},{16,20},{20,24},{24,28},{1,5},{5,9},{9,... | collective-permute-start | bytes 786440 | tf_op jit(solution)/shard_map/ppermute | solution.py:481
  49.7 1.3 %collective-permute-start.8 = (bf16[2,200,256]{2,1,0:T(8,128)(2,1)S(1)}, bf16[2,200,256]{2,1,0:T(8,128)(2,1)S(1)}, u32[]{:S(2)}, u32[]{:S(2)}) collective-permute-start(bf16[2,200,256]{2,1,0:T(8,128)(2,1)S(1)} %shard_map.114.own_ref), channel_id=1, source_target_pairs={{0,8},{4,12},{8,0},{12,4},{16,24},{20,28},{24,16},{28,20},{1,9},{5... | collective-permute-start | bytes 614408 | tf_op jit(solution)/shard_map/ppermute | solution.py:435
  51.0 0.0 collective-permute-start.7
  51.0 3.3 %collective-permute-done.9.r3_ref = bf16[2,200,256]{2,1,0:T(8,128)(2,1)S(1)} collective-permute-done((bf16[2,200,256]{2,1,0:T(8,128)(2,1)S(1)}, bf16[2,200,256]{2,1,0:T(8,128)(2,1)S(1)}, u32[]{:S(2)}, u32[]{:S(2)}) %collective-permute-start.9) | collective-permute-done | bytes 204832 | tf_op jit(solution)/shard_map/ppermute | solution.py:435
  54.3 0.0 copy-done.5
  54.3 0.0 collective-permute-start.5
  54.3 2.1 %collective-permute-done.8.r2_ref = bf16[2,200,256]{2,1,0:T(8,128)(2,1)S(1)} collective-permute-done((bf16[2,200,256]{2,1,0:T(8,128)(2,1)S(1)}, bf16[2,200,256]{2,1,0:T(8,128)(2,1)S(1)}, u32[]{:S(2)}, u32[]{:S(2)}) %collective-permute-start.8) | collective-permute-done | bytes 204832 | tf_op jit(solution)/shard_map/ppermute | solution.py:435
  56.4 4.3 %collective-permute-done.7.r1_ref = bf16[2,200,256]{2,1,0:T(8,128)(2,1)S(1)} collective-permute-done((bf16[2,200,256]{2,1,0:T(8,128)(2,1)S(1)}, bf16[2,200,256]{2,1,0:T(8,128)(2,1)S(1)}, u32[]{:S(2)}, u32[]{:S(2)}) %collective-permute-start.7) | collective-permute-done | bytes 204832 | tf_op jit(solution)/shard_map/ppermute | solution.py:435
  60.7 0.0 copy-done.3
  60.7 2.5 %collective-permute-start.12 = (bf16[256,512]{1,0:T(8,128)(2,1)S(1)}, bf16[256,512]{1,0:T(8,128)(2,1)S(1)}, u32[]{:S(2)}, u32[]{:S(2)}) collective-permute-start(bf16[256,512]{1,0:T(8,128)(2,1)S(1)} %copy-done.3), channel_id=1, source_target_pairs={{0,4},{4,8},{8,12},{12,16},{16,20},{20,24},{24,28},{28,0},{1,5},{5... | collective-permute-start | bytes 786440 | tf_op jit(solution)/shard_map/ppermute | solution.py:485
  63.2 0.3 collective-permute-done.5.refs_5_
  63.6 0.0 collective-permute-done.4.refs_4_
  63.6 0.0 collective-permute-done.6.refs_6_
  63.6 2.1 %shard_map.116 = (f32[512,512]{1,0:T(8,128)S(1)}, bf16[256,512]{1,0:T(8,128)(2,1)S(1)}) custom-call(s32[1]{0:T(128)} %bitcast.2.refs_0_, bf16[1024,512]{1,0:T(8,128)(2,1)S(1)} %get-tuple-element.28.refs_1_.q_ref, bf16[1024,512]{1,0:T(8,128)(2,1)S(1)} %get-tuple-element.37.refs_2_, bf16[1024,512]{1,0:T(8,128)(2,1)S(1)} %get-tuple-element.32.refs_3_, ...), custom_call_target="tpu_custom_call" | custom-call | flops 1073741824 | bytes 2097152 | tf_op jit(solution)/shard_map/pallas_call | solution.py:38
  65.6 0.0 copy-done.2
  65.7 3.9 %shard_map.117 = (f32[1024,512]{1,0:T(8,128)S(1)}, f32[1,1024]{1,0:T(1,128)S(1)}, f32[2,768,256]{2,1,0:T(8,128)S(1)}) custom-call(s32[1]{0:T(128)} %bitcast.quarter, f32[2]{0:T(128)S(1)} %copy-done.2, bf16[1024,512]{1,0:T(8,128)(2,1)S(1)} %get-tuple-element.28.refs_1_.q_ref, bf16[2,200,256]{2,1,0:T(8,128)(2,1)S(1)} %shard_map.114.own_ref, ...), custom_call_target="tpu_custom_call" | custom-call | flops 2147483648 | bytes 2097152 | tf_op jit(solution)/shard_map/pallas_call | solution.py:38
  69.5 0.1 collective-permute-start.10
  69.6 1.2 %collective-permute-done.10 = f32[1,1024]{1,0:T(1,128)S(1)} collective-permute-done((f32[1,1024]{1,0:T(1,128)S(1)}, f32[1,1024]{1,0:T(1,128)S(1)}, u32[]{:S(2)}, u32[]{:S(2)}) %collective-permute-start.10) | collective-permute-done | bytes 4128 | tf_op jit(solution)/shard_map/ppermute | solution.py:435
  70.8 1.5 %collective-permute-start.11 = (f32[1,1024]{1,0:T(1,128)S(1)}, f32[1,1024]{1,0:T(1,128)S(1)}, u32[]{:S(2)}, u32[]{:S(2)}) collective-permute-start(f32[1,1024]{1,0:T(1,128)S(1)} %add.10), channel_id=1, source_target_pairs={{0,2},{1,3},{2,0},{3,1},{4,6},{5,7},{6,4},{7,5},{8,10},{9,11},{10,... | collective-permute-start | bytes 12296 | tf_op jit(solution)/shard_map/ppermute | solution.py:435
  72.3 1.3 %shard_map.119 = (f32[2,256,256]{2,1,0:T(8,128)}, f32[2,256,256]{2,1,0:T(8,128)}, f32[2,256,256]{2,1,0:T(8,128)}) custom-call(f32[2,768,256]{2,1,0:T(8,128)S(1)} %get-tuple-element.48.n_ref), custom_call_target="tpu_custom_call" | custom-call | flops 16777216 | bytes 2097152 | tf_op jit(solution)/shard_map/pallas_call | solution.py:38
  73.6 0.8 %collective-permute-done.11 = f32[1,1024]{1,0:T(1,128)S(1)} collective-permute-done((f32[1,1024]{1,0:T(1,128)S(1)}, f32[1,1024]{1,0:T(1,128)S(1)}, u32[]{:S(2)}, u32[]{:S(2)}) %collective-permute-start.11) | collective-permute-done | bytes 4128 | tf_op jit(solution)/shard_map/ppermute | solution.py:435
  74.4 0.0 collective-permute-done.12.late_ref
  74.4 1.7 %shard_map.118 = f32[1024,512]{1,0:T(8,128)} custom-call(f32[1,1024]{1,0:T(1,128)S(1)} %add.11.r_ref, f32[1024,512]{1,0:T(8,128)S(1)} %get-tuple-element.44.z_ref, f32[512,512]{1,0:T(8,128)S(1)} %get-tuple-element.41.low_ref, f32[512,512]{1,0:T(8,128)S(1)} %shard_map.112.high_ref, bf16[256,512]{1,0:T(8,128)(2,1)S(1)} %get-tuple-element.45.probs_ref, ...), custom_call_target="tpu_custom_call" | custom-call | flops 16777216 | bytes 2097152 | tf_op jit(solution)/shard_map/pallas_call | solution.py:38
  (2 shorter events, 0.0 us)
Async XLA Ops:
  9.8 8.3 %collective-permute-start = (bf16[2,200,256]{2,1,0:T(8,128)(2,1)}, bf16[2,200,256]{2,1,0:T(8,128)(2,1)S(1)}, u32[]{:S(2)}, u32[]{:S(2)}) collective-permute-start(bf16[2,200,256]{2,1,0:T(8,128)(2,1)} %get-tuple-element.34), channel_id=1, source_target_pairs={{0,4},{4,0},{8,12},{12,8},{16,20},{20,16},{24,28},{28,24},{1,5},{5... | collective-permute-start | bytes 614408 | tf_op jit(solution)/shard_map/ppermute | solution.py:435
  12.8 8.2 %collective-permute-start.1 = (bf16[2,200,256]{2,1,0:T(8,128)(2,1)}, bf16[2,200,256]{2,1,0:T(8,128)(2,1)S(1)}, u32[]{:S(2)}, u32[]{:S(2)}) collective-permute-start(bf16[2,200,256]{2,1,0:T(8,128)(2,1)} %get-tuple-element.35), channel_id=1, source_target_pairs={{0,8},{4,12},{8,0},{12,4},{16,24},{20,28},{24,16},{28,20},{1,9},{5... | collective-permute-start | bytes 614408 | tf_op jit(solution)/shard_map/ppermute | solution.py:435
  14.4 9.5 %collective-permute-start.2 = (bf16[2,200,256]{2,1,0:T(8,128)(2,1)}, bf16[2,200,256]{2,1,0:T(8,128)(2,1)}, u32[]{:S(2)}, u32[]{:S(2)}) collective-permute-start(bf16[2,200,256]{2,1,0:T(8,128)(2,1)} %get-tuple-element.36), channel_id=1, source_target_pairs={{0,12},{4,8},{8,4},{12,0},{16,28},{20,24},{24,20},{28,16},{1,13},{... | collective-permute-start | bytes 614408 | tf_op jit(solution)/shard_map/ppermute | solution.py:435
  14.4 9.5 %copy-start.1 = (f32[2,192,256]{2,1,0:T(8,128)S(1)}, f32[2,192,256]{2,1,0:T(8,128)}, u32[]{:S(2)}) copy-start(f32[2,192,256]{2,1,0:T(8,128)} %get-tuple-element.33.own_ref) | copy-start | bytes 1179652
  16.1 17.6 %copy-start = (f32[2,192,256]{2,1,0:T(8,128)S(1)}, f32[2,192,256]{2,1,0:T(8,128)}, u32[]{:S(2)}) copy-start(f32[2,192,256]{2,1,0:T(8,128)} %get-tuple-element.29.w_far) | copy-start | bytes 1179652
  16.1 32.2 %copy-start.4 = (bf16[256,512]{1,0:T(8,128)(2,1)S(1)}, bf16[256,512]{1,0:T(8,128)(2,1)}, u32[]{:S(2)}) copy-start(bf16[256,512]{1,0:T(8,128)(2,1)} %get-tuple-element.40) | copy-start | bytes 786436
  16.2 38.2 %copy-start.5 = (bf16[128,512]{1,0:T(8,128)(2,1)S(1)}, bf16[128,512]{1,0:T(8,128)(2,1)}, u32[]{:S(2)}) copy-start(bf16[128,512]{1,0:T(8,128)(2,1)} %get-tuple-element.38) | copy-start | bytes 393220
  16.2 44.6 %copy-start.3 = (bf16[256,512]{1,0:T(8,128)(2,1)S(1)}, bf16[256,512]{1,0:T(8,128)(2,1)}, u32[]{:S(2)}) copy-start(bf16[256,512]{1,0:T(8,128)(2,1)} %get-tuple-element.47) | copy-start | bytes 786436
  25.9 7.9 %collective-permute-start.3 = (bf16[2,200,256]{2,1,0:T(8,128)(2,1)S(1)}, bf16[2,200,256]{2,1,0:T(8,128)(2,1)S(1)}, u32[]{:S(2)}, u32[]{:S(2)}) collective-permute-start(bf16[2,200,256]{2,1,0:T(8,128)(2,1)S(1)} %shard_map.113.mine_ref), channel_id=1, source_target_pairs={{0,24},{4,28},{8,16},{12,20},{16,8},{20,12},{24,0},{28,4},{1,25},{... | collective-permute-start | bytes 614408 | tf_op jit(solution)/shard_map/ppermute | solution.py:435
  30.7 32.9 %collective-permute-start.4 = (bf16[384,512]{1,0:T(8,128)(2,1)S(1)}, bf16[384,512]{1,0:T(8,128)(2,1)S(1)}, u32[]{:S(2)}, u32[]{:S(2)}) collective-permute-start(bf16[384,512]{1,0:T(8,128)(2,1)S(1)} %shard_map.115), channel_id=1, source_target_pairs={{0,4},{4,8},{8,12},{12,16},{16,20},{20,24},{24,28},{28,0},{1,5},{5... | collective-permute-start | bytes 1179656 | tf_op jit(solution)/shard_map/ppermute | solution.py:471
  35.0 30.6 %copy-start.2 = (f32[2]{0:T(128)S(1)}, f32[2]{0:T(128)}, u32[]{:S(2)}) copy-start(f32[2]{0:T(128)} %s_ref.1) | copy-start | bytes 28
  35.0 19.3 %collective-permute-start.9 = (bf16[2,200,256]{2,1,0:T(8,128)(2,1)S(1)}, bf16[2,200,256]{2,1,0:T(8,128)(2,1)S(1)}, u32[]{:S(2)}, u32[]{:S(2)}) collective-permute-start(bf16[2,200,256]{2,1,0:T(8,128)(2,1)S(1)} %shard_map.114.own_ref), channel_id=1, source_target_pairs={{0,12},{4,8},{8,4},{12,0},{16,28},{20,24},{24,20},{28,16},{1,13},{... | collective-permute-start | bytes 614408 | tf_op jit(solution)/shard_map/ppermute | solution.py:435
  48.4 15.2 %collective-permute-start.6 = (bf16[256,512]{1,0:T(8,128)(2,1)S(1)}, bf16[256,512]{1,0:T(8,128)(2,1)S(1)}, u32[]{:S(2)}, u32[]{:S(2)}) collective-permute-start(bf16[256,512]{1,0:T(8,128)(2,1)S(1)} %copy-done.4), channel_id=1, source_target_pairs={{0,4},{4,8},{8,12},{12,16},{16,20},{20,24},{24,28},{1,5},{5,9},{9,... | collective-permute-start | bytes 786440 | tf_op jit(solution)/shard_map/ppermute | solution.py:481
  49.7 6.8 %collective-permute-start.8 = (bf16[2,200,256]{2,1,0:T(8,128)(2,1)S(1)}, bf16[2,200,256]{2,1,0:T(8,128)(2,1)S(1)}, u32[]{:S(2)}, u32[]{:S(2)}) collective-permute-start(bf16[2,200,256]{2,1,0:T(8,128)(2,1)S(1)} %shard_map.114.own_ref), channel_id=1, source_target_pairs={{0,8},{4,12},{8,0},{12,4},{16,24},{20,28},{24,16},{28,20},{1,9},{5... | collective-permute-start | bytes 614408 | tf_op jit(solution)/shard_map/ppermute | solution.py:435
  51.0 9.8 %collective-permute-start.7 = (bf16[2,200,256]{2,1,0:T(8,128)(2,1)S(1)}, bf16[2,200,256]{2,1,0:T(8,128)(2,1)S(1)}, u32[]{:S(2)}, u32[]{:S(2)}) collective-permute-start(bf16[2,200,256]{2,1,0:T(8,128)(2,1)S(1)} %shard_map.114.own_ref), channel_id=1, source_target_pairs={{0,4},{4,0},{8,12},{12,8},{16,20},{20,16},{24,28},{28,24},{1,5},{5... | collective-permute-start | bytes 614408 | tf_op jit(solution)/shard_map/ppermute | solution.py:435
  54.3 9.2 %collective-permute-start.5 = (bf16[128,512]{1,0:T(8,128)(2,1)S(1)}, bf16[128,512]{1,0:T(8,128)(2,1)S(1)}, u32[]{:S(2)}, u32[]{:S(2)}) collective-permute-start(bf16[128,512]{1,0:T(8,128)(2,1)S(1)} %copy-done.5), channel_id=1, source_target_pairs={{0,4},{4,8},{8,12},{12,16},{16,20},{20,24},{24,28},{28,0},{1,5},{5... | collective-permute-start | bytes 393224 | tf_op jit(solution)/shard_map/ppermute | solution.py:475
  60.7 13.6 %collective-permute-start.12 = (bf16[256,512]{1,0:T(8,128)(2,1)S(1)}, bf16[256,512]{1,0:T(8,128)(2,1)S(1)}, u32[]{:S(2)}, u32[]{:S(2)}) collective-permute-start(bf16[256,512]{1,0:T(8,128)(2,1)S(1)} %copy-done.3), channel_id=1, source_target_pairs={{0,4},{4,8},{8,12},{12,16},{16,20},{20,24},{24,28},{28,0},{1,5},{5... | collective-permute-start | bytes 786440 | tf_op jit(solution)/shard_map/ppermute | solution.py:485
  69.5 1.2 %collective-permute-start.10 = (f32[1,1024]{1,0:T(1,128)S(1)}, f32[1,1024]{1,0:T(1,128)S(1)}, u32[]{:S(2)}, u32[]{:S(2)}) collective-permute-start(f32[1,1024]{1,0:T(1,128)S(1)} %get-tuple-element.43), channel_id=1, source_target_pairs={{0,1},{1,0},{2,3},{3,2},{4,5},{5,4},{6,7},{7,6},{8,9},{9,8},{10,11... | collective-permute-start | bytes 12296 | tf_op jit(solution)/shard_map/ppermute | solution.py:435
  70.8 3.6 %collective-permute-start.11 = (f32[1,1024]{1,0:T(1,128)S(1)}, f32[1,1024]{1,0:T(1,128)S(1)}, u32[]{:S(2)}, u32[]{:S(2)}) collective-permute-start(f32[1,1024]{1,0:T(1,128)S(1)} %add.10), channel_id=1, source_target_pairs={{0,2},{1,3},{2,0},{3,1},{4,6},{5,7},{6,4},{7,5},{8,10},{9,11},{10,... | collective-permute-start | bytes 12296 | tf_op jit(solution)/shard_map/ppermute | solution.py:435

commit v4 on v3

--- a/solution.py
+++ b/solution.py
@@ -482,14 +482,18 @@
     scratch = (pltpu.VMEM((heads, rows, size), F32), pltpu.SemaphoreType.DMA)
     new = call(renorm_body, wire, (mine_w, mine, other), [FAR, VM, VM], scratch=scratch)
     pieces = (new, *spread((new, new, new)))
-    late = lax.ppermute(after(rest, *pieces), "seq", ring)
+    late = lax.ppermute(after(rest, pieces[1]), "seq", ring)
     low, probs = attend(first, q, after(k, new), v, halo, blocks[:half], size)
     pieces = (after(new, low), *pieces[1:])
     zed, total, new_t = apply(quarter, q, head_scale, pieces)
-    mask = 1
-    while mask < lax.axis_size("head"):
-        total = total + swap(total, "head", mask)
-        mask *= 2
+    mask, reach = 1, lax.axis_size("head")
+    while mask < reach:
+        masks = (3 * mask, 2 * mask, mask) if 4 * mask <= reach else (mask,)
+        parts = []
+        for m in masks:
+            parts.append(swap(total, "head", m))
+        total = sum(parts, total)
+        mask *= len(masks) + 1
     new_one, new_three, new_two = weights(new_t)
     features = heads * lax.axis_size("head") * size
     mixed = mix(total, zed, low, high, probs, late, features, heads)

time: 77.3 us -> 69.8 us (0.903); the launches traced: 76.2 us -> 69.5 us
  waiting for transfers between devices: 21.2 us -> 10.7 us
  starting transfers between devices: 30 us -> 32.6 us
  Pallas kernels: 24 us -> 25.2 us
    ppermute x9 -> x10, waiting for transfers between devices: 20.9 us -> 10.7 us  [swap(): lax.ppermute(x, axis, [(i, i ^ mask) for i in range(lax.axis_size(axis))])]
    ppermute x1, starting transfers between devices: 0.01 us -> 5.18 us  [per_device(): halo.append(lax.ppermute(part, 'seq', ring))]
    ppermute x9 -> x10, starting transfers between devices: 24.6 us -> 21.7 us  [swap(): lax.ppermute(x, axis, [(i, i ^ mask) for i in range(lax.axis_size(axis))])]
    pallas_call x9, Pallas kernels: 24 us -> 25.2 us  [call(): pl.pallas_call(body, out_shape=tuple(made) if many else made[0], in_specs...]
    ppermute x1, starting transfers between devices: 1.29 us -> 2.09 us  [per_device(): halo.append(lax.ppermute(after(end, mine), 'seq', line))]
    ppermute x1, starting transfers between devices: 2.48 us -> 1.71 us  [per_device(): late = lax.ppermute(after(rest, pieces[1]), 'seq', ring)]
  transfers between devices with their start and end apart: 13 -> 14, of which waited for: 10 -> 6; matrix products, arithmetic and copies ran while one was open for 0% -> 0% of each run, Pallas kernels for 15% -> 21%
where the time goes in v4:
time: 69.8 us; the launch traced here: 69.5 us
  starting transfers between devices  32.6 us (47%)
  Pallas kernels  25.2 us (36%)
  waiting for transfers between devices  10.7 us (15%)
  between operations  0.95 us (1%)
    pallas_call x9, Pallas kernels, call(): pl.pallas_call(body, out_shape=tuple(made) if many else made[0], in_specs...  25.2 us
    ppermute x10, starting transfers between devices, swap(): lax.ppermute(x, axis, [(i, i ^ mask) for i in range(lax.axis_size(axis))])  21.7 us
    ppermute x10, waiting for transfers between devices, swap(): lax.ppermute(x, axis, [(i, i ^ mask) for i in range(lax.axis_size(axis))])  10.7 us
    ppermute x1, starting transfers between devices, per_device(): halo.append(lax.ppermute(part, 'seq', ring))  5.18 us
    ppermute x1, starting transfers between devices, per_device(): halo.append(lax.ppermute(after(end, mine), 'seq', line))  2.09 us
    ppermute x1, starting transfers between devices, per_device(): halo = [lax.ppermute(tail(keys), 'seq', ring)]  1.96 us
    ppermute x1, starting transfers between devices, per_device(): late = lax.ppermute(after(rest, pieces[1]), 'seq', ring)  1.71 us
  transfers between devices with their start and end apart: 14, of which 6 were waited for; matrix products, arithmetic and copies ran while one was open for 0% of the time, Pallas kernels for 21%

profile of v4, /device:TPU:0, one launch (start us, length us, event | category | flops | bytes accessed | tf_op | source)
XLA Modules:
  0.0 69.5 jit_solution(7282124531223917147)
XLA Ops:
  0.6 9.1 %shard_map.111 = (f32[2,192,256]{2,1,0:T(8,128)}, bf16[2,200,256]{2,1,0:T(8,128)(2,1)}, bf16[2,200,256]{2,1,0:T(8,128)(2,1)}, bf16[2,200,256]{2,1,0:T(8,128)(2,1...) custom-call(s32[1]{0:T(128)} %bitcast.quarter, ...), custom_call_target="tpu_custom_call" | custom-call | flops 2147483648 | bytes 2097152 | tf_op jit(solution)/shard_map/pallas_call | solution.py:38
  9.8 3.0 %collective-permute-start = (bf16[2,200,256]{2,1,0:T(8,128)(2,1)}, bf16[2,200,256]{2,1,0:T(8,128)(2,1)}, u32[]{:S(2)}, u32[]{:S(2)}) collective-permute-start(bf16[2,200,256]{2,1,0:T(8,128)(2,1)} %get-tuple-element.34), channel_id=1, source_target_pairs={{0,4},{4,0},{8,12},{12,8},{16,20},{20,16},{24,28},{28,24},{1,5},{5... | collective-permute-start | bytes 614408 | tf_op jit(solution)/shard_map/ppermute | solution.py:435
  12.8 1.6 %collective-permute-start.1 = (bf16[2,200,256]{2,1,0:T(8,128)(2,1)}, bf16[2,200,256]{2,1,0:T(8,128)(2,1)}, u32[]{:S(2)}, u32[]{:S(2)}) collective-permute-start(bf16[2,200,256]{2,1,0:T(8,128)(2,1)} %get-tuple-element.35), channel_id=1, source_target_pairs={{0,8},{4,12},{8,0},{12,4},{16,24},{20,28},{24,16},{28,20},{1,9},{5... | collective-permute-start | bytes 614408 | tf_op jit(solution)/shard_map/ppermute | solution.py:435
  14.4 0.0 collective-permute-start.2
  14.4 1.0 %shard_map.115 = bf16[384,512]{1,0:T(8,128)(2,1)S(1)} custom-call(bf16[1024,512]{1,0:T(8,128)(2,1)} %k_far.3), custom_call_target="tpu_custom_call" | custom-call | flops 16777216 | bytes 2097152 | tf_op jit(solution)/shard_map/pallas_call | solution.py:38
  15.4 2.0 %collective-permute-start.4 = (bf16[384,512]{1,0:T(8,128)(2,1)S(1)}, bf16[384,512]{1,0:T(8,128)(2,1)}, u32[]{:S(2)}, u32[]{:S(2)}) collective-permute-start(bf16[384,512]{1,0:T(8,128)(2,1)S(1)} %shard_map.115), channel_id=1, source_target_pairs={{0,4},{4,8},{8,12},{12,16},{16,20},{20,24},{24,28},{28,0},{1,5},{5... | collective-permute-start | bytes 1179656 | tf_op jit(solution)/shard_map/ppermute | solution.py:471
  17.4 0.0 copy-start.1
  17.4 0.0 copy-start.5
  17.4 0.0 copy-start
  17.4 1.7 %shard_map.112.high_ref = f32[512,512]{1,0:T(8,128)S(1)} custom-call(s32[1]{0:T(128)} %bitcast.2.refs_0_, bf16[1024,512]{1,0:T(8,128)(2,1)S(1)} %get-tuple-element.28.refs_1_.q_ref, bf16[1024,512]{1,0:T(8,128)(2,1)S(1)} %get-tuple-element.37.refs_2_, bf16[1024,512]{1,0:T(8,128)(2,1)S(1)} %get-tuple-element.32.refs_3_), custom_call_target="tpu_custom_call" | custom-call | flops 1073741824 | bytes 2097152 | tf_op jit(solution)/shard_map/pallas_call | solution.py:38
  19.1 0.0 collective-permute-done.r1_ref
  19.1 1.9 %collective-permute-done.1.r2_ref = bf16[2,200,256]{2,1,0:T(8,128)(2,1)} collective-permute-done((bf16[2,200,256]{2,1,0:T(8,128)(2,1)}, bf16[2,200,256]{2,1,0:T(8,128)(2,1)}, u32[]{:S(2)}, u32[]{:S(2)}) %collective-permute-start.1) | collective-permute-done | bytes 204832 | tf_op jit(solution)/shard_map/ppermute | solution.py:435
  21.1 2.8 %collective-permute-done.2.r3_ref = bf16[2,200,256]{2,1,0:T(8,128)(2,1)} collective-permute-done((bf16[2,200,256]{2,1,0:T(8,128)(2,1)}, bf16[2,200,256]{2,1,0:T(8,128)(2,1)}, u32[]{:S(2)}, u32[]{:S(2)}) %collective-permute-start.2) | collective-permute-done | bytes 204832 | tf_op jit(solution)/shard_map/ppermute | solution.py:435
  23.9 0.0 copy-done.1
  23.9 2.2 %shard_map.113.mine_ref = bf16[2,200,256]{2,1,0:T(8,128)(2,1)S(1)} custom-call(f32[2,192,256]{2,1,0:T(8,128)S(1)} %copy-done.1, bf16[2,200,256]{2,1,0:T(8,128)(2,1)} %collective-permute-done.r1_ref, bf16[2,200,256]{2,1,0:T(8,128)(2,1)} %collective-permute-done.1.r2_ref, bf16[2,200,256]{2,1,0:T(8,128)(2,1)} %collective-permute-done.2.r3_ref), custom_call_target="tpu_custom_call" | custom-call | flops 16777216 | bytes 2097152 | tf_op jit(solution)/shard_map/pallas_call | solution.py:38
  26.1 5.2 %collective-permute-start.3 = (bf16[2,200,256]{2,1,0:T(8,128)(2,1)S(1)}, bf16[2,200,256]{2,1,0:T(8,128)(2,1)S(1)}, u32[]{:S(2)}, u32[]{:S(2)}) collective-permute-start(bf16[2,200,256]{2,1,0:T(8,128)(2,1)S(1)} %shard_map.113.mine_ref), channel_id=1, source_target_pairs={{0,24},{4,28},{8,16},{12,20},{16,8},{20,12},{24,0},{28,4},{1,25},{... | collective-permute-start | bytes 614408 | tf_op jit(solution)/shard_map/ppermute | solution.py:435
  31.3 0.0 copy-done.4
  31.3 2.1 %collective-permute-start.6 = (bf16[256,512]{1,0:T(8,128)(2,1)S(1)}, bf16[256,512]{1,0:T(8,128)(2,1)S(1)}, u32[]{:S(2)}, u32[]{:S(2)}) collective-permute-start(bf16[256,512]{1,0:T(8,128)(2,1)S(1)} %copy-done.4), channel_id=1, source_target_pairs={{0,4},{4,8},{8,12},{12,16},{16,20},{20,24},{24,28},{1,5},{5,9},{9,... | collective-permute-start | bytes 786440 | tf_op jit(solution)/shard_map/ppermute | solution.py:481
  33.4 0.0 copy-done.5
  33.4 5.2 %collective-permute-start.5 = (bf16[128,512]{1,0:T(8,128)(2,1)S(1)}, bf16[128,512]{1,0:T(8,128)(2,1)S(1)}, u32[]{:S(2)}, u32[]{:S(2)}) collective-permute-start(bf16[128,512]{1,0:T(8,128)(2,1)S(1)} %copy-done.5), channel_id=1, source_target_pairs={{0,4},{4,8},{8,12},{12,16},{16,20},{20,24},{24,28},{28,0},{1,5},{5... | collective-permute-start | bytes 393224 | tf_op jit(solution)/shard_map/ppermute | solution.py:475
  38.6 0.0 collective-permute-done.3.other_ref
  38.6 0.0 copy-done
  38.6 1.2 %shard_map.114.own_ref = bf16[2,200,256]{2,1,0:T(8,128)(2,1)S(1)} custom-call(f32[2,192,256]{2,1,0:T(8,128)S(1)} %copy-done, bf16[2,200,256]{2,1,0:T(8,128)(2,1)S(1)} %shard_map.113.mine_ref, bf16[2,200,256]{2,1,0:T(8,128)(2,1)S(1)} %collective-permute-done.3.other_ref), custom_call_target="tpu_custom_call" | custom-call | flops 16777216 | bytes 2097152 | tf_op jit(solution)/shard_map/pallas_call | solution.py:38
  39.8 0.0 copy-start.3
  39.8 0.0 copy-start.2
  39.9 3.7 %collective-permute-start.7 = (bf16[2,200,256]{2,1,0:T(8,128)(2,1)S(1)}, bf16[2,200,256]{2,1,0:T(8,128)(2,1)S(1)}, u32[]{:S(2)}, u32[]{:S(2)}) collective-permute-start(bf16[2,200,256]{2,1,0:T(8,128)(2,1)S(1)} %shard_map.114.own_ref), channel_id=1, source_target_pairs={{0,4},{4,0},{8,12},{12,8},{16,20},{20,16},{24,28},{28,24},{1,5},{5... | collective-permute-start | bytes 614408 | tf_op jit(solution)/shard_map/ppermute | solution.py:435
  43.5 5.8 %collective-permute-start.9 = (bf16[2,200,256]{2,1,0:T(8,128)(2,1)S(1)}, bf16[2,200,256]{2,1,0:T(8,128)(2,1)S(1)}, u32[]{:S(2)}, u32[]{:S(2)}) collective-permute-start(bf16[2,200,256]{2,1,0:T(8,128)(2,1)S(1)} %shard_map.114.own_ref), channel_id=1, source_target_pairs={{0,12},{4,8},{8,4},{12,0},{16,28},{20,24},{24,20},{28,16},{1,13},{... | collective-permute-start | bytes 614408 | tf_op jit(solution)/shard_map/ppermute | solution.py:435
  49.3 0.0 collective-permute-done.5.refs_5_
  49.3 0.5 collective-permute-start.8
  49.8 0.0 collective-permute-done.4.refs_4_
  49.8 0.0 collective-permute-done.6.refs_6_
  49.8 3.1 %shard_map.116 = (f32[512,512]{1,0:T(8,128)S(1)}, bf16[256,512]{1,0:T(8,128)(2,1)S(1)}) custom-call(s32[1]{0:T(128)} %bitcast.2.refs_0_, bf16[1024,512]{1,0:T(8,128)(2,1)S(1)} %get-tuple-element.28.refs_1_.q_ref, bf16[1024,512]{1,0:T(8,128)(2,1)S(1)} %get-tuple-element.37.refs_2_, bf16[1024,512]{1,0:T(8,128)(2,1)S(1)} %get-tuple-element.32.refs_3_, ...), custom_call_target="tpu_custom_call" | custom-call | flops 1073741824 | bytes 2097152 | tf_op jit(solution)/shard_map/pallas_call | solution.py:38
  52.9 0.0 collective-permute-done.7.r1_ref
  52.9 0.0 copy-done.3
  52.9 1.7 %collective-permute-start.13 = (bf16[256,512]{1,0:T(8,128)(2,1)S(1)}, bf16[256,512]{1,0:T(8,128)(2,1)S(1)}, u32[]{:S(2)}, u32[]{:S(2)}) collective-permute-start(bf16[256,512]{1,0:T(8,128)(2,1)S(1)} %copy-done.3), channel_id=1, source_target_pairs={{0,4},{4,8},{8,12},{12,16},{16,20},{20,24},{24,28},{28,0},{1,5},{5... | collective-permute-start | bytes 786440 | tf_op jit(solution)/shard_map/ppermute | solution.py:485
  54.6 0.6 collective-permute-done.9.r3_ref
  55.2 3.9 %collective-permute-done.8.r2_ref = bf16[2,200,256]{2,1,0:T(8,128)(2,1)S(1)} collective-permute-done((bf16[2,200,256]{2,1,0:T(8,128)(2,1)S(1)}, bf16[2,200,256]{2,1,0:T(8,128)(2,1)S(1)}, u32[]{:S(2)}, u32[]{:S(2)}) %collective-permute-start.8) | collective-permute-done | bytes 204832 | tf_op jit(solution)/shard_map/ppermute | solution.py:435
  59.1 0.0 copy-done.2
  59.1 3.9 %shard_map.117 = (f32[1024,512]{1,0:T(8,128)S(1)}, f32[1,1024]{1,0:T(1,128)S(1)}, f32[2,768,256]{2,1,0:T(8,128)S(1)}) custom-call(s32[1]{0:T(128)} %bitcast.quarter, f32[2]{0:T(128)S(1)} %copy-done.2, bf16[1024,512]{1,0:T(8,128)(2,1)S(1)} %get-tuple-element.28.refs_1_.q_ref, bf16[2,200,256]{2,1,0:T(8,128)(2,1)S(1)} %shard_map.114.own_ref, ...), custom_call_target="tpu_custom_call" | custom-call | flops 2147483648 | bytes 2097152 | tf_op jit(solution)/shard_map/pallas_call | solution.py:38
  63.0 0.1 collective-permute-start.12
  63.1 1.6 %collective-permute-start.11 = (f32[1,1024]{1,0:T(1,128)S(1)}, f32[1,1024]{1,0:T(1,128)S(1)}, u32[]{:S(2)}, u32[]{:S(2)}) collective-permute-start(f32[1,1024]{1,0:T(1,128)S(1)} %get-tuple-element.43), channel_id=1, source_target_pairs={{0,2},{1,3},{2,0},{3,1},{4,6},{5,7},{6,4},{7,5},{8,10},{9,11},{10,... | collective-permute-start | bytes 12296 | tf_op jit(solution)/shard_map/ppermute | solution.py:435
  64.7 0.3 collective-permute-start.10
  64.9 1.3 %shard_map.119 = (f32[2,256,256]{2,1,0:T(8,128)}, f32[2,256,256]{2,1,0:T(8,128)}, f32[2,256,256]{2,1,0:T(8,128)}) custom-call(f32[2,768,256]{2,1,0:T(8,128)S(1)} %get-tuple-element.48.n_ref), custom_call_target="tpu_custom_call" | custom-call | flops 16777216 | bytes 2097152 | tf_op jit(solution)/shard_map/pallas_call | solution.py:38
  66.3 0.0 collective-permute-done.12
  66.3 0.5 collective-permute-done.11
  66.8 0.9 %collective-permute-done.10 = f32[1,1024]{1,0:T(1,128)S(1)} collective-permute-done((f32[1,1024]{1,0:T(1,128)S(1)}, f32[1,1024]{1,0:T(1,128)S(1)}, u32[]{:S(2)}, u32[]{:S(2)}) %collective-permute-start.10) | collective-permute-done | bytes 4128 | tf_op jit(solution)/shard_map/ppermute | solution.py:435
  67.7 0.0 collective-permute-done.13.late_ref
  67.7 1.7 %shard_map.118 = f32[1024,512]{1,0:T(8,128)} custom-call(f32[1,1024]{1,0:T(1,128)S(1)} %add_add_fusion.r_ref, f32[1024,512]{1,0:T(8,128)S(1)} %get-tuple-element.44.z_ref, f32[512,512]{1,0:T(8,128)S(1)} %get-tuple-element.41.low_ref, f32[512,512]{1,0:T(8,128)S(1)} %shard_map.112.high_ref, bf16[256,512]{1,0:T(8,128)(2,1)S(1)} %get-tuple-element.45.probs_ref, ...), custom_call_target="tpu_custom_call" | custom-call | flops 16777216 | bytes 2097152 | tf_op jit(solution)/shard_map/pallas_call | solution.py:38
  (2 shorter events, 0.0 us)
Async XLA Ops:
  9.8 9.3 %collective-permute-start = (bf16[2,200,256]{2,1,0:T(8,128)(2,1)}, bf16[2,200,256]{2,1,0:T(8,128)(2,1)}, u32[]{:S(2)}, u32[]{:S(2)}) collective-permute-start(bf16[2,200,256]{2,1,0:T(8,128)(2,1)} %get-tuple-element.34), channel_id=1, source_target_pairs={{0,4},{4,0},{8,12},{12,8},{16,20},{20,16},{24,28},{28,24},{1,5},{5... | collective-permute-start | bytes 614408 | tf_op jit(solution)/shard_map/ppermute | solution.py:435
  12.8 8.3 %collective-permute-start.1 = (bf16[2,200,256]{2,1,0:T(8,128)(2,1)}, bf16[2,200,256]{2,1,0:T(8,128)(2,1)}, u32[]{:S(2)}, u32[]{:S(2)}) collective-permute-start(bf16[2,200,256]{2,1,0:T(8,128)(2,1)} %get-tuple-element.35), channel_id=1, source_target_pairs={{0,8},{4,12},{8,0},{12,4},{16,24},{20,28},{24,16},{28,20},{1,9},{5... | collective-permute-start | bytes 614408 | tf_op jit(solution)/shard_map/ppermute | solution.py:435
  14.4 9.5 %collective-permute-start.2 = (bf16[2,200,256]{2,1,0:T(8,128)(2,1)}, bf16[2,200,256]{2,1,0:T(8,128)(2,1)}, u32[]{:S(2)}, u32[]{:S(2)}) collective-permute-start(bf16[2,200,256]{2,1,0:T(8,128)(2,1)} %get-tuple-element.36), channel_id=1, source_target_pairs={{0,12},{4,8},{8,4},{12,0},{16,28},{20,24},{24,20},{28,16},{1,13},{... | collective-permute-start | bytes 614408 | tf_op jit(solution)/shard_map/ppermute | solution.py:435
  15.4 34.4 %collective-permute-start.4 = (bf16[384,512]{1,0:T(8,128)(2,1)S(1)}, bf16[384,512]{1,0:T(8,128)(2,1)}, u32[]{:S(2)}, u32[]{:S(2)}) collective-permute-start(bf16[384,512]{1,0:T(8,128)(2,1)S(1)} %shard_map.115), channel_id=1, source_target_pairs={{0,4},{4,8},{8,12},{12,16},{16,20},{20,24},{24,28},{28,0},{1,5},{5... | collective-permute-start | bytes 1179656 | tf_op jit(solution)/shard_map/ppermute | solution.py:471
  17.4 6.5 %copy-start.1 = (f32[2,192,256]{2,1,0:T(8,128)S(1)}, f32[2,192,256]{2,1,0:T(8,128)}, u32[]{:S(2)}) copy-start(f32[2,192,256]{2,1,0:T(8,128)} %get-tuple-element.33.own_ref) | copy-start | bytes 1179652
  17.4 13.9 %copy-start.4 = (bf16[256,512]{1,0:T(8,128)(2,1)S(1)}, bf16[256,512]{1,0:T(8,128)(2,1)}, u32[]{:S(2)}) copy-start(bf16[256,512]{1,0:T(8,128)(2,1)} %get-tuple-element.40) | copy-start | bytes 786436
  17.4 16.0 %copy-start.5 = (bf16[128,512]{1,0:T(8,128)(2,1)S(1)}, bf16[128,512]{1,0:T(8,128)(2,1)}, u32[]{:S(2)}) copy-start(bf16[128,512]{1,0:T(8,128)(2,1)} %get-tuple-element.38) | copy-start | bytes 393220
  17.4 21.2 %copy-start = (f32[2,192,256]{2,1,0:T(8,128)S(1)}, f32[2,192,256]{2,1,0:T(8,128)}, u32[]{:S(2)}) copy-start(f32[2,192,256]{2,1,0:T(8,128)} %get-tuple-element.29.w_far) | copy-start | bytes 1179652
  26.1 12.5 %collective-permute-start.3 = (bf16[2,200,256]{2,1,0:T(8,128)(2,1)S(1)}, bf16[2,200,256]{2,1,0:T(8,128)(2,1)S(1)}, u32[]{:S(2)}, u32[]{:S(2)}) collective-permute-start(bf16[2,200,256]{2,1,0:T(8,128)(2,1)S(1)} %shard_map.113.mine_ref), channel_id=1, source_target_pairs={{0,24},{4,28},{8,16},{12,20},{16,8},{20,12},{24,0},{28,4},{1,25},{... | collective-permute-start | bytes 614408 | tf_op jit(solution)/shard_map/ppermute | solution.py:435
  31.3 18.5 %collective-permute-start.6 = (bf16[256,512]{1,0:T(8,128)(2,1)S(1)}, bf16[256,512]{1,0:T(8,128)(2,1)S(1)}, u32[]{:S(2)}, u32[]{:S(2)}) collective-permute-start(bf16[256,512]{1,0:T(8,128)(2,1)S(1)} %copy-done.4), channel_id=1, source_target_pairs={{0,4},{4,8},{8,12},{12,16},{16,20},{20,24},{24,28},{1,5},{5,9},{9,... | collective-permute-start | bytes 786440 | tf_op jit(solution)/shard_map/ppermute | solution.py:481
  33.4 15.9 %collective-permute-start.5 = (bf16[128,512]{1,0:T(8,128)(2,1)S(1)}, bf16[128,512]{1,0:T(8,128)(2,1)S(1)}, u32[]{:S(2)}, u32[]{:S(2)}) collective-permute-start(bf16[128,512]{1,0:T(8,128)(2,1)S(1)} %copy-done.5), channel_id=1, source_target_pairs={{0,4},{4,8},{8,12},{12,16},{16,20},{20,24},{24,28},{28,0},{1,5},{5... | collective-permute-start | bytes 393224 | tf_op jit(solution)/shard_map/ppermute | solution.py:475
  39.8 13.0 %copy-start.3 = (bf16[256,512]{1,0:T(8,128)(2,1)S(1)}, bf16[256,512]{1,0:T(8,128)(2,1)}, u32[]{:S(2)}) copy-start(bf16[256,512]{1,0:T(8,128)(2,1)} %get-tuple-element.47) | copy-start | bytes 786436
  39.8 19.3 %copy-start.2 = (f32[2]{0:T(128)S(1)}, f32[2]{0:T(128)}, u32[]{:S(2)}) copy-start(f32[2]{0:T(128)} %s_ref.1) | copy-start | bytes 28
  39.9 13.0 %collective-permute-start.7 = (bf16[2,200,256]{2,1,0:T(8,128)(2,1)S(1)}, bf16[2,200,256]{2,1,0:T(8,128)(2,1)S(1)}, u32[]{:S(2)}, u32[]{:S(2)}) collective-permute-start(bf16[2,200,256]{2,1,0:T(8,128)(2,1)S(1)} %shard_map.114.own_ref), channel_id=1, source_target_pairs={{0,4},{4,0},{8,12},{12,8},{16,20},{20,16},{24,28},{28,24},{1,5},{5... | collective-permute-start | bytes 614408 | tf_op jit(solution)/shard_map/ppermute | solution.py:435
  43.5 11.7 %collective-permute-start.9 = (bf16[2,200,256]{2,1,0:T(8,128)(2,1)S(1)}, bf16[2,200,256]{2,1,0:T(8,128)(2,1)S(1)}, u32[]{:S(2)}, u32[]{:S(2)}) collective-permute-start(bf16[2,200,256]{2,1,0:T(8,128)(2,1)S(1)} %shard_map.114.own_ref), channel_id=1, source_target_pairs={{0,12},{4,8},{8,4},{12,0},{16,28},{20,24},{24,20},{28,16},{1,13},{... | collective-permute-start | bytes 614408 | tf_op jit(solution)/shard_map/ppermute | solution.py:435
  49.3 9.8 %collective-permute-start.8 = (bf16[2,200,256]{2,1,0:T(8,128)(2,1)S(1)}, bf16[2,200,256]{2,1,0:T(8,128)(2,1)S(1)}, u32[]{:S(2)}, u32[]{:S(2)}) collective-permute-start(bf16[2,200,256]{2,1,0:T(8,128)(2,1)S(1)} %shard_map.114.own_ref), channel_id=1, source_target_pairs={{0,8},{4,12},{8,0},{12,4},{16,24},{20,28},{24,16},{28,20},{1,9},{5... | collective-permute-start | bytes 614408 | tf_op jit(solution)/shard_map/ppermute | solution.py:435
  52.9 14.8 %collective-permute-start.13 = (bf16[256,512]{1,0:T(8,128)(2,1)S(1)}, bf16[256,512]{1,0:T(8,128)(2,1)S(1)}, u32[]{:S(2)}, u32[]{:S(2)}) collective-permute-start(bf16[256,512]{1,0:T(8,128)(2,1)S(1)} %copy-done.3), channel_id=1, source_target_pairs={{0,4},{4,8},{8,12},{12,16},{16,20},{20,24},{24,28},{28,0},{1,5},{5... | collective-permute-start | bytes 786440 | tf_op jit(solution)/shard_map/ppermute | solution.py:485
  63.0 3.3 %collective-permute-start.12 = (f32[1,1024]{1,0:T(1,128)S(1)}, f32[1,1024]{1,0:T(1,128)S(1)}, u32[]{:S(2)}, u32[]{:S(2)}) collective-permute-start(f32[1,1024]{1,0:T(1,128)S(1)} %get-tuple-element.43), channel_id=1, source_target_pairs={{0,1},{1,0},{2,3},{3,2},{4,5},{5,4},{6,7},{7,6},{8,9},{9,8},{10,11... | collective-permute-start | bytes 12296 | tf_op jit(solution)/shard_map/ppermute | solution.py:435
  63.1 3.7 %collective-permute-start.11 = (f32[1,1024]{1,0:T(1,128)S(1)}, f32[1,1024]{1,0:T(1,128)S(1)}, u32[]{:S(2)}, u32[]{:S(2)}) collective-permute-start(f32[1,1024]{1,0:T(1,128)S(1)} %get-tuple-element.43), channel_id=1, source_target_pairs={{0,2},{1,3},{2,0},{3,1},{4,6},{5,7},{6,4},{7,5},{8,10},{9,11},{10,... | collective-permute-start | bytes 12296 | tf_op jit(solution)/shard_map/ppermute | solution.py:435
  64.7 3.0 %collective-permute-start.10 = (f32[1,1024]{1,0:T(1,128)S(1)}, f32[1,1024]{1,0:T(1,128)S(1)}, u32[]{:S(2)}, u32[]{:S(2)}) collective-permute-start(f32[1,1024]{1,0:T(1,128)S(1)} %get-tuple-element.43), channel_id=1, source_target_pairs={{0,3},{1,2},{2,1},{3,0},{4,7},{5,6},{6,5},{7,4},{8,11},{9,10},{10,... | collective-permute-start | bytes 12296 | tf_op jit(solution)/shard_map/ppermute | solution.py:435

commit v5 on v4

--- a/solution.py
+++ b/solution.py
@@ -11,7 +11,7 @@
 WINDOW_SPAN = 512
 EPS = 1e-06
 PAD = 8
-CUT = 128
+CUT = 192
 KIND = 0
 ORDERS = ((1, 2, 3), (2, 1, 3))
 WIRE = jnp.bfloat16
@@ -86,7 +86,7 @@
     acc, part, sent, wire, r_ref, w1_ref, w3_ref, w2_ref, sems = refs[-9:]
     heads, size = w1_ref.shape[0], w1_ref.shape[1]
     tokens = k_ref.shape[0]
-    step = min(256, tokens)
+    step = min(512, tokens)
     count = tokens // step
     used = []
 
@@ -191,7 +191,7 @@
     heads, size = w1.shape[0], w1.shape[1]
     rows = 3 * size // 4
     whole = pltpu.VMEM(w1.shape, F32)
-    step = min(256, keys.shape[0])
+    step = min(512, keys.shape[0])
     copies = 1 + 3 * heads + 2 * (keys.shape[0] // step) + 1 + 5 * heads + 3
     scratch = (
         pltpu.VMEM((3 * size, size), F32),
@@ -472,7 +472,7 @@
     out = grads(quarter, queries, keys, values, rates.T, w_one, w_three, w_two)
     own, p1, p2, p3, mine_w, q, k, v, end, rest, part = out
     got = spread((p1, p2, p3))
-    halo.append(lax.ppermute(part, "seq", ring))
+    halo.append(lax.ppermute(part, "seq", line))
     high = attend(first, q, k, v, (), blocks[half:], size)
     mine = call(gather_body, wire, (after(own, high), *got))
     for mask in shared[:-1]:
@@ -482,7 +482,7 @@
     scratch = (pltpu.VMEM((heads, rows, size), F32), pltpu.SemaphoreType.DMA)
     new = call(renorm_body, wire, (mine_w, mine, other), [FAR, VM, VM], scratch=scratch)
     pieces = (new, *spread((new, new, new)))
-    late = lax.ppermute(after(rest, pieces[1]), "seq", ring)
+    late = lax.ppermute(after(rest, pieces[1]), "seq", line)
     low, probs = attend(first, q, after(k, new), v, halo, blocks[:half], size)
     pieces = (after(new, low), *pieces[1:])
     zed, total, new_t = apply(quarter, q, head_scale, pieces)

time: 69.8 us -> 70 us (level)
  the two profiles are of different devices: /device:TPU:0 before, /device:TPU:11 now
where the time goes in v5:
time: 70 us; the launch traced here: 69.8 us
  Pallas kernels  24.9 us (36%)
  starting transfers between devices  23.7 us (34%)
  waiting for transfers between devices  20 us (29%)
  between operations  1 us (1%)
    pallas_call x9, Pallas kernels, call(): pl.pallas_call(body, out_shape=tuple(made) if many else made[0], in_specs...  24.9 us
    ppermute x10, waiting for transfers between devices, swap(): lax.ppermute(x, axis, [(i, i ^ mask) for i in range(lax.axis_size(axis))])  18.7 us
    ppermute x10, starting transfers between devices, swap(): lax.ppermute(x, axis, [(i, i ^ mask) for i in range(lax.axis_size(axis))])  9.27 us
    ppermute x1, starting transfers between devices, per_device(): late = lax.ppermute(after(rest, pieces[1]), 'seq', line)  7.41 us
    ppermute x1, starting transfers between devices, per_device(): halo.append(lax.ppermute(part, 'seq', line))  3.82 us
    ppermute x1, starting transfers between devices, per_device(): halo.append(lax.ppermute(after(end, mine), 'seq', line))  1.92 us
  transfers between devices with their start and end apart: 14, of which 5 were waited for; matrix products, arithmetic and copies ran while one was open for 0% of the time, Pallas kernels for 21%

profile of v5, /device:TPU:11, one launch (start us, length us, event | category | flops | bytes accessed | tf_op | source)
XLA Modules:
  0.0 69.8 jit_solution(15765044859669960526)
XLA Ops:
  0.6 8.9 %shard_map.111 = (f32[2,192,256]{2,1,0:T(8,128)}, bf16[2,200,256]{2,1,0:T(8,128)(2,1)}, bf16[2,200,256]{2,1,0:T(8,128)(2,1)}, bf16[2,200,256]{2,1,0:T(8,128)(2,1...) custom-call(s32[1]{0:T(128)} %bitcast.quarter, ...), custom_call_target="tpu_custom_call" | custom-call | flops 2147483648 | bytes 2097152 | tf_op jit(solution)/shard_map/pallas_call | solution.py:38
  9.5 0.3 collective-permute-start
  9.9 0.0 collective-permute-start.1
  9.9 2.4 %collective-permute-start.2 = (bf16[2,200,256]{2,1,0:T(8,128)(2,1)}, bf16[2,200,256]{2,1,0:T(8,128)(2,1)}, u32[]{:S(2)}, u32[]{:S(2)}) collective-permute-start(bf16[2,200,256]{2,1,0:T(8,128)(2,1)} %get-tuple-element.36), channel_id=1, source_target_pairs={{0,12},{4,8},{8,4},{12,0},{16,28},{20,24},{24,20},{28,16},{1,13},{... | collective-permute-start | bytes 614408 | tf_op jit(solution)/shard_map/ppermute | solution.py:435
  12.3 1.0 %shard_map.115 = bf16[320,512]{1,0:T(8,128)(2,1)S(1)} custom-call(bf16[1024,512]{1,0:T(8,128)(2,1)} %k_far.3), custom_call_target="tpu_custom_call" | custom-call | flops 16777216 | bytes 2097152 | tf_op jit(solution)/shard_map/pallas_call | solution.py:38
  13.2 1.3 %collective-permute-start.4 = (bf16[320,512]{1,0:T(8,128)(2,1)S(1)}, bf16[320,512]{1,0:T(8,128)(2,1)}, u32[]{:S(2)}, u32[]{:S(2)}) collective-permute-start(bf16[320,512]{1,0:T(8,128)(2,1)S(1)} %shard_map.115), channel_id=1, source_target_pairs={{0,4},{4,8},{8,12},{12,16},{16,20},{20,24},{24,28},{28,0},{1,5},{5... | collective-permute-start | bytes 983048 | tf_op jit(solution)/shard_map/ppermute | solution.py:471
  14.6 0.0 copy-start.1
  14.6 0.0 copy-start.4
  14.6 0.0 copy-start
  14.6 1.7 %shard_map.112.high_ref = f32[512,512]{1,0:T(8,128)S(1)} custom-call(s32[1]{0:T(128)} %bitcast.2.refs_0_, bf16[1024,512]{1,0:T(8,128)(2,1)S(1)} %get-tuple-element.28.refs_1_.q_ref, bf16[1024,512]{1,0:T(8,128)(2,1)S(1)} %get-tuple-element.37.refs_2_, bf16[1024,512]{1,0:T(8,128)(2,1)S(1)} %get-tuple-element.32.refs_3_), custom_call_target="tpu_custom_call" | custom-call | flops 1073741824 | bytes 2097152 | tf_op jit(solution)/shard_map/pallas_call | solution.py:38
  16.3 0.0 collective-permute-done.r1_ref
  16.3 0.0 collective-permute-done.1.r2_ref
  16.3 4.9 %collective-permute-done.2.r3_ref = bf16[2,200,256]{2,1,0:T(8,128)(2,1)} collective-permute-done((bf16[2,200,256]{2,1,0:T(8,128)(2,1)}, bf16[2,200,256]{2,1,0:T(8,128)(2,1)}, u32[]{:S(2)}, u32[]{:S(2)}) %collective-permute-start.2) | collective-permute-done | bytes 204832 | tf_op jit(solution)/shard_map/ppermute | solution.py:435
  21.2 0.0 copy-done.1
  21.2 2.2 %shard_map.113.mine_ref = bf16[2,200,256]{2,1,0:T(8,128)(2,1)S(1)} custom-call(f32[2,192,256]{2,1,0:T(8,128)S(1)} %copy-done.1, bf16[2,200,256]{2,1,0:T(8,128)(2,1)} %collective-permute-done.r1_ref, bf16[2,200,256]{2,1,0:T(8,128)(2,1)} %collective-permute-done.1.r2_ref, bf16[2,200,256]{2,1,0:T(8,128)(2,1)} %collective-permute-done.2.r3_ref), custom_call_target="tpu_custom_call" | custom-call | flops 16777216 | bytes 2097152 | tf_op jit(solution)/shard_map/pallas_call | solution.py:38
  23.4 1.3 %collective-permute-start.3 = (bf16[2,200,256]{2,1,0:T(8,128)(2,1)S(1)}, bf16[2,200,256]{2,1,0:T(8,128)(2,1)S(1)}, u32[]{:S(2)}, u32[]{:S(2)}) collective-permute-start(bf16[2,200,256]{2,1,0:T(8,128)(2,1)S(1)} %shard_map.113.mine_ref), channel_id=1, source_target_pairs={{0,24},{4,28},{8,16},{12,20},{16,8},{20,12},{24,0},{28,4},{1,25},{... | collective-permute-start | bytes 614408 | tf_op jit(solution)/shard_map/ppermute | solution.py:435
  24.8 0.0 copy-done.5
  24.8 3.8 %collective-permute-start.5 = (bf16[192,512]{1,0:T(8,128)(2,1)S(1)}, bf16[192,512]{1,0:T(8,128)(2,1)S(1)}, u32[]{:S(2)}, u32[]{:S(2)}) collective-permute-start(bf16[192,512]{1,0:T(8,128)(2,1)S(1)} %copy-done.5), channel_id=1, source_target_pairs={{0,4},{4,8},{8,12},{12,16},{16,20},{20,24},{24,28},{1,5},{5,9},{9,... | collective-permute-start | bytes 589832 | tf_op jit(solution)/shard_map/ppermute | solution.py:475
  28.6 0.0 copy-done.4
  28.6 1.9 %collective-permute-start.6 = (bf16[256,512]{1,0:T(8,128)(2,1)S(1)}, bf16[256,512]{1,0:T(8,128)(2,1)S(1)}, u32[]{:S(2)}, u32[]{:S(2)}) collective-permute-start(bf16[256,512]{1,0:T(8,128)(2,1)S(1)} %copy-done.4), channel_id=1, source_target_pairs={{0,4},{4,8},{8,12},{12,16},{16,20},{20,24},{24,28},{1,5},{5,9},{9,... | collective-permute-start | bytes 786440 | tf_op jit(solution)/shard_map/ppermute | solution.py:481
  30.5 9.1 %collective-permute-done.3.other_ref = bf16[2,200,256]{2,1,0:T(8,128)(2,1)S(1)} collective-permute-done((bf16[2,200,256]{2,1,0:T(8,128)(2,1)S(1)}, bf16[2,200,256]{2,1,0:T(8,128)(2,1)S(1)}, u32[]{:S(2)}, u32[]{:S(2)}) %collective-permute-start.3) | collective-permute-done | bytes 204832 | tf_op jit(solution)/shard_map/ppermute | solution.py:435
  39.6 0.0 copy-done
  39.6 1.2 %shard_map.114.own_ref = bf16[2,200,256]{2,1,0:T(8,128)(2,1)S(1)} custom-call(f32[2,192,256]{2,1,0:T(8,128)S(1)} %copy-done, bf16[2,200,256]{2,1,0:T(8,128)(2,1)S(1)} %shard_map.113.mine_ref, bf16[2,200,256]{2,1,0:T(8,128)(2,1)S(1)} %collective-permute-done.3.other_ref), custom_call_target="tpu_custom_call" | custom-call | flops 16777216 | bytes 2097152 | tf_op jit(solution)/shard_map/pallas_call | solution.py:38
  40.9 0.0 copy-start.3
  40.9 0.0 copy-start.2
  40.9 0.1 collective-permute-start.7
  41.0 0.1 collective-permute-start.9
  41.1 0.0 collective-permute-done.5.refs_5_
  41.1 2.5 %collective-permute-start.8 = (bf16[2,200,256]{2,1,0:T(8,128)(2,1)S(1)}, bf16[2,200,256]{2,1,0:T(8,128)(2,1)S(1)}, u32[]{:S(2)}, u32[]{:S(2)}) collective-permute-start(bf16[2,200,256]{2,1,0:T(8,128)(2,1)S(1)} %shard_map.114.own_ref), channel_id=1, source_target_pairs={{0,8},{4,12},{8,0},{12,4},{16,24},{20,28},{24,16},{28,20},{1,9},{5... | collective-permute-start | bytes 614408 | tf_op jit(solution)/shard_map/ppermute | solution.py:435
  43.6 0.0 collective-permute-done.4.refs_4_
  43.6 1.4 %collective-permute-done.6.refs_6_ = bf16[256,512]{1,0:T(8,128)(2,1)S(1)} collective-permute-done((bf16[256,512]{1,0:T(8,128)(2,1)S(1)}, bf16[256,512]{1,0:T(8,128)(2,1)S(1)}, u32[]{:S(2)}, u32[]{:S(2)}) %collective-permute-start.6) | collective-permute-done | bytes 262176 | tf_op jit(solution)/shard_map/ppermute | solution.py:481
  45.0 3.0 %shard_map.116 = (f32[512,512]{1,0:T(8,128)S(1)}, bf16[256,512]{1,0:T(8,128)(2,1)S(1)}) custom-call(s32[1]{0:T(128)} %bitcast.2.refs_0_, bf16[1024,512]{1,0:T(8,128)(2,1)S(1)} %get-tuple-element.28.refs_1_.q_ref, bf16[1024,512]{1,0:T(8,128)(2,1)S(1)} %get-tuple-element.37.refs_2_, bf16[1024,512]{1,0:T(8,128)(2,1)S(1)} %get-tuple-element.32.refs_3_, ...), custom_call_target="tpu_custom_call" | custom-call | flops 1073741824 | bytes 2097152 | tf_op jit(solution)/shard_map/pallas_call | solution.py:38
  48.0 3.5 %collective-permute-done.7.r1_ref = bf16[2,200,256]{2,1,0:T(8,128)(2,1)S(1)} collective-permute-done((bf16[2,200,256]{2,1,0:T(8,128)(2,1)S(1)}, bf16[2,200,256]{2,1,0:T(8,128)(2,1)S(1)}, u32[]{:S(2)}, u32[]{:S(2)}) %collective-permute-start.7) | collective-permute-done | bytes 204832 | tf_op jit(solution)/shard_map/ppermute | solution.py:435
  51.5 0.0 copy-done.3
  51.5 7.4 %collective-permute-start.13 = (bf16[256,512]{1,0:T(8,128)(2,1)S(1)}, bf16[256,512]{1,0:T(8,128)(2,1)S(1)}, u32[]{:S(2)}, u32[]{:S(2)}) collective-permute-start(bf16[256,512]{1,0:T(8,128)(2,1)S(1)} %copy-done.3), channel_id=1, source_target_pairs={{0,4},{4,8},{8,12},{12,16},{16,20},{20,24},{24,28},{1,5},{5,9},{9,... | collective-permute-start | bytes 786440 | tf_op jit(solution)/shard_map/ppermute | solution.py:485
  58.9 0.0 collective-permute-done.9.r3_ref
  58.9 0.0 collective-permute-done.8.r2_ref
  58.9 0.0 copy-done.2
  58.9 3.9 %shard_map.117 = (f32[1024,512]{1,0:T(8,128)S(1)}, f32[1,1024]{1,0:T(1,128)S(1)}, f32[2,768,256]{2,1,0:T(8,128)S(1)}) custom-call(s32[1]{0:T(128)} %bitcast.quarter, f32[2]{0:T(128)S(1)} %copy-done.2, bf16[1024,512]{1,0:T(8,128)(2,1)S(1)} %get-tuple-element.28.refs_1_.q_ref, bf16[2,200,256]{2,1,0:T(8,128)(2,1)S(1)} %shard_map.114.own_ref, ...), custom_call_target="tpu_custom_call" | custom-call | flops 2147483648 | bytes 2097152 | tf_op jit(solution)/shard_map/pallas_call | solution.py:38
  62.8 0.8 %collective-permute-start.12 = (f32[1,1024]{1,0:T(1,128)S(1)}, f32[1,1024]{1,0:T(1,128)S(1)}, u32[]{:S(2)}, u32[]{:S(2)}) collective-permute-start(f32[1,1024]{1,0:T(1,128)S(1)} %get-tuple-element.43), channel_id=1, source_target_pairs={{0,1},{1,0},{2,3},{3,2},{4,5},{5,4},{6,7},{7,6},{8,9},{9,8},{10,11... | collective-permute-start | bytes 12296 | tf_op jit(solution)/shard_map/ppermute | solution.py:435
  63.6 1.2 %collective-permute-start.11 = (f32[1,1024]{1,0:T(1,128)S(1)}, f32[1,1024]{1,0:T(1,128)S(1)}, u32[]{:S(2)}, u32[]{:S(2)}) collective-permute-start(f32[1,1024]{1,0:T(1,128)S(1)} %get-tuple-element.43), channel_id=1, source_target_pairs={{0,2},{1,3},{2,0},{3,1},{4,6},{5,7},{6,4},{7,5},{8,10},{9,11},{10,... | collective-permute-start | bytes 12296 | tf_op jit(solution)/shard_map/ppermute | solution.py:435
  64.9 0.5 collective-permute-start.10
  65.3 1.3 %shard_map.119 = (f32[2,256,256]{2,1,0:T(8,128)}, f32[2,256,256]{2,1,0:T(8,128)}, f32[2,256,256]{2,1,0:T(8,128)}) custom-call(f32[2,768,256]{2,1,0:T(8,128)S(1)} %get-tuple-element.48.n_ref), custom_call_target="tpu_custom_call" | custom-call | flops 16777216 | bytes 2097152 | tf_op jit(solution)/shard_map/pallas_call | solution.py:38
  66.7 0.0 collective-permute-done.12
  66.7 0.0 collective-permute-done.11
  66.7 1.2 %collective-permute-done.10 = f32[1,1024]{1,0:T(1,128)S(1)} collective-permute-done((f32[1,1024]{1,0:T(1,128)S(1)}, f32[1,1024]{1,0:T(1,128)S(1)}, u32[]{:S(2)}, u32[]{:S(2)}) %collective-permute-start.10) | collective-permute-done | bytes 4128 | tf_op jit(solution)/shard_map/ppermute | solution.py:435
  67.9 0.0 collective-permute-done.13.late_ref
  67.9 1.7 %shard_map.118 = f32[1024,512]{1,0:T(8,128)} custom-call(f32[1,1024]{1,0:T(1,128)S(1)} %add_add_fusion.r_ref, f32[1024,512]{1,0:T(8,128)S(1)} %get-tuple-element.44.z_ref, f32[512,512]{1,0:T(8,128)S(1)} %get-tuple-element.41.low_ref, f32[512,512]{1,0:T(8,128)S(1)} %shard_map.112.high_ref, bf16[256,512]{1,0:T(8,128)(2,1)S(1)} %get-tuple-element.45.probs_ref, ...), custom_call_target="tpu_custom_call" | custom-call | flops 16777216 | bytes 2097152 | tf_op jit(solution)/shard_map/pallas_call | solution.py:38
  (2 shorter events, 0.0 us)
Async XLA Ops:
  9.5 6.8 %collective-permute-start = (bf16[2,200,256]{2,1,0:T(8,128)(2,1)}, bf16[2,200,256]{2,1,0:T(8,128)(2,1)}, u32[]{:S(2)}, u32[]{:S(2)}) collective-permute-start(bf16[2,200,256]{2,1,0:T(8,128)(2,1)} %get-tuple-element.34), channel_id=1, source_target_pairs={{0,4},{4,0},{8,12},{12,8},{16,20},{20,16},{24,28},{28,24},{1,5},{5... | collective-permute-start | bytes 614408 | tf_op jit(solution)/shard_map/ppermute | solution.py:435
  9.9 6.5 %collective-permute-start.1 = (bf16[2,200,256]{2,1,0:T(8,128)(2,1)}, bf16[2,200,256]{2,1,0:T(8,128)(2,1)}, u32[]{:S(2)}, u32[]{:S(2)}) collective-permute-start(bf16[2,200,256]{2,1,0:T(8,128)(2,1)} %get-tuple-element.35), channel_id=1, source_target_pairs={{0,8},{4,12},{8,0},{12,4},{16,24},{20,28},{24,16},{28,20},{1,9},{5... | collective-permute-start | bytes 614408 | tf_op jit(solution)/shard_map/ppermute | solution.py:435
  9.9 11.4 %collective-permute-start.2 = (bf16[2,200,256]{2,1,0:T(8,128)(2,1)}, bf16[2,200,256]{2,1,0:T(8,128)(2,1)}, u32[]{:S(2)}, u32[]{:S(2)}) collective-permute-start(bf16[2,200,256]{2,1,0:T(8,128)(2,1)} %get-tuple-element.36), channel_id=1, source_target_pairs={{0,12},{4,8},{8,4},{12,0},{16,28},{20,24},{24,20},{28,16},{1,13},{... | collective-permute-start | bytes 614408 | tf_op jit(solution)/shard_map/ppermute | solution.py:435
  13.2 30.4 %collective-permute-start.4 = (bf16[320,512]{1,0:T(8,128)(2,1)S(1)}, bf16[320,512]{1,0:T(8,128)(2,1)}, u32[]{:S(2)}, u32[]{:S(2)}) collective-permute-start(bf16[320,512]{1,0:T(8,128)(2,1)S(1)} %shard_map.115), channel_id=1, source_target_pairs={{0,4},{4,8},{8,12},{12,16},{16,20},{20,24},{24,28},{28,0},{1,5},{5... | collective-permute-start | bytes 983048 | tf_op jit(solution)/shard_map/ppermute | solution.py:471
  14.6 6.7 %copy-start.1 = (f32[2,192,256]{2,1,0:T(8,128)S(1)}, f32[2,192,256]{2,1,0:T(8,128)}, u32[]{:S(2)}) copy-start(f32[2,192,256]{2,1,0:T(8,128)} %get-tuple-element.33.own_ref) | copy-start | bytes 1179652
  14.6 10.2 %copy-start.5 = (bf16[192,512]{1,0:T(8,128)(2,1)S(1)}, bf16[192,512]{1,0:T(8,128)(2,1)}, u32[]{:S(2)}) copy-start(bf16[192,512]{1,0:T(8,128)(2,1)} %get-tuple-element.38) | copy-start | bytes 589828
  14.6 14.0 %copy-start.4 = (bf16[256,512]{1,0:T(8,128)(2,1)S(1)}, bf16[256,512]{1,0:T(8,128)(2,1)}, u32[]{:S(2)}) copy-start(bf16[256,512]{1,0:T(8,128)(2,1)} %get-tuple-element.40) | copy-start | bytes 786436
  14.6 25.1 %copy-start = (f32[2,192,256]{2,1,0:T(8,128)S(1)}, f32[2,192,256]{2,1,0:T(8,128)}, u32[]{:S(2)}) copy-start(f32[2,192,256]{2,1,0:T(8,128)} %get-tuple-element.29.w_far) | copy-start | bytes 1179652
  23.4 16.2 %collective-permute-start.3 = (bf16[2,200,256]{2,1,0:T(8,128)(2,1)S(1)}, bf16[2,200,256]{2,1,0:T(8,128)(2,1)S(1)}, u32[]{:S(2)}, u32[]{:S(2)}) collective-permute-start(bf16[2,200,256]{2,1,0:T(8,128)(2,1)S(1)} %shard_map.113.mine_ref), channel_id=1, source_target_pairs={{0,24},{4,28},{8,16},{12,20},{16,8},{20,12},{24,0},{28,4},{1,25},{... | collective-permute-start | bytes 614408 | tf_op jit(solution)/shard_map/ppermute | solution.py:435
  24.8 16.3 %collective-permute-start.5 = (bf16[192,512]{1,0:T(8,128)(2,1)S(1)}, bf16[192,512]{1,0:T(8,128)(2,1)S(1)}, u32[]{:S(2)}, u32[]{:S(2)}) collective-permute-start(bf16[192,512]{1,0:T(8,128)(2,1)S(1)} %copy-done.5), channel_id=1, source_target_pairs={{0,4},{4,8},{8,12},{12,16},{16,20},{20,24},{24,28},{1,5},{5,9},{9,... | collective-permute-start | bytes 589832 | tf_op jit(solution)/shard_map/ppermute | solution.py:475
  28.6 16.4 %collective-permute-start.6 = (bf16[256,512]{1,0:T(8,128)(2,1)S(1)}, bf16[256,512]{1,0:T(8,128)(2,1)S(1)}, u32[]{:S(2)}, u32[]{:S(2)}) collective-permute-start(bf16[256,512]{1,0:T(8,128)(2,1)S(1)} %copy-done.4), channel_id=1, source_target_pairs={{0,4},{4,8},{8,12},{12,16},{16,20},{20,24},{24,28},{1,5},{5,9},{9,... | collective-permute-start | bytes 786440 | tf_op jit(solution)/shard_map/ppermute | solution.py:481
  40.9 10.6 %copy-start.3 = (bf16[256,512]{1,0:T(8,128)(2,1)S(1)}, bf16[256,512]{1,0:T(8,128)(2,1)}, u32[]{:S(2)}) copy-start(bf16[256,512]{1,0:T(8,128)(2,1)} %get-tuple-element.47) | copy-start | bytes 786436
  40.9 18.1 %copy-start.2 = (f32[2]{0:T(128)S(1)}, f32[2]{0:T(128)}, u32[]{:S(2)}) copy-start(f32[2]{0:T(128)} %s_ref.1) | copy-start | bytes 28
  40.9 10.6 %collective-permute-start.7 = (bf16[2,200,256]{2,1,0:T(8,128)(2,1)S(1)}, bf16[2,200,256]{2,1,0:T(8,128)(2,1)S(1)}, u32[]{:S(2)}, u32[]{:S(2)}) collective-permute-start(bf16[2,200,256]{2,1,0:T(8,128)(2,1)S(1)} %shard_map.114.own_ref), channel_id=1, source_target_pairs={{0,4},{4,0},{8,12},{12,8},{16,20},{20,16},{24,28},{28,24},{1,5},{5... | collective-permute-start | bytes 614408 | tf_op jit(solution)/shard_map/ppermute | solution.py:435
  41.0 17.9 %collective-permute-start.9 = (bf16[2,200,256]{2,1,0:T(8,128)(2,1)S(1)}, bf16[2,200,256]{2,1,0:T(8,128)(2,1)S(1)}, u32[]{:S(2)}, u32[]{:S(2)}) collective-permute-start(bf16[2,200,256]{2,1,0:T(8,128)(2,1)S(1)} %shard_map.114.own_ref), channel_id=1, source_target_pairs={{0,12},{4,8},{8,4},{12,0},{16,28},{20,24},{24,20},{28,16},{1,13},{... | collective-permute-start | bytes 614408 | tf_op jit(solution)/shard_map/ppermute | solution.py:435
  41.1 17.9 %collective-permute-start.8 = (bf16[2,200,256]{2,1,0:T(8,128)(2,1)S(1)}, bf16[2,200,256]{2,1,0:T(8,128)(2,1)S(1)}, u32[]{:S(2)}, u32[]{:S(2)}) collective-permute-start(bf16[2,200,256]{2,1,0:T(8,128)(2,1)S(1)} %shard_map.114.own_ref), channel_id=1, source_target_pairs={{0,8},{4,12},{8,0},{12,4},{16,24},{20,28},{24,16},{28,20},{1,9},{5... | collective-permute-start | bytes 614408 | tf_op jit(solution)/shard_map/ppermute | solution.py:435
  51.5 16.4 %collective-permute-start.13 = (bf16[256,512]{1,0:T(8,128)(2,1)S(1)}, bf16[256,512]{1,0:T(8,128)(2,1)S(1)}, u32[]{:S(2)}, u32[]{:S(2)}) collective-permute-start(bf16[256,512]{1,0:T(8,128)(2,1)S(1)} %copy-done.3), channel_id=1, source_target_pairs={{0,4},{4,8},{8,12},{12,16},{16,20},{20,24},{24,28},{1,5},{5,9},{9,... | collective-permute-start | bytes 786440 | tf_op jit(solution)/shard_map/ppermute | solution.py:485
  62.8 3.8 %collective-permute-start.12 = (f32[1,1024]{1,0:T(1,128)S(1)}, f32[1,1024]{1,0:T(1,128)S(1)}, u32[]{:S(2)}, u32[]{:S(2)}) collective-permute-start(f32[1,1024]{1,0:T(1,128)S(1)} %get-tuple-element.43), channel_id=1, source_target_pairs={{0,1},{1,0},{2,3},{3,2},{4,5},{5,4},{6,7},{7,6},{8,9},{9,8},{10,11... | collective-permute-start | bytes 12296 | tf_op jit(solution)/shard_map/ppermute | solution.py:435
  63.6 3.0 %collective-permute-start.11 = (f32[1,1024]{1,0:T(1,128)S(1)}, f32[1,1024]{1,0:T(1,128)S(1)}, u32[]{:S(2)}, u32[]{:S(2)}) collective-permute-start(f32[1,1024]{1,0:T(1,128)S(1)} %get-tuple-element.43), channel_id=1, source_target_pairs={{0,2},{1,3},{2,0},{3,1},{4,6},{5,7},{6,4},{7,5},{8,10},{9,11},{10,... | collective-permute-start | bytes 12296 | tf_op jit(solution)/shard_map/ppermute | solution.py:435
  64.9 3.0 %collective-permute-start.10 = (f32[1,1024]{1,0:T(1,128)S(1)}, f32[1,1024]{1,0:T(1,128)S(1)}, u32[]{:S(2)}, u32[]{:S(2)}) collective-permute-start(f32[1,1024]{1,0:T(1,128)S(1)} %get-tuple-element.43), channel_id=1, source_target_pairs={{0,3},{1,2},{2,1},{3,0},{4,7},{5,6},{6,5},{7,4},{8,11},{9,10},{10,... | collective-permute-start | bytes 12296 | tf_op jit(solution)/shard_map/ppermute | solution.py:435
